TPU v7x, 32 devices: a whole 2x2x4 slice. The times are simulated.
32 devices in a mesh: row: 4 (over x, core), col: 8 (over z, y).
Axes of the slice: x: 2, y: 2, z: 4, core: 2. Of those that a mesh axis runs over, the one named last changes fastest.
Arguments:
- matrix: float32 [8, 512, 4, 1024], P(None, 'row', None, 'col'), as said below
Outputs:
- factored: float32 [8, 512, 4, 1024], P(None, 'row', None, 'col')
Inputs may be any that keep to these rules, and one draw needn't show every extreme that they name: `matrix`: Symmetric; an exponential covariance kernel exp(-distance / reach) between sites in three dimensions, plus a diagonal noise variance of 0.5 or more at each site, so every Schur complement taken during the factorization is positive definite.
All inputs are finite; a program needn't handle non-finite values.
Results may differ from a plain program's by a relative error of at most 0.00011.
Values sent between devices are 32-bit elements; how exact they have to be, the bound alone decides.
No kernel may reach another device: no remote copies, remote signals or barrier semaphores. Data moves between devices by JAX's collectives and lax.ppermute only.
A program may use at most 128 MiB of HBM per device.

v0:
```python
import jax
import jax.numpy as jnp
from jax import lax
from jax.sharding import PartitionSpec as P

STEPS = 8


def spread(block, axis, source):
    block = jnp.where(lax.axis_index(axis) == source, block, jnp.zeros_like(block))
    return lax.psum(block, axis)


def keep_blocks(rows_in, keep, block_size):
    blocked = rows_in.reshape(keep.shape[0], block_size, rows_in.shape[1])
    return jnp.where(keep[:, None, None], blocked, 0.0).reshape(rows_in.shape)


def pick_rows(rows_in, which, fold_ratio, block_size):
    blocked = rows_in.reshape(
        rows_in.shape[0] // (fold_ratio * block_size), fold_ratio, block_size, rows_in.shape[1]
    )
    chosen = lax.dynamic_slice_in_dim(blocked, which, 1, 1)
    return chosen.reshape(-1, rows_in.shape[1])


def product(left_rows, right_rows):
    return jnp.dot(
        left_rows, right_rows.T, precision=lax.Precision.HIGHEST, preferred_element_type=jnp.float32
    )


def finish(segment, panel_step, panel_rows, factor, row_ids, my_col, cols_dev, block_size):
    block_rows = row_ids.shape[0]
    block_count = segment.shape[1] // block_size
    blocked = segment.reshape(block_rows, block_size, block_count, block_size)
    col_here = jnp.arange(block_count, dtype=jnp.int32) * cols_dev + my_col
    below_mask = (row_ids > panel_step)[:, None, None, None]
    on_diagonal = (row_ids == panel_step)[:, None, None, None]
    written = jnp.where(
        below_mask,
        panel_rows.reshape(block_rows, block_size, 1, block_size),
        jnp.where(on_diagonal, factor[None, :, None, :], blocked),
    )
    blocked = jnp.where((col_here == panel_step)[None, None, :, None], written, blocked)
    blocked = jnp.where(on_diagonal & (col_here > panel_step)[None, None, :, None], 0.0, blocked)
    return blocked.reshape(segment.shape)


def local(matrix):
    rows_dev = lax.axis_size("row")
    cols_dev = lax.axis_size("col")
    my_row = lax.axis_index("row")
    my_col = lax.axis_index("col")
    block_rows = matrix.shape[0]
    block_size = matrix.shape[1]
    block_cols = matrix.shape[2]
    fold_ratio = cols_dev // rows_dev
    current = matrix.reshape(block_rows * block_size, block_cols * block_size)
    row_ids = jnp.arange(block_rows, dtype=jnp.int32) * rows_dev + my_row
    identity = jnp.eye(block_size, dtype=jnp.float32)
    upcoming = current[:, :block_size]
    for panel_step in range(STEPS):
        root_row = panel_step % rows_dev
        root_col = panel_step % cols_dev
        diag_first = panel_step // rows_dev * block_size
        diag_piece = upcoming[diag_first : diag_first + block_size]
        diagonal = spread(diag_piece, "row", root_row)
        factor = jnp.linalg.cholesky(diagonal)
        inverse = jax.scipy.linalg.solve_triangular(factor, identity, lower=True)
        panel_rows = keep_blocks(product(upcoming, inverse), row_ids > panel_step, block_size)
        across = spread(panel_rows, "col", root_col)
        mirrored = spread(
            pick_rows(across, my_col // rows_dev, fold_ratio, block_size), "row", my_col % rows_dev
        )
        current = finish(
            current - product(across, mirrored),
            panel_step,
            panel_rows,
            factor,
            row_ids,
            my_col,
            cols_dev,
            block_size,
        )
        next_first = (panel_step + 1) // cols_dev * block_size
        upcoming = current[:, next_first : next_first + block_size]
    return current.reshape(matrix.shape)


def solution(mesh):
    placed = (P(None, "row", None, "col"),)
    return jax.shard_map(
        local, mesh=mesh, in_specs=placed, out_specs=P(None, "row", None, "col"), check_vma=False
    )
```

profile of v0, /device:TPU:8, one launch (start us, length us, event | category | flops | bytes accessed | tf_op | source)
XLA Modules:
  0.0 1396.6 jit_solution(8074853636242637044)
XLA Ops:
  13.6 31.1 %all-reduce.25.cloned.1.call-done = f32[128,128]{0,1:T(8,128)} async-done(((f32[128,128]{0,1:T(8,128)}), f32[128,128]{0,1:T(8,128)}) %all-reduce.25.cloned.1.call-update) | async-done | bytes 65552 | tf_op jit(solution)/shard_map/psum | solution.py:11
  71.6 71.6 %all-reduce.27.cloned.1.call-done = f32[1024,128]{0,1:T(8,128)} async-done(((f32[1024,128]{0,1:T(8,128)}), f32[1024,128]{0,1:T(8,128)}) %all-reduce.27.cloned.1.call-update) | async-done | bytes 524304 | tf_op jit(solution)/shard_map/psum | solution.py:11
  146.6 31.6 %all-reduce.29.cloned.1.call-done = f32[512,128]{0,1:T(8,128)} async-done(((f32[512,128]{0,1:T(8,128)}), f32[512,128]{0,1:T(8,128)}) %all-reduce.29.cloned.1.call-update) | async-done | bytes 262160 | tf_op jit(solution)/shard_map/psum | solution.py:11
  183.5 31.1 %all-reduce.31.cloned.1.call-done = f32[128,128]{0,1:T(8,128)} async-done(((f32[128,128]{0,1:T(8,128)}), f32[128,128]{0,1:T(8,128)}) %all-reduce.31.cloned.1.call-update) | async-done | bytes 65552 | tf_op jit(solution)/shard_map/psum | solution.py:11
  242.7 71.0 %all-reduce.33.cloned.1.call-done = f32[1024,128]{0,1:T(8,128)} async-done(((f32[1024,128]{0,1:T(8,128)}), f32[1024,128]{0,1:T(8,128)}) %all-reduce.33.cloned.1.call-update) | async-done | bytes 524304 | tf_op jit(solution)/shard_map/psum | solution.py:11
  317.0 31.8 %all-reduce.35.cloned.1.call-done = f32[512,128]{0,1:T(8,128)} async-done(((f32[512,128]{0,1:T(8,128)}), f32[512,128]{0,1:T(8,128)}) %all-reduce.35.cloned.1.call-update) | async-done | bytes 262160 | tf_op jit(solution)/shard_map/psum | solution.py:11
  353.9 31.1 %all-reduce.37.cloned.1.call-done = f32[128,128]{0,1:T(8,128)} async-done(((f32[128,128]{0,1:T(8,128)}), f32[128,128]{0,1:T(8,128)}) %all-reduce.37.cloned.1.call-update) | async-done | bytes 65552 | tf_op jit(solution)/shard_map/psum | solution.py:11
  413.4 70.7 %all-reduce.39.cloned.1.call-done = f32[1024,128]{0,1:T(8,128)} async-done(((f32[1024,128]{0,1:T(8,128)}), f32[1024,128]{0,1:T(8,128)}) %all-reduce.39.cloned.1.call-update) | async-done | bytes 524304 | tf_op jit(solution)/shard_map/psum | solution.py:11
  487.5 31.6 %all-reduce.41.cloned.1.call-done = f32[512,128]{0,1:T(8,128)} async-done(((f32[512,128]{0,1:T(8,128)}), f32[512,128]{0,1:T(8,128)}) %all-reduce.41.cloned.1.call-update) | async-done | bytes 262160 | tf_op jit(solution)/shard_map/psum | solution.py:11
  524.9 31.2 %all-reduce.43.cloned.1.call-done = f32[128,128]{0,1:T(8,128)} async-done(((f32[128,128]{0,1:T(8,128)}), f32[128,128]{0,1:T(8,128)}) %all-reduce.43.cloned.1.call-update) | async-done | bytes 65552 | tf_op jit(solution)/shard_map/psum | solution.py:11
  585.1 71.3 %all-reduce.45.cloned.1.call-done = f32[1024,128]{0,1:T(8,128)} async-done(((f32[1024,128]{0,1:T(8,128)}), f32[1024,128]{0,1:T(8,128)}) %all-reduce.45.cloned.1.call-update) | async-done | bytes 524304 | tf_op jit(solution)/shard_map/psum | solution.py:11
  659.6 31.7 %all-reduce.47.cloned.1.call-done = f32[512,128]{0,1:T(8,128)} async-done(((f32[512,128]{0,1:T(8,128)}), f32[512,128]{0,1:T(8,128)}) %all-reduce.47.cloned.1.call-update) | async-done | bytes 262160 | tf_op jit(solution)/shard_map/psum | solution.py:11
  697.1 31.2 %all-reduce.49.cloned.1.call-done = f32[128,128]{0,1:T(8,128)} async-done(((f32[128,128]{0,1:T(8,128)}), f32[128,128]{0,1:T(8,128)}) %all-reduce.49.cloned.1.call-update) | async-done | bytes 65552 | tf_op jit(solution)/shard_map/psum | solution.py:11
  757.1 71.5 %all-reduce.51.cloned.1.call-done = f32[1024,128]{0,1:T(8,128)} async-done(((f32[1024,128]{0,1:T(8,128)}), f32[1024,128]{0,1:T(8,128)}) %all-reduce.51.cloned.1.call-update) | async-done | bytes 524304 | tf_op jit(solution)/shard_map/psum | solution.py:11
  832.2 31.3 %all-reduce.53.cloned.1.call-done = f32[512,128]{0,1:T(8,128)} async-done(((f32[512,128]{0,1:T(8,128)}), f32[512,128]{0,1:T(8,128)}) %all-reduce.53.cloned.1.call-update) | async-done | bytes 262160 | tf_op jit(solution)/shard_map/psum | solution.py:11
  868.7 31.1 %all-reduce.55.cloned.1.call-done = f32[128,128]{0,1:T(8,128)} async-done(((f32[128,128]{0,1:T(8,128)}), f32[128,128]{0,1:T(8,128)}) %all-reduce.55.cloned.1.call-update) | async-done | bytes 65552 | tf_op jit(solution)/shard_map/psum | solution.py:11
  928.3 70.5 %all-reduce.57.cloned.1.call-done = f32[1024,128]{0,1:T(8,128)} async-done(((f32[1024,128]{0,1:T(8,128)}), f32[1024,128]{0,1:T(8,128)}) %all-reduce.57.cloned.1.call-update) | async-done | bytes 524304 | tf_op jit(solution)/shard_map/psum | solution.py:11
  1002.1 31.8 %all-reduce.59.cloned.1.call-done = f32[512,128]{0,1:T(8,128)} async-done(((f32[512,128]{0,1:T(8,128)}), f32[512,128]{0,1:T(8,128)}) %all-reduce.59.cloned.1.call-update) | async-done | bytes 262160 | tf_op jit(solution)/shard_map/psum | solution.py:11
  1039.7 31.1 %all-reduce.61.cloned.1.call-done = f32[128,128]{0,1:T(8,128)} async-done(((f32[128,128]{0,1:T(8,128)}), f32[128,128]{0,1:T(8,128)}) %all-reduce.61.cloned.1.call-update) | async-done | bytes 65552 | tf_op jit(solution)/shard_map/psum | solution.py:11
  1099.5 71.5 %all-reduce.63.cloned.1.call-done = f32[1024,128]{0,1:T(8,128)} async-done(((f32[1024,128]{0,1:T(8,128)}), f32[1024,128]{0,1:T(8,128)}) %all-reduce.63.cloned.1.call-update) | async-done | bytes 524304 | tf_op jit(solution)/shard_map/psum | solution.py:11
  1174.5 31.6 %all-reduce.65.cloned.1.call-done = f32[512,128]{0,1:T(8,128)} async-done(((f32[512,128]{0,1:T(8,128)}), f32[512,128]{0,1:T(8,128)}) %all-reduce.65.cloned.1.call-update) | async-done | bytes 262160 | tf_op jit(solution)/shard_map/psum | solution.py:11
  1211.9 31.1 %all-reduce.67.cloned.1.call-done = f32[128,128]{0,1:T(8,128)} async-done(((f32[128,128]{0,1:T(8,128)}), f32[128,128]{0,1:T(8,128)}) %all-reduce.67.cloned.1.call-update) | async-done | bytes 65552 | tf_op jit(solution)/shard_map/psum | solution.py:11
  1271.9 71.4 %all-reduce.69.cloned.1.call-done = f32[1024,128]{0,1:T(8,128)} async-done(((f32[1024,128]{0,1:T(8,128)}), f32[1024,128]{0,1:T(8,128)}) %all-reduce.69.cloned.1.call-update) | async-done | bytes 524304 | tf_op jit(solution)/shard_map/psum | solution.py:11
  1350.4 29.8 %all-reduce.71.cloned.1.call-done = f32[512,128]{0,1:T(8,128)} async-done(((f32[512,128]{0,1:T(8,128)}), f32[512,128]{0,1:T(8,128)}) %all-reduce.71.cloned.1.call-update) | async-done | bytes 262160 | tf_op jit(solution)/shard_map/psum | solution.py:11
  (343 shorter events, 311.5 us)
Async XLA Ops:
  6.5 38.1 %all-reduce.25.cloned.1.call-start = ((), (), s32[]{:S(2)}) async-start(), calls=%async_computation | async-start | bytes 131072 | tf_op jit(solution)/shard_map/psum | solution.py:11
  12.3 130.9 %all-reduce.27.cloned.1.call-start = ((), (), s32[]{:S(2)}) async-start(), calls=%async_computation.1 | async-start | bytes 1048576 | tf_op jit(solution)/shard_map/psum | solution.py:11
  71.2 107.1 %all-reduce.29.cloned.1.call-start = ((), (), s32[]{:S(2)}) async-start(), calls=%async_computation.2 | async-start | bytes 524288 | tf_op jit(solution)/shard_map/psum | solution.py:11
  146.3 68.3 %all-reduce.31.cloned.1.call-start = ((), (), s32[]{:S(2)}) async-start(), calls=%async_computation.3 | async-start | bytes 131072 | tf_op jit(solution)/shard_map/psum | solution.py:11
  183.4 130.4 %all-reduce.33.cloned.1.call-start = ((), (), s32[]{:S(2)}) async-start(), calls=%async_computation.4 | async-start | bytes 1048576 | tf_op jit(solution)/shard_map/psum | solution.py:11
  241.8 107.0 %all-reduce.35.cloned.1.call-start = ((), (), s32[]{:S(2)}) async-start(), calls=%async_computation.5 | async-start | bytes 524288 | tf_op jit(solution)/shard_map/psum | solution.py:11
  316.8 68.2 %all-reduce.37.cloned.1.call-start = ((), (), s32[]{:S(2)}) async-start(), calls=%async_computation.6 | async-start | bytes 131072 | tf_op jit(solution)/shard_map/psum | solution.py:11
  353.8 130.3 %all-reduce.39.cloned.1.call-start = ((), (), s32[]{:S(2)}) async-start(), calls=%async_computation.7 | async-start | bytes 1048576 | tf_op jit(solution)/shard_map/psum | solution.py:11
  412.1 107.1 %all-reduce.41.cloned.1.call-start = ((), (), s32[]{:S(2)}) async-start(), calls=%async_computation.8 | async-start | bytes 524288 | tf_op jit(solution)/shard_map/psum | solution.py:11
  487.2 68.9 %all-reduce.43.cloned.1.call-start = ((), (), s32[]{:S(2)}) async-start(), calls=%async_computation.9 | async-start | bytes 131072 | tf_op jit(solution)/shard_map/psum | solution.py:11
  524.9 131.5 %all-reduce.45.cloned.1.call-start = ((), (), s32[]{:S(2)}) async-start(), calls=%async_computation.10 | async-start | bytes 1048576 | tf_op jit(solution)/shard_map/psum | solution.py:11
  584.3 107.0 %all-reduce.47.cloned.1.call-start = ((), (), s32[]{:S(2)}) async-start(), calls=%async_computation.11 | async-start | bytes 524288 | tf_op jit(solution)/shard_map/psum | solution.py:11
  659.4 68.9 %all-reduce.49.cloned.1.call-start = ((), (), s32[]{:S(2)}) async-start(), calls=%async_computation.12 | async-start | bytes 131072 | tf_op jit(solution)/shard_map/psum | solution.py:11
  697.1 131.5 %all-reduce.51.cloned.1.call-start = ((), (), s32[]{:S(2)}) async-start(), calls=%async_computation.13 | async-start | bytes 1048576 | tf_op jit(solution)/shard_map/psum | solution.py:11
  756.5 107.0 %all-reduce.53.cloned.1.call-start = ((), (), s32[]{:S(2)}) async-start(), calls=%async_computation.14 | async-start | bytes 524288 | tf_op jit(solution)/shard_map/psum | solution.py:11
  831.6 68.2 %all-reduce.55.cloned.1.call-start = ((), (), s32[]{:S(2)}) async-start(), calls=%async_computation.15 | async-start | bytes 131072 | tf_op jit(solution)/shard_map/psum | solution.py:11
  868.6 130.3 %all-reduce.57.cloned.1.call-start = ((), (), s32[]{:S(2)}) async-start(), calls=%async_computation.16 | async-start | bytes 1048576 | tf_op jit(solution)/shard_map/psum | solution.py:11
  926.9 107.0 %all-reduce.59.cloned.1.call-start = ((), (), s32[]{:S(2)}) async-start(), calls=%async_computation.17 | async-start | bytes 524288 | tf_op jit(solution)/shard_map/psum | solution.py:11
  1002.0 68.8 %all-reduce.61.cloned.1.call-start = ((), (), s32[]{:S(2)}) async-start(), calls=%async_computation.18 | async-start | bytes 131072 | tf_op jit(solution)/shard_map/psum | solution.py:11
  1039.6 131.4 %all-reduce.63.cloned.1.call-start = ((), (), s32[]{:S(2)}) async-start(), calls=%async_computation.19 | async-start | bytes 1048576 | tf_op jit(solution)/shard_map/psum | solution.py:11
  1099.0 107.1 %all-reduce.65.cloned.1.call-start = ((), (), s32[]{:S(2)}) async-start(), calls=%async_computation.20 | async-start | bytes 524288 | tf_op jit(solution)/shard_map/psum | solution.py:11
  1174.1 68.9 %all-reduce.67.cloned.1.call-start = ((), (), s32[]{:S(2)}) async-start(), calls=%async_computation.21 | async-start | bytes 131072 | tf_op jit(solution)/shard_map/psum | solution.py:11
  1211.8 131.4 %all-reduce.69.cloned.1.call-start = ((), (), s32[]{:S(2)}) async-start(), calls=%async_computation.22 | async-start | bytes 1048576 | tf_op jit(solution)/shard_map/psum | solution.py:11
  1271.2 109.0 %all-reduce.71.cloned.1.call-start = ((), (), s32[]{:S(2)}) async-start(), calls=%async_computation.23 | async-start | bytes 524288 | tf_op jit(solution)/shard_map/psum | solution.py:11
  (29 other events, 720.1 us)
Sparse Core Ops, SparseCore 0:
  12.4 32.2 all-reduce.24
  71.3 71.8 all-reduce.26
  146.4 31.8 all-reduce.28
  183.5 31.0 all-reduce.30
  241.9 71.8 all-reduce.32
  317.0 31.7 all-reduce.34
  354.0 31.0 all-reduce.36
  412.2 71.8 all-reduce.38
  487.3 31.7 all-reduce.40
  525.0 31.0 all-reduce.42
  584.4 71.8 all-reduce.44
  659.6 31.7 all-reduce.46
  697.2 31.0 all-reduce.48
  756.6 71.8 all-reduce.50
  831.7 31.7 all-reduce.52
  868.7 31.0 all-reduce.54
  927.0 71.8 all-reduce.56
  1002.1 31.7 all-reduce.58
  1039.7 31.0 all-reduce.60
  1099.1 71.8 all-reduce.62
  1174.2 31.8 all-reduce.64
  1211.9 31.0 all-reduce.66
  1271.3 71.8 all-reduce.68
  1348.4 31.7 all-reduce.70
where the time goes:
time: 1410 us; the launch traced here: 1400 us
  waiting for transfers between devices  1070 us (76%)
  other arithmetic  214 us (15%)
  local copies, waits for them, and re-layouts  56.8 us (4%)
  matrix products  37.2 us (3%)
  between operations  15.4 us (1%)
    psum x24, waiting for transfers between devices, spread(): return lax.psum(block, axis)  1070 us
    another operation x24, other arithmetic, local(): factor = jnp.linalg.cholesky(diagonal)  99.6 us
    another operation x16, other arithmetic, local(): inverse = jax.scipy.linalg.solve_triangular(factor, identity, lower=True)  84 us
    dot_general x16, matrix products, product(): jnp.dot(left_rows, right_rows.T, precision=lax.Precision.HIGHEST, preferr...  34.9 us
  transfers between devices with their start and end apart: 24, of which 24 were waited for; matrix products, arithmetic and copies ran while one was open for 1% of the time, Pallas kernels for 0%

commit v1 on v0

v1 whole, which is shorter than its diff:
```python
import functools

import jax
import jax.numpy as jnp
from jax import lax
from jax.experimental import pallas as pl
from jax.experimental.pallas import tpu as pltpu
from jax.sharding import PartitionSpec as P

STEPS = 8
PANEL = 16
F32 = jnp.float32
BF16 = jnp.bfloat16


def split2(x):
    high = x.astype(BF16)
    return high, (x - high.astype(F32)).astype(BF16)


def split3(x):
    high = x.astype(BF16)
    rest = x - high.astype(F32)
    mid = rest.astype(BF16)
    return high, mid, (rest - mid.astype(F32)).astype(BF16)


def contract(left, right, dims):
    return lax.dot_general(left, right, (dims, ((), ())), preferred_element_type=F32)


def gram(rows_in, rows_wide):
    h, m, l = split3(rows_in)
    hw, mw, lw = split3(rows_wide)
    left = jnp.concatenate([h, h, m, m, h, l], 0)
    right = jnp.concatenate([hw, mw, hw, mw, lw, hw], 0)
    return contract(left, right, ((0,), (0,)))


def three(left, right, dims):
    (lh, lm), (rh, rm) = left, right
    return contract(lh, rh, dims) + (contract(lh, rm, dims) + contract(lm, rh, dims))


def factor_tile(tile, nb):
    for first in range(0, nb, PANEL):
        rows = [tile[pl.ds(first + i, 8, stride=0), :] for i in range(PANEL)]
        left = [r[:, :nb] for r in rows]
        right = [r[:, nb:] for r in rows]
        entry = {}
        for i in range(PANEL):
            for s in range(i + 1):
                lane = first + i
                entry[i, s] = jnp.broadcast_to(left[s][:, lane : lane + 1], (8, nb))
        for s in range(PANEL):
            scale = lax.rsqrt(entry[s, s])
            left[s] = left[s] * scale
            right[s] = right[s] * scale
            for i in range(s + 1, PANEL):
                entry[i, s] = entry[i, s] * scale
            for i in range(s + 1, PANEL):
                for t in range(s + 1, i + 1):
                    entry[i, t] = entry[i, t] - entry[i, s] * entry[t, s]
            for i in range(s + 1, PANEL):
                left[i] = left[i] - entry[i, s] * left[s]
                right[i] = right[i] - entry[i, s] * right[s]
        for s in range(PANEL):
            tile[first + s : first + s + 1, :nb] = left[s][:1]
            tile[first + s : first + s + 1, nb:] = right[s][:1]
        after = first + PANEL
        if after < nb:
            done = tile[first:after, :]
            tile[after:, :] = tile[after:, :] - gram(done[:, :nb], done)[after:, :]


def factor_kernel(
    place, lead, side, solved, top, tile, up_h, up_m, gk, yh, ym, mh, mm, *, nb, na, rows_dev, cols_dev, fwd
):
    my_row, my_col = place[0], place[1]
    width = STEPS * nb
    ii = lax.broadcasted_iota(jnp.int32, (nb, nb), 0)
    jj = lax.broadcasted_iota(jnp.int32, (nb, nb), 1)
    eye = jnp.where(ii == jj, 1.0, 0.0).astype(F32)
    wide_b = side.shape[1]
    ND = ((0,), (0,))
    MM = ((1,), (0,))

    @pl.loop(0, STEPS)
    def _(k):
        base = pl.multiple_of(k * nb, nb)
        for step in range(STEPS):

            @pl.when(k == step)
            def _():
                lo = step * nb
                if step == 0:
                    tile[:, :nb] = lead[:nb, :nb]
                else:
                    l = (up_h[:lo, lo : lo + nb], up_m[:lo, lo : lo + nb])
                    tile[:, :nb] = lead[lo : lo + nb, lo : lo + nb] - three(l, l, ND)

        tile[:, nb:] = eye
        factor_tile(tile, nb)
        gk[pl.ds(base, nb), :] = tile[:, nb:]
        for step in range(STEPS):

            @pl.when(k == step)
            def _():
                lo, hi = step * nb, step * nb + nb
                rest = side[lo:hi, :]
                g = split2(tile[:, nb:])
                if step:
                    l = (up_h[:lo, lo:hi], up_m[:lo, lo:hi])
                    rest = rest - three(l, (yh[:lo, :], ym[:lo, :]), ND)
                h, m = split2(three(g, split2(rest), MM))
                yh[lo:hi, :] = h
                ym[lo:hi, :] = m
                h, m = split2(jnp.where(ii <= jj, tile[:, :nb], 0.0))
                up_h[lo:hi, lo:hi] = h
                up_m[lo:hi, lo:hi] = m
                if hi < width:
                    right = lead[lo:hi, hi:]
                    if step:
                        right = right - three(l, (up_h[:lo, hi:], up_m[:lo, hi:]), ND)
                    block = three(g, split2(right), MM)
                    h, m = split2(block)
                    up_h[lo:hi, hi:] = h
                    up_m[lo:hi, hi:] = m
                mine = my_col == step
                for a in range(na):
                    for p in range(rows_dev):
                        row = a * rows_dev + p

                        @pl.when(mine & (my_row == p))
                        def _():
                            if row < step:
                                top[a] = jnp.zeros((nb, nb), F32)
                            elif row == step:
                                top[a] = jnp.where(ii >= jj, tile[:, :nb].T, 0.0)
                            else:
                                at = row * nb - hi
                                top[a] = block[:, at : at + nb].T

    @pl.when(my_col >= STEPS)
    def _():
        top[...] = jnp.zeros(top.shape, F32)

    for step in reversed(range(STEPS)):
        lo, hi = step * nb, step * nb + nb
        lead_part = jnp.where(my_col == step, eye, 0.0)
        known_h, known_m = yh[lo:hi, :], ym[lo:hi, :]
        known = known_h.astype(F32) + known_m.astype(F32)
        if fwd == 0:
            lead_part = jnp.where(my_col < STEPS, lead_part, known[:, :nb])
            known = known[:, nb:]
        rest = jnp.concatenate([lead_part, known], 1)
        if hi < width:
            rest = rest - three((up_h[lo:hi, hi:], up_m[lo:hi, hi:]), (mh[hi:, :], mm[hi:, :]), MM)
        h, m = split2(three(split2(gk[lo:hi, :]), split2(rest), ND))
        mh[lo:hi, :] = h
        mm[lo:hi, :] = m
    solved[0] = mh[...]
    solved[1] = mm[...]


def close_kernel(place, across, mine, solved, top, out, *, nb, na, block_rows, block_cols):
    my_col = place[1]
    left = split2(across[...])
    prod = three(left, (solved[0], solved[1]), ((1,), (0,)))
    is_panel = my_col < STEPS
    for a in range(block_rows):
        for b in range(block_cols):
            where = pl.ds(a * nb * block_cols + b, nb, stride=block_cols)
            if a < na:
                out[where, :] = top[a] if b == 0 else jnp.zeros((nb, nb), F32)
            else:
                part = prod[(a - na) * nb : (a - na + 1) * nb, b * nb : (b + 1) * nb]
                old = mine[where, :]
                if b == 0:
                    out[where, :] = jnp.where(is_panel, part, old - part)
                else:
                    out[where, :] = old - part


def local(matrix):
    rows_dev = lax.axis_size("row")
    cols_dev = lax.axis_size("col")
    my_row = lax.axis_index("row")
    my_col = lax.axis_index("col")
    block_rows, nb, block_cols, _ = matrix.shape
    na = STEPS // rows_dev
    fwd = STEPS // cols_dev
    width = STEPS * nb
    place = jnp.stack([my_row, my_col]).astype(jnp.int32)

    first = matrix[:na, :, 0, :]
    lead = lax.all_gather(first, ("row", "col"))
    lead = lead.reshape(rows_dev, cols_dev, na, nb, nb)[:, :STEPS]
    lead = lead.transpose(2, 0, 3, 1, 4).reshape(width, width)
    side = matrix[:na, :, fwd:, :]
    side = lax.all_gather(side, "row")
    side = side.transpose(1, 0, 2, 3, 4).reshape(width, (block_cols - fwd) * nb)
    across = lax.all_gather(matrix[na:, :, 0, :], "col")[:STEPS]
    across = across.transpose(1, 2, 0, 3).reshape((block_rows - na) * nb, width)

    wide = block_cols * nb
    vmem = pl.BlockSpec(memory_space=pltpu.VMEM)
    smem = pl.BlockSpec(memory_space=pltpu.SMEM)
    solved, top = pl.pallas_call(
        functools.partial(
            factor_kernel, nb=nb, na=na, rows_dev=rows_dev, cols_dev=cols_dev, fwd=fwd
        ),
        out_shape=[
            jax.ShapeDtypeStruct((2, width, wide), BF16),
            jax.ShapeDtypeStruct((na, nb, nb), F32),
        ],
        in_specs=[smem, vmem, vmem],
        out_specs=[vmem, vmem],
        scratch_shapes=[
            pltpu.VMEM((nb, 2 * nb), F32),
            pltpu.VMEM((width, width), BF16),
            pltpu.VMEM((width, width), BF16),
            pltpu.VMEM((width, nb), F32),
            pltpu.VMEM((width, side.shape[1]), BF16),
            pltpu.VMEM((width, side.shape[1]), BF16),
            pltpu.VMEM((width, wide), BF16),
            pltpu.VMEM((width, wide), BF16),
        ],
        compiler_params=pltpu.CompilerParams(vmem_limit_bytes=56 << 20),
        name="factor",
    )(place, lead, side)
    out = pl.pallas_call(
        functools.partial(close_kernel, nb=nb, na=na, block_rows=block_rows, block_cols=block_cols),
        out_shape=jax.ShapeDtypeStruct((block_rows * nb * block_cols, nb), F32),
        in_specs=[smem, vmem, vmem, vmem, vmem],
        out_specs=vmem,
        compiler_params=pltpu.CompilerParams(vmem_limit_bytes=56 << 20),
        name="close",
    )(place, across, matrix.reshape(-1, nb), solved, top)
    return out.reshape(matrix.shape)


def solution(mesh):
    placed = (P(None, "row", None, "col"),)
    return jax.shard_map(
        local, mesh=mesh, in_specs=placed, out_specs=P(None, "row", None, "col"), check_vma=False
    )
```

time: 1410 us -> 234 us (0.17)
  waiting for transfers between devices: 1070 us -> 133 us
  other arithmetic: 214 us -> 0.55 us
  Pallas kernels: 0 us -> 61.8 us
  matrix products: 37.2 us -> 0 us
  local copies, waits for them, and re-layouts: 56.8 us -> 23.9 us
    psum x24 -> x0, waiting for transfers between devices: 1070 us -> none  [spread(): return lax.psum(block, axis)]
    another operation x40 -> x1, other arithmetic: 184 us -> 0.55 us  [local(): place = jnp.stack([my_row, my_col]).astype(jnp.int32)]
    all_gather x0 -> x3, waiting for transfers between devices: none -> 133 us  [the longest x1 58.5 us: local(): across = lax.all_gather(matrix[na:, :, 0, :], 'col')[:STEPS]]
    pallas_call x0 -> x2, Pallas kernels: none -> 61.8 us  [the longest x1 54.7 us: local(): pl.pallas_call(functools.partial(factor_kernel, nb=nb, na=na, rows_dev=ro...]
    dot_general x16 -> x0, matrix products: 34.9 us -> none  [product(): jnp.dot(left_rows, right_rows.T, precision=lax.Precision.HIGHEST, preferr...]
    select_n x32 -> x0, other arithmetic: 22.8 us -> none  [the longest x23 18.9 us: spread(): jnp.where(lax.axis_index(axis) == source, block, jnp.zeros_like(block))]
    unnamed x69 -> x3, local copies, waits for them, and re-layouts: 21.1 us -> 6.12 us
  transfers between devices with their start and end apart: 24 -> 3, of which waited for: 24 -> 3; matrix products, arithmetic and copies ran while one was open for 1% -> 6% of each run, Pallas kernels for 0% -> 0%
where the time goes in v1:
time: 234 us; the launch traced here: 232 us
  waiting for transfers between devices  133 us (57%)
  Pallas kernels  61.8 us (26%)
  local copies, waits for them, and re-layouts  23.9 us (10%)
  between operations  13.1 us (6%)
    all_gather x1, waiting for transfers between devices, local(): across = lax.all_gather(matrix[na:, :, 0, :], 'col')[:STEPS]  58.5 us
    all_gather x1, waiting for transfers between devices, local(): lead = lax.all_gather(first, ('row', 'col'))  57.7 us
    pallas_call x1, Pallas kernels, local(): pl.pallas_call(functools.partial(factor_kernel, nb=nb, na=na, rows_dev=ro...  54.7 us
    all_gather x1, waiting for transfers between devices, local(): side = lax.all_gather(side, 'row')  16.3 us
    pallas_call x1, Pallas kernels, local(): pl.pallas_call(functools.partial(close_kernel, nb=nb, na=na, block_rows=b...  7.12 us
    unnamed x3, local copies, waits for them, and re-layouts  6.12 us
  transfers between devices with their start and end apart: 3, of which 3 were waited for; matrix products, arithmetic and copies ran while one was open for 6% of the time, Pallas kernels for 0%

profile of v1, /device:TPU:8, one launch (start us, length us, event | category | flops | bytes accessed | tf_op | source)
XLA Modules:
  0.0 232.0 jit_solution(4776433487460757083)
XLA Ops:
  6.5 0.0 all-gather.11.cloned.1.call-start
  6.5 1.2 slice.11
  7.7 0.8 copy.18
  8.5 0.0 all-gather.11.cloned.1.call-update
  8.5 0.0 all-gather.7.cloned.1.call-start
  8.6 2.5 %slice.9 = f32[6,128,1,128]{3,2,1,0:T(1,128)} slice(f32[8,128,4,128]{3,2,1,0:T(4,128)} %param.1), slice={[2:8], [0:128], [0:1], [0:128]} | slice | bytes 786432 | tf_op jit(solution)/shard_map/slice | solution.py:203
  11.0 0.0 all-gather.7.cloned.1.call-update
  11.0 0.0 all-gather.9.cloned.1.call-start
  11.1 1.8 slice.10
  12.9 0.0 all-gather.9.cloned.1.call-update
  12.9 0.6 pad_add_fusion.place
  13.5 16.3 %all-gather.11.cloned.1.call-done = f32[8,128,3,128]{3,1,2,0:T(8,128)} async-done(((f32[2,128,3,128]{3,1,2,0:T(8,128)}), f32[8,128,3,128]{3,1,2,0:T(8,128)}) %all-gather.11.cloned.1.call-update) | async-done | bytes 1572880 | tf_op jit(solution)/shard_map/all_gather | solution.py:201
  29.8 1.8 copy.14
  31.6 0.6 reshape.22
  32.3 1.6 copy.15.side
  33.9 58.5 %all-gather.7.cloned.1.call-done = f32[48,128,1,128]{3,1,2,0:T(8,128)} async-done(((f32[6,128,1,128]{3,1,2,0:T(8,128)}), f32[48,128,1,128]{3,1,2,0:T(8,128)}) %all-gather.7.cloned.1.call-update) | async-done | bytes 3145744 | tf_op jit(solution)/shard_map/all_gather | solution.py:203
  92.4 3.7 %copy.10 = f32[8,6,128,128]{3,0,2,1:T(8,128)S(1)} copy(f32[8,6,128,128]{3,2,1,0:T(8,128)} %bitcast.31) | data formatting | bytes 6291456 | tf_op jit(solution)/shard_map/all_gather | solution.py:203
  96.1 2.4 %copy.24 = f32[96,8,8,128]{3,1,2,0:T(8,128)} copy(f32[96,8,8,128]{3,2,1,0:T(8,128)S(1)} %bitcast.26) | data formatting | bytes 6291456
  98.5 57.7 %all-gather.9.cloned.1.call-done = f32[64,128,1,128]{3,1,2,0:T(8,128)} async-done(((f32[2,128,1,128]{3,1,2,0:T(8,128)}), f32[64,128,1,128]{3,1,2,0:T(8,128)}) %all-gather.9.cloned.1.call-update) | async-done | bytes 4194320 | tf_op jit(solution)/shard_map/all_gather | solution.py:197
  156.2 4.6 %copy.12 = f32[4,8,2,128,128]{4,1,3,0,2:T(8,128)S(1)} copy(f32[4,8,2,128,128]{4,3,2,1,0:T(8,128)} %bitcast.30) | data formatting | bytes 8388608 | tf_op jit(solution)/shard_map/reshape | solution.py:198
  160.8 3.0 %copy.23 = f32[128,8,8,128]{3,1,2,0:T(8,128)} copy(f32[128,8,8,128]{3,2,1,0:T(8,128)S(1)} %bitcast.25) | data formatting | bytes 8388608
  163.7 54.7 %factor.1 = (bf16[2,1024,512]{2,1,0:T(8,128)(2,1)}, f32[2,128,128]{2,1,0:T(8,128)}) custom-call(s32[2]{0:T(128)} %pad_add_fusion.place, f32[1024,1024]{1,0:T(8,128)} %bitcast.24, f32[1024,384]{1,0:T(8,128)} %copy.15.side), custom_call_target="tpu_custom_call" | custom-call | tf_op jit(solution)/shard_map/factor/pallas_call | solution.py:209
  218.4 7.1 %close.1 = f32[4096,128]{1,0:T(8,128)} custom-call(s32[2]{0:T(128)} %pad_add_fusion.place, f32[768,1024]{1,0:T(8,128)} %bitcast.27, f32[4096,128]{1,0:T(8,128)} %bitcast.29, bf16[2,1024,512]{2,1,0:T(8,128)(2,1)} %get-tuple-element.7.solved, f32[2,128,128]{2,1,0:T(8,128)} %get-tuple-element.8.top), custom_call_target="tpu_custom_call" | custom-call | tf_op jit(solution)/shard_map/close/pallas_call | solution.py:232
Async XLA Ops:
  6.5 23.2 %all-gather.11.cloned.1.call-start = ((), (), s32[]{:S(2)}) async-start(), calls=%async_computation.2 | async-start | bytes 1966080 | tf_op jit(solution)/shard_map/all_gather | solution.py:201
  8.5 83.9 %all-gather.7.cloned.1.call-start = ((), (), s32[]{:S(2)}) async-start(), calls=%async_computation | async-start | bytes 3538944 | tf_op jit(solution)/shard_map/all_gather | solution.py:203
  11.0 145.1 %all-gather.9.cloned.1.call-start = ((), (), s32[]{:S(2)}) async-start(), calls=%async_computation.1 | async-start | bytes 4325376 | tf_op jit(solution)/shard_map/all_gather | solution.py:197
Sparse Core Ops, SparseCore 0:
  8.9 20.8 all-gather.10
  31.9 60.4 all-gather.6
  95.5 60.6 all-gather.8

commit v2 on v1

v2 whole, which is shorter than its diff:
```python
import functools

import jax
import jax.numpy as jnp
from jax import lax
from jax.experimental import pallas as pl
from jax.experimental.pallas import tpu as pltpu
from jax.sharding import PartitionSpec as P

STEPS = 8
PANEL = 16
F32 = jnp.float32
BF16 = jnp.bfloat16


def split2(x):
    high = x.astype(BF16)
    return high, (x - high.astype(F32)).astype(BF16)


def split3(x):
    high = x.astype(BF16)
    rest = x - high.astype(F32)
    mid = rest.astype(BF16)
    return high, mid, (rest - mid.astype(F32)).astype(BF16)


def contract(left, right, dims):
    return lax.dot_general(left, right, (dims, ((), ())), preferred_element_type=F32)


def gram(rows_in, rows_wide):
    h, m, l = split3(rows_in)
    hw, mw, lw = split3(rows_wide)
    left = jnp.concatenate([h, h, m, m, h, l], 0)
    right = jnp.concatenate([hw, mw, hw, mw, lw, hw], 0)
    return contract(left, right, ((0,), (0,)))


def three(left, right, dims):
    (lh, lm), (rh, rm) = left, right
    return contract(lh, rh, dims) + (contract(lh, rm, dims) + contract(lm, rh, dims))


def factor_tile(tile, nb, filler):
    for turn, first in enumerate(range(0, nb, PANEL)):
        rows = [tile[pl.ds(first + i, 8, stride=0), :] for i in range(PANEL)]
        left = [r[:, :nb] for r in rows]
        right = [r[:, nb:] for r in rows]
        entry = {}
        for i in range(PANEL):
            for s in range(i + 1):
                lane = first + i
                entry[i, s] = jnp.broadcast_to(left[s][:, lane : lane + 1], (8, nb))
        for s in range(PANEL):
            scale = lax.rsqrt(entry[s, s])
            left[s] = left[s] * scale
            right[s] = right[s] * scale
            for i in range(s + 1, PANEL):
                entry[i, s] = entry[i, s] * scale
            for i in range(s + 1, PANEL):
                for t in range(s + 1, i + 1):
                    entry[i, t] = entry[i, t] - entry[i, s] * entry[t, s]
            for i in range(s + 1, PANEL):
                left[i] = left[i] - entry[i, s] * left[s]
                right[i] = right[i] - entry[i, s] * right[s]
        for s in range(PANEL):
            tile[first + s : first + s + 1, :nb] = left[s][:1]
            tile[first + s : first + s + 1, nb:] = right[s][:1]
        filler(turn)
        after = first + PANEL
        if after < nb:
            done = tile[first:after, :]
            tile[after:, :] = tile[after:, :] - gram(done[:, :nb], done)[after:, :]


def sweep_kernel(*refs, phase, last, nb, na, rows_dev, cols_dev, fwd, n_pieces, n_low):
    place = refs[0]
    pieces = refs[1 : 1 + n_pieces]
    side = refs[1 + n_pieces]
    refs = refs[2 + n_pieces :]
    if phase:
        old, old_col, old_top = refs[:3]
        refs = refs[3:]
    outs, (grid_ref, col_ref, tile, lcol, rrow) = refs[:-5], refs[-5:]
    my_row, my_col = place[0], place[1]
    lead = STEPS * nb
    c0 = phase * rows_dev * nb
    rows = c0 + rows_dev * nb
    n_side = side.shape[2]
    wide = lead + n_side * nb
    top = outs[-1]
    ii = lax.broadcasted_iota(jnp.int32, (nb, nb), 0)
    jj = lax.broadcasted_iota(jnp.int32, (nb, nb), 1)
    eye = jnp.where(ii == jj, 1.0, 0.0).astype(F32)
    MM = ((1,), (0,))

    for array, (back_hi, back_lo) in zip(
        pieces, [(h, l) for l in range(2) for h in range(rows_dev // 2)], strict=True
    ):
        row_hi = lax.rem(my_row // 2 - back_hi + rows_dev // 2, rows_dev // 2)
        row_lo = lax.rem(lax.rem(my_row, 2) + back_lo, 2)
        at = pl.multiple_of(c0 + (row_hi * 2 + row_lo) * nb, nb)
        n_high = cols_dev // n_low
        for i in range(cols_dev):
            back_l, back_h = i // n_high, i % n_high
            col_hi = lax.rem(my_col // n_low - back_h + n_high, n_high)
            col_lo = lax.rem(lax.rem(my_col, n_low) - back_l + n_low, n_low)
            col = col_hi * n_low + col_lo

            @pl.when(col < STEPS)
            def _():
                grid_ref[pl.ds(at, nb), pl.ds(pl.multiple_of(col * nb, nb), nb)] = array[i]

    for p in range(rows_dev):
        for b in range(n_side):
            grid_ref[c0 + p * nb : c0 + p * nb + nb, lead + b * nb : lead + b * nb + nb] = side[p, phase, b]
    if phase:
        grid_ref[:c0, c0:] = old[...]
        grid_ref[c0:rows, c0:] = grid_ref[c0:rows, c0:] - three(
            split2(grid_ref[c0:rows, :c0]), split2(grid_ref[:c0, c0:]), MM
        )
        col_ref[...] = old_col[...]
        top[...] = old_top[...]
    else:
        col_ref[...] = jnp.zeros(col_ref.shape, F32)
        top[...] = jnp.zeros(top.shape, F32)
    lcol[...] = jnp.zeros(lcol.shape, BF16)
    rrow[...] = jnp.zeros(rrow.shape, BF16)

    def pending(i):
        at = slice(i * nb, i * nb + nb)
        grid_ref[at, c0:] = grid_ref[at, c0:] - three((lcol[0, at, :], lcol[1, at, :]), (rrow[0], rrow[1]), MM)

    @pl.loop(phase * rows_dev, (phase + 1) * rows_dev)
    def _(k):
        base = pl.multiple_of(k * nb, nb)
        here = pl.ds(base, nb)
        inner = pl.ds(pl.multiple_of(base - c0, nb), nb)
        tile[:, :nb] = grid_ref[here, here] - three(
            (lcol[0, here, :], lcol[1, here, :]), (rrow[0, :, inner], rrow[1, :, inner]), MM
        )
        tile[:, nb:] = eye

        def filler(turn):
            for i in range(rows // nb):
                if i % (nb // PANEL) == turn:
                    pending(i)

        factor_tile(tile, nb, filler)
        g = tile[:, nb:]
        gs = split2(g)

        @pl.when(k == my_col)
        def _():
            for a in range(na):
                row = a * rows_dev + my_row

                @pl.when(row == k)
                def _():
                    top[a] = jnp.where(ii >= jj, tile[:, :nb].T, 0.0)

                @pl.when(row > k)
                def _():
                    block = grid_ref[here, pl.ds(pl.multiple_of(row * nb, nb), nb)]
                    top[a] = three(gs, split2(block), MM).T

            at = lax.broadcasted_iota(jnp.int32, (rows, nb), 0)
            found = three(split2(grid_ref[:rows, here]), gs, ((1,), (1,)))
            col_ref[:rows, :] = jnp.where(at < base, -found, 0.0)
            col_ref[here, :] = g.T

        r = three(split2(gram(g, g)), split2(grid_ref[here, c0:]), MM)
        at = lax.broadcasted_iota(jnp.int32, (rows, nb), 0)
        column = jnp.where((at >= base) & (at < base + nb), 0.0, grid_ref[:rows, here])
        lcol[0], lcol[1] = split2(column)
        rrow[0], rrow[1] = split2(r)
        grid_ref[here, c0:] = r

    for i in range(rows // nb):
        pending(i)
    if last:
        solved = outs[0]
        first = col_ref[...]
        if not fwd:
            first = jnp.where(my_col < STEPS, first, grid_ref[:, lead : lead + nb])
        solved[0, :, :nb], solved[1, :, :nb] = split2(first)
        solved[0, :, nb:], solved[1, :, nb:] = split2(grid_ref[:, lead + (nb if not fwd else 0) :])
    else:
        outs[0][...] = grid_ref[:rows, rows:]
        outs[1][...] = col_ref[...]


def close_kernel(place, across, mine, solved, top, out, left_h, left_m, *, nb, na, block_rows, block_cols):
    my_col = place[1]
    for k in range(STEPS):
        at = slice(k * nb, k * nb + nb)
        left_h[:, at], left_m[:, at] = split2(across[k])
    prod = three((left_h[...], left_m[...]), (solved[0], solved[1]), ((1,), (0,)))
    is_panel = my_col < STEPS
    for a in range(block_rows):
        for b in range(block_cols):
            where = pl.ds(a * nb * block_cols + b, nb, stride=block_cols)
            if a < na:
                out[where, :] = top[a] if b == 0 else jnp.zeros((nb, nb), F32)
            else:
                part = prod[(a - na) * nb : (a - na + 1) * nb, b * nb : (b + 1) * nb]
                old = mine[where, :]
                if b == 0:
                    out[where, :] = jnp.where(is_panel, part, old - part)
                else:
                    out[where, :] = old - part


def local(matrix):
    rows_dev = lax.axis_size("row")
    cols_dev = lax.axis_size("col")
    my_row = lax.axis_index("row")
    my_col = lax.axis_index("col")
    block_rows, nb, block_cols, _ = matrix.shape
    na = STEPS // rows_dev
    fwd = STEPS // cols_dev
    lead = STEPS * nb
    wide = block_cols * nb
    n_side = block_cols - fwd
    n_low = 2
    n_high = cols_dev // n_low
    place = jnp.stack([my_row, my_col]).astype(jnp.int32)

    def step_to(x, axis, size, low, back_high, back_low):
        pairs = []
        for i in range(size):
            high, rest = divmod(i, low)
            pairs.append((i, (high + back_high) % (size // low) * low + (rest + back_low) % low))
        return lax.ppermute(x, axis, pairs)

    side = matrix[:na, :, fwd:, :].transpose(0, 2, 1, 3)
    side = lax.all_gather(side, "row")
    across = lax.all_gather(matrix[na:, :, 0, :], "col")
    across = across.reshape(cols_dev, (block_rows - na) * nb, nb)

    phases = []
    for a in range(na):
        block = matrix[a, :, 0, :]
        line = jnp.stack([block] + [step_to(block, "col", cols_dev, n_low, h, 0) for h in range(1, n_high)])
        strip = jnp.concatenate([line, step_to(line, "col", cols_dev, n_low, 0, 1)])
        near = [strip] + [step_to(strip, "row", rows_dev, 2, h, 0) for h in range(1, rows_dev // 2)]
        phases.append(near + [step_to(s, "row", rows_dev, 2, 0, 1) for s in near])

    vmem = pl.BlockSpec(memory_space=pltpu.VMEM)
    smem = pl.BlockSpec(memory_space=pltpu.SMEM)
    params = pltpu.CompilerParams(vmem_limit_bytes=56 << 20)
    carried = []
    for phase, pieces in enumerate(phases):
        last = phase == na - 1
        c0 = phase * rows_dev * nb
        rows = c0 + rows_dev * nb
        width = lead + n_side * nb
        out_shape = [jax.ShapeDtypeStruct((na, nb, nb), F32)]
        if last:
            out_shape = [jax.ShapeDtypeStruct((2, lead, wide), BF16)] + out_shape
        else:
            out_shape = [
                jax.ShapeDtypeStruct((rows, width - rows), F32),
                jax.ShapeDtypeStruct((lead, nb), F32),
            ] + out_shape
        carried = pl.pallas_call(
            functools.partial(
                sweep_kernel,
                phase=phase,
                last=last,
                nb=nb,
                na=na,
                rows_dev=rows_dev,
                cols_dev=cols_dev,
                fwd=fwd,
                n_pieces=len(pieces),
                n_low=n_low,
            ),
            out_shape=out_shape,
            in_specs=[smem] + [vmem] * (len(pieces) + 1 + len(carried)),
            out_specs=[vmem] * len(out_shape),
            scratch_shapes=[
                pltpu.VMEM((lead, width), F32),
                pltpu.VMEM((lead, nb), F32),
                pltpu.VMEM((nb, 2 * nb), F32),
                pltpu.VMEM((2, rows, nb), BF16),
                pltpu.VMEM((2, nb, width - c0), BF16),
            ],
            compiler_params=params,
            cost_estimate=pl.CostEstimate(flops=3 * 10**10, bytes_accessed=10**7, transcendentals=0),
            name="sweep%d" % phase,
        )(place, *pieces, side, *carried)
    solved, top = carried
    out = pl.pallas_call(
        functools.partial(close_kernel, nb=nb, na=na, block_rows=block_rows, block_cols=block_cols),
        out_shape=jax.ShapeDtypeStruct((block_rows * nb * block_cols, nb), F32),
        in_specs=[smem, vmem, vmem, vmem, vmem],
        out_specs=vmem,
        scratch_shapes=[pltpu.VMEM(((block_rows - na) * nb, lead), BF16)] * 2,
        compiler_params=params,
        name="close",
    )(place, across, matrix.reshape(-1, nb), solved, top)
    return out.reshape(matrix.shape)


def solution(mesh):
    placed = (P(None, "row", None, "col"),)
    return jax.shard_map(
        local, mesh=mesh, in_specs=placed, out_specs=P(None, "row", None, "col"), check_vma=False
    )
```

time: 234 us -> 132 us (0.56)
  waiting for transfers between devices: 133 us -> 30.7 us
  local copies, waits for them, and re-layouts: 23.9 us -> 6.56 us
  starting transfers between devices: 0.09 us -> 14.1 us
  Pallas kernels: 61.8 us -> 65.3 us
    all_gather x2 -> x1, waiting for transfers between devices: 116 us -> 0.01 us  [local(): across = lax.all_gather(matrix[na:, :, 0, :], 'col')]
    ppermute x0 -> x14, waiting for transfers between devices: none -> 30.7 us  [step_to(): return lax.ppermute(x, axis, pairs)]
    all_gather x1, waiting for transfers between devices: 16.3 us -> 0.02 us  [local(): side = lax.all_gather(side, 'row')]
    ppermute x0 -> x14, starting transfers between devices: none -> 14.1 us  [step_to(): return lax.ppermute(x, axis, pairs)]
    reshape x3 -> x0, local copies, waits for them, and re-layouts: 6.81 us -> none  [the longest x1 4.56 us: local(): lead = lead.reshape(rows_dev, cols_dev, na, nb, nb)[:, :STEPS]]
    all_gather x2 -> x0, local copies, waits for them, and re-layouts: 5.53 us -> none  [the longest x1 3.68 us: local(): across = lax.all_gather(matrix[na:, :, 0, :], 'col')[:STEPS]]
    unnamed x3 -> x19, local copies, waits for them, and re-layouts: 6.12 us -> 1.6 us
    pallas_call x1 -> x2, Pallas kernels: 54.7 us -> 58.2 us  [local(): pl.pallas_call(functools.partial(sweep_kernel, phase=phase, last=last, nb...]
  transfers between devices with their start and end apart: 3 -> 16, of which waited for: 3 -> 6; matrix products, arithmetic and copies ran while one was open for 6% -> 4% of each run, Pallas kernels for 0% -> 44%
where the time goes in v2:
time: 132 us; the launch traced here: 131 us
  Pallas kernels  65.3 us (49%)
  waiting for transfers between devices  30.7 us (23%)
  starting transfers between devices  14.1 us (11%)
  between operations  13.6 us (10%)
  local copies, waits for them, and re-layouts  6.56 us (5%)
    pallas_call x2, Pallas kernels, local(): pl.pallas_call(functools.partial(sweep_kernel, phase=phase, last=last, nb...  58.2 us
    ppermute x14, waiting for transfers between devices, step_to(): return lax.ppermute(x, axis, pairs)  30.7 us
    ppermute x14, starting transfers between devices, step_to(): return lax.ppermute(x, axis, pairs)  14.1 us
    pallas_call x1, Pallas kernels, local(): pl.pallas_call(functools.partial(close_kernel, nb=nb, na=na, block_rows=b...  7.16 us
  transfers between devices with their start and end apart: 16, of which 6 were waited for; matrix products, arithmetic and copies ran while one was open for 4% of the time, Pallas kernels for 44%

profile of v2, /device:TPU:8, one launch (start us, length us, event | category | flops | bytes accessed | tf_op | source)
XLA Modules:
  0.0 131.0 jit_solution(8166847154542620329)
XLA Ops:
  6.5 1.1 fusion
  7.7 1.6 %collective-permute-start.7 = (f32[128,128]{1,0:T(8,128)S(1)}, f32[128,128]{1,0:T(8,128)S(1)}, u32[]{:S(2)}, u32[]{:S(2)}) collective-permute-start(f32[128,128]{1,0:T(8,128)S(1)} %bitcast.41), channel_id=1, source_target_pairs={{0,2},{1,3},{2,4},{3,5},{4,6},{5,7},{6,0},{7,1},{8,10},{9,11},{10,... | collective-permute-start | bytes 196616 | tf_op jit(solution)/shard_map/ppermute | solution.py:235
  9.3 1.1 collective-permute-start.8
  10.4 1.9 %collective-permute-start.9 = (f32[128,128]{1,0:T(8,128)S(1)}, f32[128,128]{1,0:T(8,128)S(1)}, u32[]{:S(2)}, u32[]{:S(2)}) collective-permute-start(f32[128,128]{1,0:T(8,128)S(1)} %bitcast.43), channel_id=1, source_target_pairs={{0,6},{1,7},{2,0},{3,1},{4,2},{5,3},{6,4},{7,5},{8,14},{9,15},{10,... | collective-permute-start | bytes 196616 | tf_op jit(solution)/shard_map/ppermute | solution.py:235
  12.4 3.6 %collective-permute-start.1 = (f32[128,128]{1,0:T(8,128)S(1)}, f32[128,128]{1,0:T(8,128)S(1)}, u32[]{:S(2)}, u32[]{:S(2)}) collective-permute-start(f32[128,128]{1,0:T(8,128)S(1)} %bitcast.37), channel_id=1, source_target_pairs={{0,4},{1,5},{2,6},{3,7},{4,0},{5,1},{6,2},{7,3},{8,12},{9,13},{10,... | collective-permute-start | bytes 196616 | tf_op jit(solution)/shard_map/ppermute | solution.py:235
  16.0 1.2 slice.14
  17.2 0.8 copy.14
  18.2 1.4 %collective-permute-done.9 = f32[128,128]{1,0:T(8,128)S(1)} collective-permute-done((f32[128,128]{1,0:T(8,128)S(1)}, f32[128,128]{1,0:T(8,128)S(1)}, u32[]{:S(2)}, u32[]{:S(2)}) %collective-permute-start.9) | collective-permute-done | bytes 65568 | tf_op jit(solution)/shard_map/ppermute | solution.py:235
  19.6 1.9 %collective-permute-start.10 = (f32[4,128,128]{2,1,0:T(8,128)S(1)}, f32[4,128,128]{2,1,0:T(8,128)S(1)}, u32[]{:S(2)}, u32[]{:S(2)}) collective-permute-start(f32[4,128,128]{2,1,0:T(8,128)S(1)} %pad_maximum_fusion.1), channel_id=1, source_target_pairs={{0,1},{1,0},{2,3},{3,2},{4,5},{5,4},{6,7},{7,6},{8,9},{9,8},{10,11... | collective-permute-start | bytes 786440 | tf_op jit(solution)/shard_map/ppermute | solution.py:235
  21.5 1.0 collective-permute-done.2
  22.4 1.6 %collective-permute-start.3 = (f32[4,128,128]{2,1,0:T(8,128)S(1)}, f32[4,128,128]{2,1,0:T(8,128)S(1)}, u32[]{:S(2)}, u32[]{:S(2)}) collective-permute-start(f32[4,128,128]{2,1,0:T(8,128)S(1)} %pad_maximum_fusion), channel_id=1, source_target_pairs={{0,1},{1,0},{2,3},{3,2},{4,5},{5,4},{6,7},{7,6},{8,9},{9,8},{10,11... | collective-permute-start | bytes 786440 | tf_op jit(solution)/shard_map/ppermute | solution.py:235
  24.1 4.8 %collective-permute-done.10 = f32[4,128,128]{2,1,0:T(8,128)S(1)} collective-permute-done((f32[4,128,128]{2,1,0:T(8,128)S(1)}, f32[4,128,128]{2,1,0:T(8,128)S(1)}, u32[]{:S(2)}, u32[]{:S(2)}) %collective-permute-start.10) | collective-permute-done | bytes 262176 | tf_op jit(solution)/shard_map/ppermute | solution.py:235
  28.9 1.3 %collective-permute-start.11 = (f32[8,128,128]{2,1,0:T(8,128)S(1)}, f32[8,128,128]{2,1,0:T(8,128)S(1)}, u32[]{:S(2)}, u32[]{:S(2)}) collective-permute-start(f32[8,128,128]{2,1,0:T(8,128)S(1)} %constant_dynamic-update-slice_fusion.5.refs_1_), channel_id=1, source_target_pairs={{0,16},{8,24},{16,0},{24,8},{1,17},{9,25},{17,1},{25,9},{2,18},{10... | collective-permute-start | bytes 1572872 | tf_op jit(solution)/shard_map/ppermute | solution.py:235
  30.2 2.7 %collective-permute-done.3 = f32[4,128,128]{2,1,0:T(8,128)S(1)} collective-permute-done((f32[4,128,128]{2,1,0:T(8,128)S(1)}, f32[4,128,128]{2,1,0:T(8,128)S(1)}, u32[]{:S(2)}, u32[]{:S(2)}) %collective-permute-start.3) | collective-permute-done | bytes 262176 | tf_op jit(solution)/shard_map/ppermute | solution.py:235
  33.0 0.5 collective-permute-start.4
  33.5 14.5 %collective-permute-done.11.refs_2_ = f32[8,128,128]{2,1,0:T(8,128)S(1)} collective-permute-done((f32[8,128,128]{2,1,0:T(8,128)S(1)}, f32[8,128,128]{2,1,0:T(8,128)S(1)}, u32[]{:S(2)}, u32[]{:S(2)}) %collective-permute-start.11) | collective-permute-done | bytes 524320 | tf_op jit(solution)/shard_map/ppermute | solution.py:235
  48.0 2.6 %slice.12 = f32[6,128,1,128]{3,2,1,0:T(1,128)} slice(f32[8,128,4,128]{3,2,1,0:T(4,128)} %param.1), slice={[2:8], [0:128], [0:1], [0:128]} | slice | bytes 786432 | tf_op jit(solution)/shard_map/slice | solution.py:239
  50.7 0.6 pad_add_fusion.refs_0_.place
  51.3 0.3 collective-permute-start.5
  51.6 6.3 %collective-permute-done.4.refs_2_ = f32[8,128,128]{2,1,0:T(8,128)S(1)} collective-permute-done((f32[8,128,128]{2,1,0:T(8,128)S(1)}, f32[8,128,128]{2,1,0:T(8,128)S(1)}, u32[]{:S(2)}, u32[]{:S(2)}) %collective-permute-start.4) | collective-permute-done | bytes 524320 | tf_op jit(solution)/shard_map/ppermute | solution.py:235
  58.0 0.8 copy-done.4
  58.8 27.7 %sweep0.1 = (f32[512,896]{1,0:T(8,128)}, f32[1024,128]{1,0:T(8,128)}, f32[2,128,128]{2,1,0:T(8,128)}) custom-call(s32[2]{0:T(128)} %pad_add_fusion.refs_0_.place, f32[8,128,128]{2,1,0:T(8,128)} %copy-done.1, f32[8,128,128]{2,1,0:T(8,128)} %copy-done.2, f32[8,128,128]{2,1,0:T(8,128)} %copy-done.4, f32[8,128,128]{2,1,0:T(8,128)} %collective-permute-done.13.refs_4_, ...), custom_call_target="tpu_custom_call" | custom-call | flops 30000001024 | bytes 10000000 | tf_op jit(solution)/shard_map/sweep0/pallas_call | solution.py:267
  86.5 30.5 %sweep1.1 = (bf16[2,1024,512]{2,1,0:T(8,128)(2,1)}, f32[2,128,128]{2,1,0:T(8,128)}) custom-call(s32[2]{0:T(128)} %pad_add_fusion.refs_0_.place, f32[8,128,128]{2,1,0:T(8,128)} %copy-done, f32[8,128,128]{2,1,0:T(8,128)} %copy-done.3, f32[8,128,128]{2,1,0:T(8,128)} %collective-permute-done.5.refs_3_, f32[8,128,128]{2,1,0:T(8,128)} %collective-permute-done.6.refs_4_, ...), custom_call_target="tpu_custom_call" | custom-call | flops 30000001024 | bytes 10000000 | tf_op jit(solution)/shard_map/sweep1/pallas_call | solution.py:267
  117.0 7.2 %close.1 = f32[4096,128]{1,0:T(8,128)} custom-call(s32[2]{0:T(128)} %pad_add_fusion.refs_0_.place, f32[8,768,128]{2,1,0:T(8,128)} %bitcast.33, f32[4096,128]{1,0:T(8,128)} %bitcast.32, bf16[2,1024,512]{2,1,0:T(8,128)(2,1)} %get-tuple-element.13.solved, f32[2,128,128]{2,1,0:T(8,128)} %get-tuple-element.14.top), custom_call_target="tpu_custom_call" | custom-call | tf_op jit(solution)/shard_map/close/pallas_call | solution.py:295
  (40 shorter events, 0.4 us)
Async XLA Ops:
  6.5 51.4 %all-gather.7.cloned.1.call-start = ((), (), s32[]{:S(2)}) async-start(), calls=%async_computation.1 | async-start | bytes 1966080 | tf_op jit(solution)/shard_map/all_gather | solution.py:238
  7.7 10.4 %collective-permute-start.7 = (f32[128,128]{1,0:T(8,128)S(1)}, f32[128,128]{1,0:T(8,128)S(1)}, u32[]{:S(2)}, u32[]{:S(2)}) collective-permute-start(f32[128,128]{1,0:T(8,128)S(1)} %bitcast.41), channel_id=1, source_target_pairs={{0,2},{1,3},{2,4},{3,5},{4,6},{5,7},{6,0},{7,1},{8,10},{9,11},{10,... | collective-permute-start | bytes 196616 | tf_op jit(solution)/shard_map/ppermute | solution.py:235
  9.3 8.9 %collective-permute-start.8 = (f32[128,128]{1,0:T(8,128)S(1)}, f32[128,128]{1,0:T(8,128)S(1)}, u32[]{:S(2)}, u32[]{:S(2)}) collective-permute-start(f32[128,128]{1,0:T(8,128)S(1)} %bitcast.42), channel_id=1, source_target_pairs={{0,4},{1,5},{2,6},{3,7},{4,0},{5,1},{6,2},{7,3},{8,12},{9,13},{10,... | collective-permute-start | bytes 196616 | tf_op jit(solution)/shard_map/ppermute | solution.py:235
  10.4 9.2 %collective-permute-start.9 = (f32[128,128]{1,0:T(8,128)S(1)}, f32[128,128]{1,0:T(8,128)S(1)}, u32[]{:S(2)}, u32[]{:S(2)}) collective-permute-start(f32[128,128]{1,0:T(8,128)S(1)} %bitcast.43), channel_id=1, source_target_pairs={{0,6},{1,7},{2,0},{3,1},{4,2},{5,3},{6,4},{7,5},{8,14},{9,15},{10,... | collective-permute-start | bytes 196616 | tf_op jit(solution)/shard_map/ppermute | solution.py:235
  12.3 9.1 %collective-permute-start = (f32[128,128]{1,0:T(8,128)S(1)}, f32[128,128]{1,0:T(8,128)S(1)}, u32[]{:S(2)}, u32[]{:S(2)}) collective-permute-start(f32[128,128]{1,0:T(8,128)S(1)} %bitcast.36), channel_id=1, source_target_pairs={{0,2},{1,3},{2,4},{3,5},{4,6},{5,7},{6,0},{7,1},{8,10},{9,11},{10,... | collective-permute-start | bytes 196616 | tf_op jit(solution)/shard_map/ppermute | solution.py:235
  12.4 9.0 %collective-permute-start.1 = (f32[128,128]{1,0:T(8,128)S(1)}, f32[128,128]{1,0:T(8,128)S(1)}, u32[]{:S(2)}, u32[]{:S(2)}) collective-permute-start(f32[128,128]{1,0:T(8,128)S(1)} %bitcast.37), channel_id=1, source_target_pairs={{0,4},{1,5},{2,6},{3,7},{4,0},{5,1},{6,2},{7,3},{8,12},{9,13},{10,... | collective-permute-start | bytes 196616 | tf_op jit(solution)/shard_map/ppermute | solution.py:235
  18.0 99.0 %all-gather.5.cloned.1.call-start = ((), (), s32[]{:S(2)}) async-start(), calls=%async_computation | async-start | bytes 3538944 | tf_op jit(solution)/shard_map/all_gather | solution.py:239
  18.1 4.3 %collective-permute-start.2 = (f32[128,128]{1,0:T(8,128)S(1)}, f32[128,128]{1,0:T(8,128)S(1)}, u32[]{:S(2)}, u32[]{:S(2)}) collective-permute-start(f32[128,128]{1,0:T(8,128)S(1)} %bitcast.39), channel_id=1, source_target_pairs={{0,6},{1,7},{2,0},{3,1},{4,2},{5,3},{6,4},{7,5},{8,14},{9,15},{10,... | collective-permute-start | bytes 196616 | tf_op jit(solution)/shard_map/ppermute | solution.py:235
  19.6 9.3 %collective-permute-start.10 = (f32[4,128,128]{2,1,0:T(8,128)S(1)}, f32[4,128,128]{2,1,0:T(8,128)S(1)}, u32[]{:S(2)}, u32[]{:S(2)}) collective-permute-start(f32[4,128,128]{2,1,0:T(8,128)S(1)} %pad_maximum_fusion.1), channel_id=1, source_target_pairs={{0,1},{1,0},{2,3},{3,2},{4,5},{5,4},{6,7},{7,6},{8,9},{9,8},{10,11... | collective-permute-start | bytes 786440 | tf_op jit(solution)/shard_map/ppermute | solution.py:235
  22.4 10.5 %collective-permute-start.3 = (f32[4,128,128]{2,1,0:T(8,128)S(1)}, f32[4,128,128]{2,1,0:T(8,128)S(1)}, u32[]{:S(2)}, u32[]{:S(2)}) collective-permute-start(f32[4,128,128]{2,1,0:T(8,128)S(1)} %pad_maximum_fusion), channel_id=1, source_target_pairs={{0,1},{1,0},{2,3},{3,2},{4,5},{5,4},{6,7},{7,6},{8,9},{9,8},{10,11... | collective-permute-start | bytes 786440 | tf_op jit(solution)/shard_map/ppermute | solution.py:235
  28.9 29.1 %copy-start.1 = (f32[8,128,128]{2,1,0:T(8,128)}, f32[8,128,128]{2,1,0:T(8,128)S(1)}, u32[]{:S(2)}) copy-start(f32[8,128,128]{2,1,0:T(8,128)S(1)} %constant_dynamic-update-slice_fusion.5.refs_1_) | copy-start | bytes 1572868
  28.9 19.1 %collective-permute-start.11 = (f32[8,128,128]{2,1,0:T(8,128)S(1)}, f32[8,128,128]{2,1,0:T(8,128)S(1)}, u32[]{:S(2)}, u32[]{:S(2)}) collective-permute-start(f32[8,128,128]{2,1,0:T(8,128)S(1)} %constant_dynamic-update-slice_fusion.5.refs_1_), channel_id=1, source_target_pairs={{0,16},{8,24},{16,0},{24,8},{1,17},{9,25},{17,1},{25,9},{2,18},{10... | collective-permute-start | bytes 1572872 | tf_op jit(solution)/shard_map/ppermute | solution.py:235
  33.0 53.5 %copy-start = (f32[8,128,128]{2,1,0:T(8,128)}, f32[8,128,128]{2,1,0:T(8,128)S(1)}, u32[]{:S(2)}) copy-start(f32[8,128,128]{2,1,0:T(8,128)S(1)} %constant_dynamic-update-slice_fusion.refs_1_) | copy-start | bytes 1572868
  33.0 24.9 %collective-permute-start.4 = (f32[8,128,128]{2,1,0:T(8,128)S(1)}, f32[8,128,128]{2,1,0:T(8,128)S(1)}, u32[]{:S(2)}, u32[]{:S(2)}) collective-permute-start(f32[8,128,128]{2,1,0:T(8,128)S(1)} %constant_dynamic-update-slice_fusion.refs_1_), channel_id=1, source_target_pairs={{0,16},{8,24},{16,0},{24,8},{1,17},{9,25},{17,1},{25,9},{2,18},{10... | collective-permute-start | bytes 1572872 | tf_op jit(solution)/shard_map/ppermute | solution.py:235
  33.5 24.4 %collective-permute-start.12 = (f32[8,128,128]{2,1,0:T(8,128)S(1)}, f32[8,128,128]{2,1,0:T(8,128)S(1)}, u32[]{:S(2)}, u32[]{:S(2)}) collective-permute-start(f32[8,128,128]{2,1,0:T(8,128)S(1)} %constant_dynamic-update-slice_fusion.5.refs_1_), channel_id=1, source_target_pairs={{0,8},{8,0},{16,24},{24,16},{1,9},{9,1},{17,25},{25,17},{2,10},{10... | collective-permute-start | bytes 1572872 | tf_op jit(solution)/shard_map/ppermute | solution.py:235
  48.0 10.0 %copy-start.2 = (f32[8,128,128]{2,1,0:T(8,128)}, f32[8,128,128]{2,1,0:T(8,128)S(1)}, u32[]{:S(2)}) copy-start(f32[8,128,128]{2,1,0:T(8,128)S(1)} %collective-permute-done.11.refs_2_) | copy-start | bytes 1572868
  48.0 9.9 %collective-permute-start.13 = (f32[8,128,128]{2,1,0:T(8,128)S(1)}, f32[8,128,128]{2,1,0:T(8,128)}, u32[]{:S(2)}, u32[]{:S(2)}) collective-permute-start(f32[8,128,128]{2,1,0:T(8,128)S(1)} %collective-permute-done.11.refs_2_), channel_id=1, source_target_pairs={{0,8},{8,0},{16,24},{24,16},{1,9},{9,1},{17,25},{25,17},{2,10},{10... | collective-permute-start | bytes 1572872 | tf_op jit(solution)/shard_map/ppermute | solution.py:235
  51.3 35.2 %collective-permute-start.5 = (f32[8,128,128]{2,1,0:T(8,128)S(1)}, f32[8,128,128]{2,1,0:T(8,128)}, u32[]{:S(2)}, u32[]{:S(2)}) collective-permute-start(f32[8,128,128]{2,1,0:T(8,128)S(1)} %constant_dynamic-update-slice_fusion.refs_1_), channel_id=1, source_target_pairs={{0,8},{8,0},{16,24},{24,16},{1,9},{9,1},{17,25},{25,17},{2,10},{10... | collective-permute-start | bytes 1572872 | tf_op jit(solution)/shard_map/ppermute | solution.py:235
  57.9 28.5 %copy-start.3 = (f32[8,128,128]{2,1,0:T(8,128)}, f32[8,128,128]{2,1,0:T(8,128)S(1)}, u32[]{:S(2)}) copy-start(f32[8,128,128]{2,1,0:T(8,128)S(1)} %collective-permute-done.4.refs_2_) | copy-start | bytes 1572868
  57.9 28.6 %collective-permute-start.6 = (f32[8,128,128]{2,1,0:T(8,128)S(1)}, f32[8,128,128]{2,1,0:T(8,128)}, u32[]{:S(2)}, u32[]{:S(2)}) collective-permute-start(f32[8,128,128]{2,1,0:T(8,128)S(1)} %collective-permute-done.4.refs_2_), channel_id=1, source_target_pairs={{0,8},{8,0},{16,24},{24,16},{1,9},{9,1},{17,25},{25,17},{2,10},{10... | collective-permute-start | bytes 1572872 | tf_op jit(solution)/shard_map/ppermute | solution.py:235
  57.9 0.8 copy-start.4
Sparse Core Ops, SparseCore 0:
  18.1 24.6 all-gather.6
  50.8 59.8 all-gather.4

commit v3 on v2

v3 whole, which is shorter than its diff:
```python
import functools

import jax
import jax.numpy as jnp
from jax import lax
from jax.experimental import pallas as pl
from jax.experimental.pallas import tpu as pltpu
from jax.sharding import PartitionSpec as P

STEPS = 8
PANEL = 16
F32 = jnp.float32
BF16 = jnp.bfloat16


def split2(x):
    high = x.astype(BF16)
    return high, (x - high.astype(F32)).astype(BF16)


def split3(x):
    high = x.astype(BF16)
    rest = x - high.astype(F32)
    mid = rest.astype(BF16)
    return high, mid, (rest - mid.astype(F32)).astype(BF16)


def contract(left, right, dims):
    return lax.dot_general(left, right, (dims, ((), ())), preferred_element_type=F32)


def gram(rows_in, rows_wide):
    h, m, l = split3(rows_in)
    hw, mw, lw = split3(rows_wide)
    left = jnp.concatenate([h, h, m, m, h, l], 0)
    right = jnp.concatenate([hw, mw, hw, mw, lw, hw], 0)
    return contract(left, right, ((0,), (0,)))


def three(left, right, dims):
    (lh, lm), (rh, rm) = left, right
    return contract(lh, rh, dims) + (contract(lh, rm, dims) + contract(lm, rh, dims))


def factor_tile(tile, nb, filler):
    for turn, first in enumerate(range(0, nb, PANEL)):
        rows = [tile[pl.ds(first + i, 8, stride=0), :] for i in range(PANEL)]
        left = [r[:, :nb] for r in rows]
        right = [r[:, nb:] for r in rows]
        entry = {}
        for i in range(PANEL):
            for s in range(i + 1):
                lane = first + i
                entry[i, s] = jnp.broadcast_to(left[s][:, lane : lane + 1], (8, nb))
        for s in range(PANEL):
            scale = lax.rsqrt(entry[s, s])
            left[s] = left[s] * scale
            right[s] = right[s] * scale
            for i in range(s + 1, PANEL):
                entry[i, s] = entry[i, s] * scale
            for i in range(s + 1, PANEL):
                for t in range(s + 1, i + 1):
                    entry[i, t] = entry[i, t] - entry[i, s] * entry[t, s]
            for i in range(s + 1, PANEL):
                left[i] = left[i] - entry[i, s] * left[s]
                right[i] = right[i] - entry[i, s] * right[s]
        for s in range(PANEL):
            tile[first + s : first + s + 1, :nb] = left[s][:1]
            tile[first + s : first + s + 1, nb:] = right[s][:1]
        filler(turn)
        after = first + PANEL
        if after < nb:
            done = tile[first:after, :]
            tile[after:, :] = tile[after:, :] - gram(done[:, :nb], done)[after:, :]


def col_of(my_col, back_h, back_l, cols_dev, n_low):
    n_high = cols_dev // n_low
    high = lax.rem(my_col // n_low - back_h + n_high, n_high)
    return high * n_low + lax.rem(lax.rem(my_col, n_low) - back_l + n_low, n_low)


def guarded(always, condition, action):
    if always:
        action()
    else:
        pl.when(condition)(action)


def sweep_kernel(*refs, phase, last, nb, na, rows_dev, cols_dev, fwd, n_pieces, n_low):
    place = refs[0]
    pieces = refs[1 : 1 + n_pieces]
    sides = refs[1 + n_pieces : 1 + 2 * n_pieces]
    refs = refs[1 + 2 * n_pieces :]
    if phase:
        old, old_col, old_top = refs[:3]
        refs = refs[3:]
    if last:
        solved, top, solved_buf, col_ref = refs[:4]
        refs = refs[4:]
    else:
        passed, col_ref, top = refs[:3]
        refs = refs[3:]
    grid_ref, tile, held, lcol, rrow, upper, sems, out_sems = refs
    my_row, my_col = place[0], place[1]
    lead = STEPS * nb
    c0 = phase * rows_dev * nb
    rows = c0 + rows_dev * nb
    n_side = sides[0].shape[1]
    ii = lax.broadcasted_iota(jnp.int32, (nb, nb), 0)
    jj = lax.broadcasted_iota(jnp.int32, (nb, nb), 1)
    eye = jnp.where(ii == jj, 1.0, 0.0).astype(F32)
    MM = ((1,), (0,))

    lead_copies = []
    side_copies = []
    n_high = cols_dev // n_low
    for array, side, (back_hi, back_lo) in zip(
        pieces, sides, [(h, l) for l in range(2) for h in range(rows_dev // 2)], strict=True
    ):
        row_hi = lax.rem(my_row // 2 - back_hi + rows_dev // 2, rows_dev // 2)
        row_lo = lax.rem(lax.rem(my_row, 2) + back_lo, 2)
        at = pl.multiple_of(c0 + (row_hi * 2 + row_lo) * nb, nb)
        for i in range(cols_dev):
            col = col_of(my_col, i % n_high, i // n_high, cols_dev, n_low)
            copy = pltpu.make_async_copy(
                array.at[i],
                grid_ref.at[pl.ds(at, nb), pl.ds(pl.multiple_of(col * nb, nb), nb)],
                sems.at[len(lead_copies) + len(side_copies)],
            )
            lead_copies.append((col < STEPS, copy))
        for b in range(n_side):
            copy = pltpu.make_async_copy(
                side.at[phase, b],
                grid_ref.at[pl.ds(at, nb), lead + b * nb : lead + b * nb + nb],
                sems.at[len(lead_copies) + len(side_copies)],
            )
            side_copies.append((True, copy))
    if phase:
        copy = pltpu.make_async_copy(
            old, grid_ref.at[:c0, c0:], sems.at[len(lead_copies) + len(side_copies)]
        )
        lead_copies.append((True, copy))
    always = cols_dev == STEPS
    for wanted, copy in lead_copies + side_copies:
        guarded(always or wanted is True, wanted, copy.start)
    if phase:
        col_ref[:c0, :] = old_col[...]
        col_ref[c0:, :] = jnp.zeros((lead - c0, nb), F32)
        top[...] = old_top[...]
    else:
        col_ref[...] = jnp.zeros(col_ref.shape, F32)
        top[...] = jnp.zeros(top.shape, F32)
    for wanted, copy in lead_copies:
        guarded(always or wanted is True, wanted, copy.wait)

    def pending(i, first_col):
        at = slice(i * nb, i * nb + nb)
        off = first_col - c0
        grid_ref[at, first_col:] = grid_ref[at, first_col:] - three(
            (lcol[0, at, :], lcol[1, at, :]), (rrow[0, :, off:], rrow[1, :, off:]), MM
        )

    def schur(turn):
        if turn == 0:
            upper[0], upper[1] = split2(grid_ref[:c0, c0:])
        elif turn <= rows_dev:
            at = slice(c0 + (turn - 1) * nb, c0 + turn * nb)
            grid_ref[at, c0:] = grid_ref[at, c0:] - three(
                split2(grid_ref[at, :c0]), (upper[0], upper[1]), MM
            )

    def settle(k, here):
        base = k * nb
        g = held[...]
        r = three(split2(gram(g, g)), split2(grid_ref[here, c0:]), MM)
        at = lax.broadcasted_iota(jnp.int32, (rows, nb), 0)
        column = jnp.where((at >= base) & (at < base + nb), 0.0, grid_ref[:rows, here])
        lcol[0], lcol[1] = split2(column)
        rrow[0], rrow[1] = split2(r)
        grid_ref[here, c0:] = r

    def step(k, here, filler):
        base = k * nb
        tile[:, nb:] = eye
        factor_tile(tile, nb, filler)
        held[...] = tile[:, nb:]

        @pl.when(k == my_col)
        def _():
            g = held[...]
            gs = split2(g)
            for a in range(na):
                row = a * rows_dev + my_row

                @pl.when(row == k)
                def _():
                    top[a] = jnp.where(ii >= jj, tile[:, :nb].T, 0.0)

                @pl.when(row > k)
                def _():
                    block = grid_ref[here, pl.ds(pl.multiple_of(row * nb, nb), nb)]
                    top[a] = three(gs, split2(block), MM).T

            at = lax.broadcasted_iota(jnp.int32, (rows, nb), 0)
            found = three(split2(grid_ref[:rows, here]), gs, ((1,), (1,)))
            col_ref[:rows, :] = jnp.where(at < base, -found, 0.0)
            col_ref[here, :] = g.T

    here = slice(c0, c0 + nb)
    if phase:
        for wanted, copy in side_copies:
            copy.wait()
        tile[:, :nb] = grid_ref[here, here] - three(
            split2(grid_ref[here, :c0]), split2(grid_ref[:c0, here]), MM
        )
        step(phase * rows_dev, here, schur)
    else:
        tile[:, :nb] = grid_ref[here, here]

        def arrive(turn):
            if turn == nb // PANEL - 1:
                for wanted, copy in side_copies:
                    copy.wait()

        step(0, here, arrive)

    @pl.loop(phase * rows_dev + 1, (phase + 1) * rows_dev)
    def _(k):
        before = pl.ds(pl.multiple_of(k * nb - nb, nb), nb)
        here = pl.ds(pl.multiple_of(k * nb, nb), nb)
        cross = three(split2(held[...]), split2(grid_ref[before, here]), MM)
        tile[:, :nb] = grid_ref[here, here] - three(split2(cross), split2(cross), ((0,), (0,)))

        def late(turn):
            if turn == 0:
                settle(k - 1, before)
            turns = nb // PANEL - 1
            for i in range(rows // nb):
                if i % turns == turn - 1:
                    pending(i, c0)

        step(k, here, late)

    settle((phase + 1) * rows_dev - 1, slice(rows - nb, rows))
    sent = []
    for i in range(rows // nb):
        at = slice(i * nb, i * nb + nb)
        if last:
            pending(i, lead)
            first = col_ref[at, :]
            if not fwd:
                first = jnp.where(my_col < STEPS, first, grid_ref[at, lead : lead + nb])
            solved_buf[0, at, :nb], solved_buf[1, at, :nb] = split2(first)
            solved_buf[0, at, nb:], solved_buf[1, at, nb:] = split2(
                grid_ref[at, lead + (nb if not fwd else 0) :]
            )
            copy = pltpu.make_async_copy(solved_buf.at[:, at, :], solved.at[:, at, :], out_sems.at[i])
        else:
            pending(i, rows)
            copy = pltpu.make_async_copy(grid_ref.at[at, rows:], passed.at[at, :], out_sems.at[i])
        copy.start()
        sent.append(copy)
    for copy in sent:
        copy.wait()


def close_kernel(place, *refs, nb, na, block_rows, block_cols, cols_dev, n_low):
    n_high = cols_dev // n_low
    near = refs[:n_high]
    far0, far, mine, solved, top, out = refs[n_high : n_high + 6]
    raw, old, right, left_h, left_m, made, sems, out_sems = refs[n_high + 6 :]
    my_col = place[1]
    MM = ((1,), (0,))
    always = cols_dev == STEPS
    group = nb * block_cols
    loads = []
    for back_l in range(n_low):
        for back_h in range(n_high):
            n = back_l * n_high + back_h
            across = near[back_h] if back_l == 0 else far0 if back_h == 0 else far.at[back_h - 1]
            col = col_of(my_col, back_h, back_l, cols_dev, n_low)
            copy = pltpu.make_async_copy(across, raw.at[n], sems.at[n])
            guarded(always, col < STEPS, copy.start)
            loads.append((n, col, copy))
    right_copy = pltpu.make_async_copy(solved, right, sems.at[cols_dev])
    right_copy.start()
    old_copy = pltpu.make_async_copy(mine.at[na * group :, :], old, sems.at[cols_dev + 1])
    old_copy.start()

    sent = []

    def send(a):
        at = slice(a * group, a * group + group)
        copy = pltpu.make_async_copy(made.at[at, :], out.at[at, :], out_sems.at[a])
        copy.start()
        sent.append(copy)

    for a in range(na):
        made[a * group : a * group + group, :] = jnp.zeros((group, nb), F32)
        made[pl.ds(a * group, nb, stride=block_cols), :] = top[a]
        send(a)
    for n, col, copy in loads:

        def take():
            copy.wait()
            at = pl.ds(pl.multiple_of(col * nb, nb), nb)
            left_h[:, at], left_m[:, at] = split2(raw[n])

        guarded(always, col < STEPS, take)
    right_copy.wait()
    old_copy.wait()
    is_panel = my_col < STEPS
    below = block_rows - na
    chunk = 3 if below % 3 == 0 else 1
    for first in range(0, below, chunk):
        at = slice(first * nb, (first + chunk) * nb)
        prod = three((left_h[at, :], left_m[at, :]), (right[0], right[1]), MM)
        for i in range(chunk):
            for b in range(block_cols):
                part = prod[i * nb : (i + 1) * nb, b * nb : (b + 1) * nb]
                prior = old[pl.ds((first + i) * group + b, nb, stride=block_cols), :]
                value = prior - part
                if b == 0:
                    value = jnp.where(is_panel, part, value)
                made[pl.ds((first + i + na) * group + b, nb, stride=block_cols), :] = value
            send(first + i + na)
    for copy in sent:
        copy.wait()


def local(matrix):
    rows_dev = lax.axis_size("row")
    cols_dev = lax.axis_size("col")
    my_row = lax.axis_index("row")
    my_col = lax.axis_index("col")
    block_rows, nb, block_cols, _ = matrix.shape
    na = STEPS // rows_dev
    fwd = STEPS // cols_dev
    lead = STEPS * nb
    wide = block_cols * nb
    n_side = block_cols - fwd
    n_low = 2
    n_high = cols_dev // n_low
    place = jnp.stack([my_row, my_col]).astype(jnp.int32)

    def tie(x, *after):
        return lax.optimization_barrier((x,) + after)[0] if after else x

    def step_to(x, axis, size, low, back_high, back_low):
        pairs = []
        for i in range(size):
            high, rest = divmod(i, low)
            pairs.append((i, (high + back_high) % (size // low) * low + (rest + back_low) % low))
        return lax.ppermute(x, axis, pairs)

    def line_of(x, *after):
        x = tie(x, *after)
        return [x] + [step_to(x, "col", cols_dev, n_low, h, 0) for h in range(1, n_high)]

    def across_rows(x, *after):
        x = tie(x, *after)
        return [x] + [step_to(x, "row", rows_dev, 2, h, 0) for h in range(1, rows_dev // 2)]

    def swap_core(x):
        return step_to(x, "row", rows_dev, 2, 0, 1)

    blocks = [matrix[a, :, 0, :] for a in range(na)]
    lines = [line_of(blocks[0])]
    side = across_rows(matrix[:na, :, fwd:, :].transpose(0, 2, 1, 3))
    strips = []
    for a in range(na):
        if a:
            lines.append(line_of(blocks[a], line))
        line = jnp.stack(lines[a])
        strips.append(jnp.concatenate([line, step_to(line, "col", cols_dev, n_low, 0, 1)]))
    body = line_of(matrix[na:, :, 0, :].reshape(-1, nb), strips[0])
    side = side + [swap_core(x) for x in side]
    body_far = step_to(tie(body[0], strips[0]), "col", cols_dev, n_low, 0, 1)
    phases = []
    for a in range(na):
        near = across_rows(strips[a], *(phases[0][1 : rows_dev // 2] if a else ()))
        phases.append(near + [swap_core(x) for x in near])

    vmem = pl.BlockSpec(memory_space=pltpu.VMEM)
    smem = pl.BlockSpec(memory_space=pltpu.SMEM)
    hbm = pl.BlockSpec(memory_space=pl.ANY)
    params = pltpu.CompilerParams(vmem_limit_bytes=56 << 20)
    carried = []
    for phase, pieces in enumerate(phases):
        last = phase == na - 1
        c0 = phase * rows_dev * nb
        rows = c0 + rows_dev * nb
        width = lead + n_side * nb
        out_shape = [jax.ShapeDtypeStruct((na, nb, nb), F32)]
        if last:
            out_shape = [jax.ShapeDtypeStruct((2, lead, wide), BF16)] + out_shape
        else:
            out_shape = [
                jax.ShapeDtypeStruct((rows, width - rows), F32),
                jax.ShapeDtypeStruct((rows, nb), F32),
            ] + out_shape
        carried = pl.pallas_call(
            functools.partial(
                sweep_kernel,
                phase=phase,
                last=last,
                nb=nb,
                na=na,
                rows_dev=rows_dev,
                cols_dev=cols_dev,
                fwd=fwd,
                n_pieces=len(pieces),
                n_low=n_low,
            ),
            out_shape=out_shape,
            in_specs=[smem] + [hbm] * (2 * len(pieces)) + ([hbm, vmem, vmem] if phase else []),
            out_specs=[hbm] + [vmem] * (len(out_shape) - 1),
            scratch_shapes=(
                [pltpu.VMEM((2, lead, wide), BF16), pltpu.VMEM((lead, nb), F32)] if last else []
            )
            + [
                pltpu.VMEM((rows, width), F32),
                pltpu.VMEM((nb, 2 * nb), F32),
                pltpu.VMEM((nb, nb), F32),
                pltpu.VMEM((2, rows, nb), BF16),
                pltpu.VMEM((2, nb, width - c0), BF16),
                pltpu.VMEM((2, max(c0, nb), width - c0), BF16),
                pltpu.SemaphoreType.DMA((len(pieces) * (cols_dev + n_side) + 1,)),
                pltpu.SemaphoreType.DMA((rows // nb,)),
            ],
            compiler_params=params,
            cost_estimate=pl.CostEstimate(flops=8 * 10**9, bytes_accessed=10**7, transcendentals=0),
            name="sweep%d" % phase,
        )(place, *pieces, *side, *carried)
        if phase == 0:
            far = step_to(jnp.stack([tie(x, carried[0]) for x in body[1:]]), "col", cols_dev, n_low, 0, 1)
    solved, top = carried
    out = pl.pallas_call(
        functools.partial(close_kernel, nb=nb, na=na, block_rows=block_rows, block_cols=block_cols, cols_dev=cols_dev, n_low=n_low),
        out_shape=jax.ShapeDtypeStruct((block_rows * nb * block_cols, nb), F32),
        in_specs=[smem] + [hbm] * (n_high + 4) + [vmem],
        out_specs=hbm,
        scratch_shapes=[
            pltpu.VMEM((cols_dev, (block_rows - na) * nb, nb), F32),
            pltpu.VMEM(((block_rows - na) * nb * block_cols, nb), F32),
            pltpu.VMEM((2, lead, wide), BF16),
            pltpu.VMEM(((block_rows - na) * nb, lead), BF16),
            pltpu.VMEM(((block_rows - na) * nb, lead), BF16),
            pltpu.VMEM((block_rows * nb * block_cols, nb), F32),
            pltpu.SemaphoreType.DMA((cols_dev + 2,)),
            pltpu.SemaphoreType.DMA((block_rows,)),
        ],
        compiler_params=params,
        name="close",
    )(place, *body, body_far, far, matrix.reshape(-1, nb), solved, top)
    return out.reshape(matrix.shape)


def solution(mesh):
    placed = (P(None, "row", None, "col"),)
    return jax.shard_map(
        local, mesh=mesh, in_specs=placed, out_specs=P(None, "row", None, "col"), check_vma=False
    )
```

time: 132 us -> 117 us (0.89)
  between operations: 13.6 us -> 0.53 us
  starting transfers between devices: 14.1 us -> 22.3 us
  waiting for transfers between devices: 30.7 us -> 23.7 us
  Pallas kernels: 65.3 us -> 61.2 us
    ppermute x14 -> x22, starting transfers between devices: 14.1 us -> 22.3 us  [step_to(): return lax.ppermute(x, axis, pairs)]
    ppermute x14 -> x22, waiting for transfers between devices: 30.7 us -> 23.7 us  [step_to(): return lax.ppermute(x, axis, pairs)]
    pallas_call x2, Pallas kernels: 58.2 us -> 53.6 us  [local(): pl.pallas_call(functools.partial(sweep_kernel, phase=phase, last=last, nb...]
    unnamed x19 -> x45, local copies, waits for them, and re-layouts: 1.6 us -> 3.77 us
  transfers between devices with their start and end apart: 16 -> 22, of which waited for: 6 -> 5; matrix products, arithmetic and copies ran while one was open for 4% -> 3% of each run, Pallas kernels for 44% -> 46%
where the time goes in v3:
time: 117 us; the launch traced here: 116 us
  Pallas kernels  61.2 us (52%)
  waiting for transfers between devices  23.7 us (20%)
  starting transfers between devices  22.3 us (19%)
  local copies, waits for them, and re-layouts  7.78 us (7%)
    pallas_call x2, Pallas kernels, local(): pl.pallas_call(functools.partial(sweep_kernel, phase=phase, last=last, nb...  53.6 us
    ppermute x22, waiting for transfers between devices, step_to(): return lax.ppermute(x, axis, pairs)  23.7 us
    ppermute x22, starting transfers between devices, step_to(): return lax.ppermute(x, axis, pairs)  22.3 us
    pallas_call x1, Pallas kernels, local(): pl.pallas_call(functools.partial(close_kernel, nb=nb, na=na, block_rows=b...  7.64 us
    unnamed x45, local copies, waits for them, and re-layouts  3.77 us
  transfers between devices with their start and end apart: 22, of which 5 were waited for; matrix products, arithmetic and copies ran while one was open for 3% of the time, Pallas kernels for 46%

profile of v3, /device:TPU:8, one launch (start us, length us, event | category | flops | bytes accessed | tf_op | source)
XLA Modules:
  0.0 116.4 jit_solution(10895218130219925656)
XLA Ops:
  0.0 1.1 fusion
  1.1 1.6 %collective-permute-start = (f32[128,128]{1,0:T(8,128)S(1)}, f32[128,128]{1,0:T(8,128)S(1)}, u32[]{:S(2)}, u32[]{:S(2)}) collective-permute-start(f32[128,128]{1,0:T(8,128)S(1)} %bitcast.47), channel_id=1, source_target_pairs={{0,2},{1,3},{2,4},{3,5},{4,6},{5,7},{6,0},{7,1},{8,10},{9,11},{10,... | collective-permute-start | bytes 196616 | tf_op jit(solution)/shard_map/ppermute | solution.py:355
  2.8 1.1 collective-permute-start.1
  3.8 1.9 %collective-permute-start.2 = (f32[128,128]{1,0:T(8,128)S(1)}, f32[128,128]{1,0:T(8,128)S(1)}, u32[]{:S(2)}, u32[]{:S(2)}) collective-permute-start(f32[128,128]{1,0:T(8,128)S(1)} %bitcast.49), channel_id=1, source_target_pairs={{0,6},{1,7},{2,0},{3,1},{4,2},{5,3},{6,4},{7,5},{8,14},{9,15},{10,... | collective-permute-start | bytes 196616 | tf_op jit(solution)/shard_map/ppermute | solution.py:355
  5.8 1.2 %slice.14 = f32[2,128,3,128]{3,2,1,0:T(4,128)S(1)} slice(f32[8,128,4,128]{3,2,1,0:T(4,128)} %param.1), slice={[0:2], [0:128], [1:4], [0:128]} | slice | bytes 786432 | tf_op jit(solution)/shard_map/slice | solution.py:370
  7.0 1.6 %collective-permute-start.11 = (f32[2,3,128,128]{3,2,1,0:T(8,128)S(1)}, f32[2,3,128,128]{3,2,1,0:T(8,128)S(1)}, u32[]{:S(2)}, u32[]{:S(2)}) collective-permute-start(f32[2,3,128,128]{3,2,1,0:T(8,128)S(1)} %bitcast.52), channel_id=1, source_target_pairs={{0,16},{8,24},{16,0},{24,8},{1,17},{9,25},{17,1},{25,9},{2,18},{10... | collective-permute-start | bytes 1179656 | tf_op jit(solution)/shard_map/ppermute | solution.py:355
  8.6 1.7 %slice.12 = f32[6,128,1,128]{3,2,1,0:T(1,128)S(1)} slice(f32[8,128,4,128]{3,2,1,0:T(4,128)} %param.1), slice={[2:8], [0:128], [0:1], [0:128]} | slice | bytes 786432 | tf_op jit(solution)/shard_map/slice | solution.py:377
  11.3 3.5 %collective-permute-start.16 = (f32[128,128]{1,0:T(8,128)S(1)}, f32[128,128]{1,0:T(8,128)S(1)}, u32[]{:S(2)}, u32[]{:S(2)}) collective-permute-start(f32[128,128]{1,0:T(8,128)S(1)} %bitcast.43), channel_id=1, source_target_pairs={{0,4},{1,5},{2,6},{3,7},{4,0},{5,1},{6,2},{7,3},{8,12},{9,13},{10,... | collective-permute-start | bytes 196616 | tf_op jit(solution)/shard_map/ppermute | solution.py:355
  14.8 1.5 %collective-permute-start.3 = (f32[4,128,128]{2,1,0:T(8,128)S(1)}, f32[4,128,128]{2,1,0:T(8,128)S(1)}, u32[]{:S(2)}, u32[]{:S(2)}) collective-permute-start(f32[4,128,128]{2,1,0:T(8,128)S(1)} %pad_maximum_fusion.1), channel_id=1, source_target_pairs={{0,1},{1,0},{2,3},{3,2},{4,5},{5,4},{6,7},{7,6},{8,9},{9,8},{10,11... | collective-permute-start | bytes 786440 | tf_op jit(solution)/shard_map/ppermute | solution.py:355
  16.3 4.8 %collective-permute-done.3 = f32[4,128,128]{2,1,0:T(8,128)S(1)} collective-permute-done((f32[4,128,128]{2,1,0:T(8,128)S(1)}, f32[4,128,128]{2,1,0:T(8,128)S(1)}, u32[]{:S(2)}, u32[]{:S(2)}) %collective-permute-start.3) | collective-permute-done | bytes 262176 | tf_op jit(solution)/shard_map/ppermute | solution.py:355
  21.2 1.0 collective-permute-start.8
  22.3 1.6 %collective-permute-start.18 = (f32[4,128,128]{2,1,0:T(8,128)S(1)}, f32[4,128,128]{2,1,0:T(8,128)S(1)}, u32[]{:S(2)}, u32[]{:S(2)}) collective-permute-start(f32[4,128,128]{2,1,0:T(8,128)S(1)} %pad_maximum_fusion.2), channel_id=1, source_target_pairs={{0,1},{1,0},{2,3},{3,2},{4,5},{5,4},{6,7},{7,6},{8,9},{9,8},{10,11... | collective-permute-start | bytes 786440 | tf_op jit(solution)/shard_map/ppermute | solution.py:355
  24.4 7.6 %collective-permute-done.8.refs_2_ = f32[8,128,128]{2,1,0:T(8,128)S(1)} collective-permute-done((f32[8,128,128]{2,1,0:T(8,128)S(1)}, f32[8,128,128]{2,1,0:T(8,128)S(1)}, u32[]{:S(2)}, u32[]{:S(2)}) %collective-permute-start.8) | collective-permute-done | bytes 524320 | tf_op jit(solution)/shard_map/ppermute | solution.py:355
  32.1 1.8 %collective-permute-start.4 = (f32[768,128]{1,0:T(8,128)S(1)}, f32[768,128]{1,0:T(8,128)S(1)}, u32[]{:S(2)}, u32[]{:S(2)}) collective-permute-start(f32[768,128]{1,0:T(8,128)S(1)} %bitcast.37), channel_id=1, source_target_pairs={{0,2},{1,3},{2,4},{3,5},{4,6},{5,7},{6,0},{7,1},{8,10},{9,11},{10,... | collective-permute-start | bytes 1179656 | tf_op jit(solution)/shard_map/ppermute | solution.py:355
  34.0 2.4 %collective-permute-start.5 = (f32[768,128]{1,0:T(8,128)S(1)}, f32[768,128]{1,0:T(8,128)S(1)}, u32[]{:S(2)}, u32[]{:S(2)}) collective-permute-start(f32[768,128]{1,0:T(8,128)S(1)} %bitcast.38), channel_id=1, source_target_pairs={{0,4},{1,5},{2,6},{3,7},{4,0},{5,1},{6,2},{7,3},{8,12},{9,13},{10,... | collective-permute-start | bytes 1179656 | tf_op jit(solution)/shard_map/ppermute | solution.py:355
  36.4 1.3 %collective-permute-start.19 = (f32[8,128,128]{2,1,0:T(8,128)S(1)}, f32[8,128,128]{2,1,0:T(8,128)S(1)}, u32[]{:S(2)}, u32[]{:S(2)}) collective-permute-start(f32[8,128,128]{2,1,0:T(8,128)S(1)} %constant_dynamic-update-slice_fusion.5.refs_1_), channel_id=1, source_target_pairs={{0,16},{8,24},{16,0},{24,8},{1,17},{9,25},{17,1},{25,9},{2,18},{10... | collective-permute-start | bytes 1572872 | tf_op jit(solution)/shard_map/ppermute | solution.py:355
  38.6 26.3 %sweep0.1 = (f32[512,896]{1,0:T(8,128)}, f32[512,128]{1,0:T(8,128)}, f32[2,128,128]{2,1,0:T(8,128)}) custom-call(s32[2]{0:T(128)} %pad_add_fusion.refs_0_.place, f32[8,128,128]{2,1,0:T(8,128)} %copy-done.7, f32[8,128,128]{2,1,0:T(8,128)} %copy-done.9, f32[8,128,128]{2,1,0:T(8,128)} %copy-done.10, f32[8,128,128]{2,1,0:T(8,128)} %copy-done.12, ...), custom_call_target="tpu_custom_call" | custom-call | flops 8000000000 | bytes 10000000 | tf_op jit(solution)/shard_map/sweep0/pallas_call | solution.py:403
  64.9 3.3 %collective-permute-done.5.refs_2_ = f32[768,128]{1,0:T(8,128)S(1)} collective-permute-done((f32[768,128]{1,0:T(8,128)S(1)}, f32[768,128]{1,0:T(8,128)S(1)}, u32[]{:S(2)}, u32[]{:S(2)}) %collective-permute-start.5) | collective-permute-done | bytes 393248 | tf_op jit(solution)/shard_map/ppermute | solution.py:355
  68.2 2.1 %collective-permute-done.6.refs_3_ = f32[768,128]{1,0:T(8,128)S(1)} collective-permute-done((f32[768,128]{1,0:T(8,128)S(1)}, f32[768,128]{1,0:T(8,128)S(1)}, u32[]{:S(2)}, u32[]{:S(2)}) %collective-permute-start.6) | collective-permute-done | bytes 393248 | tf_op jit(solution)/shard_map/ppermute | solution.py:355
  71.3 1.5 %collective-permute-start.14 = (f32[3,768,128]{2,1,0:T(8,128)S(1)}, f32[3,768,128]{2,1,0:T(8,128)S(1)}, u32[]{:S(2)}, u32[]{:S(2)}) collective-permute-start(f32[3,768,128]{2,1,0:T(8,128)S(1)} %pad_maximum_fusion), channel_id=1, source_target_pairs={{0,1},{1,0},{2,3},{3,2},{4,5},{5,4},{6,7},{7,6},{8,9},{9,8},{10,11... | collective-permute-start | bytes 3538952 | tf_op jit(solution)/shard_map/ppermute | solution.py:355
  73.3 0.8 copy-done.13
  74.3 27.3 %sweep1.1 = (bf16[2,1024,512]{2,1,0:T(8,128)(2,1)}, f32[2,128,128]{2,1,0:T(8,128)}) custom-call(s32[2]{0:T(128)} %pad_add_fusion.refs_0_.place, f32[8,128,128]{2,1,0:T(8,128)} %copy-done.8, f32[8,128,128]{2,1,0:T(8,128)} %copy-done.11, f32[8,128,128]{2,1,0:T(8,128)} %copy-done.13, f32[8,128,128]{2,1,0:T(8,128)} %copy-done.14, f32[2,3,128,128]{3,2,1,0:T(8,128)} %bitcast.55, ...), custom_call_target="tpu_custom_call" | custom-call | flops 8000000000 | bytes 10000000 | tf_op jit(solution)/shard_map/sweep1/pallas_call | solution.py:403
  101.6 5.8 %collective-permute-done.7.refs_4_ = f32[768,128]{1,0:T(8,128)S(1)} collective-permute-done((f32[768,128]{1,0:T(8,128)S(1)}, f32[768,128]{1,0:T(8,128)S(1)}, u32[]{:S(2)}, u32[]{:S(2)}) %collective-permute-start.7) | collective-permute-done | bytes 393248 | tf_op jit(solution)/shard_map/ppermute | solution.py:355
  108.6 7.6 %close.1 = f32[4096,128]{1,0:T(8,128)} custom-call(s32[2]{0:T(128)} %pad_add_fusion.refs_0_.place, f32[768,128]{1,0:T(8,128)} %bitcast.41, f32[768,128]{1,0:T(8,128)} %copy-done, f32[768,128]{1,0:T(8,128)} %copy-done.1, f32[768,128]{1,0:T(8,128)} %copy-done.2, f32[768,128]{1,0:T(8,128)} %copy-done.5, f32[3,768,128]{2,1,0:T(8,128)} %copy-done.4, ...), custom_call_target="tpu_custom_call" | custom-call | tf_op jit(solution)/shard_map/close/pallas_call | solution.py:439
  (77 shorter events, 5.3 us)
Async XLA Ops:
  1.1 9.8 %collective-permute-start = (f32[128,128]{1,0:T(8,128)S(1)}, f32[128,128]{1,0:T(8,128)S(1)}, u32[]{:S(2)}, u32[]{:S(2)}) collective-permute-start(f32[128,128]{1,0:T(8,128)S(1)} %bitcast.47), channel_id=1, source_target_pairs={{0,2},{1,3},{2,4},{3,5},{4,6},{5,7},{6,0},{7,1},{8,10},{9,11},{10,... | collective-permute-start | bytes 196616 | tf_op jit(solution)/shard_map/ppermute | solution.py:355
  2.8 8.2 %collective-permute-start.1 = (f32[128,128]{1,0:T(8,128)S(1)}, f32[128,128]{1,0:T(8,128)S(1)}, u32[]{:S(2)}, u32[]{:S(2)}) collective-permute-start(f32[128,128]{1,0:T(8,128)S(1)} %bitcast.48), channel_id=1, source_target_pairs={{0,4},{1,5},{2,6},{3,7},{4,0},{5,1},{6,2},{7,3},{8,12},{9,13},{10,... | collective-permute-start | bytes 196616 | tf_op jit(solution)/shard_map/ppermute | solution.py:355
  3.8 7.1 %collective-permute-start.2 = (f32[128,128]{1,0:T(8,128)S(1)}, f32[128,128]{1,0:T(8,128)S(1)}, u32[]{:S(2)}, u32[]{:S(2)}) collective-permute-start(f32[128,128]{1,0:T(8,128)S(1)} %bitcast.49), channel_id=1, source_target_pairs={{0,6},{1,7},{2,0},{3,1},{4,2},{5,3},{6,4},{7,5},{8,14},{9,15},{10,... | collective-permute-start | bytes 196616 | tf_op jit(solution)/shard_map/ppermute | solution.py:355
  7.0 17.1 %collective-permute-start.11 = (f32[2,3,128,128]{3,2,1,0:T(8,128)S(1)}, f32[2,3,128,128]{3,2,1,0:T(8,128)S(1)}, u32[]{:S(2)}, u32[]{:S(2)}) collective-permute-start(f32[2,3,128,128]{3,2,1,0:T(8,128)S(1)} %bitcast.52), channel_id=1, source_target_pairs={{0,16},{8,24},{16,0},{24,8},{1,17},{9,25},{17,1},{25,9},{2,18},{10... | collective-permute-start | bytes 1179656 | tf_op jit(solution)/shard_map/ppermute | solution.py:355
  10.3 62.5 %copy-start.3 = (f32[6,128,1,128]{3,2,1,0:T(1,128)}, f32[6,128,1,128]{3,2,1,0:T(1,128)S(1)}, u32[]{:S(2)}) copy-start(f32[6,128,1,128]{3,2,1,0:T(1,128)S(1)} %slice.12) | copy-start | bytes 1179652
  11.0 11.2 %collective-permute-start.15 = (f32[128,128]{1,0:T(8,128)S(1)}, f32[128,128]{1,0:T(8,128)S(1)}, u32[]{:S(2)}, u32[]{:S(2)}) collective-permute-start(f32[128,128]{1,0:T(8,128)S(1)} %bitcast.42), channel_id=1, source_target_pairs={{0,2},{1,3},{2,4},{3,5},{4,6},{5,7},{6,0},{7,1},{8,10},{9,11},{10,... | collective-permute-start | bytes 196616 | tf_op jit(solution)/shard_map/ppermute | solution.py:355
  11.3 11.0 %collective-permute-start.16 = (f32[128,128]{1,0:T(8,128)S(1)}, f32[128,128]{1,0:T(8,128)S(1)}, u32[]{:S(2)}, u32[]{:S(2)}) collective-permute-start(f32[128,128]{1,0:T(8,128)S(1)} %bitcast.43), channel_id=1, source_target_pairs={{0,4},{1,5},{2,6},{3,7},{4,0},{5,1},{6,2},{7,3},{8,12},{9,13},{10,... | collective-permute-start | bytes 196616 | tf_op jit(solution)/shard_map/ppermute | solution.py:355
  14.8 7.5 %collective-permute-start.17 = (f32[128,128]{1,0:T(8,128)S(1)}, f32[128,128]{1,0:T(8,128)S(1)}, u32[]{:S(2)}, u32[]{:S(2)}) collective-permute-start(f32[128,128]{1,0:T(8,128)S(1)} %bitcast.44), channel_id=1, source_target_pairs={{0,6},{1,7},{2,0},{3,1},{4,2},{5,3},{6,4},{7,5},{8,14},{9,15},{10,... | collective-permute-start | bytes 196616 | tf_op jit(solution)/shard_map/ppermute | solution.py:355
  14.8 6.4 %collective-permute-start.3 = (f32[4,128,128]{2,1,0:T(8,128)S(1)}, f32[4,128,128]{2,1,0:T(8,128)S(1)}, u32[]{:S(2)}, u32[]{:S(2)}) collective-permute-start(f32[4,128,128]{2,1,0:T(8,128)S(1)} %pad_maximum_fusion.1), channel_id=1, source_target_pairs={{0,1},{1,0},{2,3},{3,2},{4,5},{5,4},{6,7},{7,6},{8,9},{9,8},{10,11... | collective-permute-start | bytes 786440 | tf_op jit(solution)/shard_map/ppermute | solution.py:355
  21.2 10.9 %collective-permute-start.8 = (f32[8,128,128]{2,1,0:T(8,128)S(1)}, f32[8,128,128]{2,1,0:T(8,128)S(1)}, u32[]{:S(2)}, u32[]{:S(2)}) collective-permute-start(f32[8,128,128]{2,1,0:T(8,128)S(1)} %constant_dynamic-update-slice_fusion.refs_1_), channel_id=1, source_target_pairs={{0,16},{8,24},{16,0},{24,8},{1,17},{9,25},{17,1},{25,9},{2,18},{10... | collective-permute-start | bytes 1572872 | tf_op jit(solution)/shard_map/ppermute | solution.py:355
  22.2 11.8 %collective-permute-start.12 = (f32[2,3,128,128]{3,2,1,0:T(8,128)S(1)}, f32[2,3,128,128]{3,2,1,0:T(8,128)S(1)}, u32[]{:S(2)}, u32[]{:S(2)}) collective-permute-start(f32[2,3,128,128]{3,2,1,0:T(8,128)S(1)} %bitcast.53), channel_id=1, source_target_pairs={{0,8},{8,0},{16,24},{24,16},{1,9},{9,1},{17,25},{25,17},{2,10},{10... | collective-permute-start | bytes 1179656 | tf_op jit(solution)/shard_map/ppermute | solution.py:355
  22.3 9.8 %collective-permute-start.18 = (f32[4,128,128]{2,1,0:T(8,128)S(1)}, f32[4,128,128]{2,1,0:T(8,128)S(1)}, u32[]{:S(2)}, u32[]{:S(2)}) collective-permute-start(f32[4,128,128]{2,1,0:T(8,128)S(1)} %pad_maximum_fusion.2), channel_id=1, source_target_pairs={{0,1},{1,0},{2,3},{3,2},{4,5},{5,4},{6,7},{7,6},{8,9},{9,8},{10,11... | collective-permute-start | bytes 786440 | tf_op jit(solution)/shard_map/ppermute | solution.py:355
  23.9 12.5 %collective-permute-start.9 = (f32[8,128,128]{2,1,0:T(8,128)S(1)}, f32[8,128,128]{2,1,0:T(8,128)S(1)}, u32[]{:S(2)}, u32[]{:S(2)}) collective-permute-start(f32[8,128,128]{2,1,0:T(8,128)S(1)} %constant_dynamic-update-slice_fusion.refs_1_), channel_id=1, source_target_pairs={{0,8},{8,0},{16,24},{24,16},{1,9},{9,1},{17,25},{25,17},{2,10},{10... | collective-permute-start | bytes 1572872 | tf_op jit(solution)/shard_map/ppermute | solution.py:355
  24.1 12.3 %collective-permute-start.13 = (f32[2,3,128,128]{3,2,1,0:T(8,128)S(1)}, f32[2,3,128,128]{3,2,1,0:T(8,128)S(1)}, u32[]{:S(2)}, u32[]{:S(2)}) collective-permute-start(f32[2,3,128,128]{3,2,1,0:T(8,128)S(1)} %collective-permute-done.11.refs_6_), channel_id=1, source_target_pairs={{0,8},{8,0},{16,24},{24,16},{1,9},{9,1},{17,25},{25,17},{2,10},{10... | collective-permute-start | bytes 1179656 | tf_op jit(solution)/shard_map/ppermute | solution.py:355
  32.1 5.7 %collective-permute-start.10 = (f32[8,128,128]{2,1,0:T(8,128)S(1)}, f32[8,128,128]{2,1,0:T(8,128)S(1)}, u32[]{:S(2)}, u32[]{:S(2)}) collective-permute-start(f32[8,128,128]{2,1,0:T(8,128)S(1)} %collective-permute-done.8.refs_2_), channel_id=1, source_target_pairs={{0,8},{8,0},{16,24},{24,16},{1,9},{9,1},{17,25},{25,17},{2,10},{10... | collective-permute-start | bytes 1572872 | tf_op jit(solution)/shard_map/ppermute | solution.py:355
  32.1 32.8 %collective-permute-start.4 = (f32[768,128]{1,0:T(8,128)S(1)}, f32[768,128]{1,0:T(8,128)S(1)}, u32[]{:S(2)}, u32[]{:S(2)}) collective-permute-start(f32[768,128]{1,0:T(8,128)S(1)} %bitcast.37), channel_id=1, source_target_pairs={{0,2},{1,3},{2,4},{3,5},{4,6},{5,7},{6,0},{7,1},{8,10},{9,11},{10,... | collective-permute-start | bytes 1179656 | tf_op jit(solution)/shard_map/ppermute | solution.py:355
  33.9 31.0 %copy-start.8 = (f32[8,128,128]{2,1,0:T(8,128)}, f32[8,128,128]{2,1,0:T(8,128)S(1)}, u32[]{:S(2)}) copy-start(f32[8,128,128]{2,1,0:T(8,128)S(1)} %constant_dynamic-update-slice_fusion.5.refs_1_) | copy-start | bytes 1572868
  34.0 34.3 %collective-permute-start.5 = (f32[768,128]{1,0:T(8,128)S(1)}, f32[768,128]{1,0:T(8,128)S(1)}, u32[]{:S(2)}, u32[]{:S(2)}) collective-permute-start(f32[768,128]{1,0:T(8,128)S(1)} %bitcast.38), channel_id=1, source_target_pairs={{0,4},{1,5},{2,6},{3,7},{4,0},{5,1},{6,2},{7,3},{8,12},{9,13},{10,... | collective-permute-start | bytes 1179656 | tf_op jit(solution)/shard_map/ppermute | solution.py:355
  36.4 33.9 %collective-permute-start.6 = (f32[768,128]{1,0:T(8,128)S(1)}, f32[768,128]{1,0:T(8,128)S(1)}, u32[]{:S(2)}, u32[]{:S(2)}) collective-permute-start(f32[768,128]{1,0:T(8,128)S(1)} %bitcast.39), channel_id=1, source_target_pairs={{0,6},{1,7},{2,0},{3,1},{4,2},{5,3},{6,4},{7,5},{8,14},{9,15},{10,... | collective-permute-start | bytes 1179656 | tf_op jit(solution)/shard_map/ppermute | solution.py:355
  36.4 33.9 %collective-permute-start.19 = (f32[8,128,128]{2,1,0:T(8,128)S(1)}, f32[8,128,128]{2,1,0:T(8,128)S(1)}, u32[]{:S(2)}, u32[]{:S(2)}) collective-permute-start(f32[8,128,128]{2,1,0:T(8,128)S(1)} %constant_dynamic-update-slice_fusion.5.refs_1_), channel_id=1, source_target_pairs={{0,16},{8,24},{16,0},{24,8},{1,17},{9,25},{17,1},{25,9},{2,18},{10... | collective-permute-start | bytes 1572872 | tf_op jit(solution)/shard_map/ppermute | solution.py:355
  37.8 35.5 %collective-permute-start.20 = (f32[8,128,128]{2,1,0:T(8,128)S(1)}, f32[8,128,128]{2,1,0:T(8,128)S(1)}, u32[]{:S(2)}, u32[]{:S(2)}) collective-permute-start(f32[8,128,128]{2,1,0:T(8,128)S(1)} %constant_dynamic-update-slice_fusion.5.refs_1_), channel_id=1, source_target_pairs={{0,8},{8,0},{16,24},{24,16},{1,9},{9,1},{17,25},{25,17},{2,10},{10... | collective-permute-start | bytes 1572872 | tf_op jit(solution)/shard_map/ppermute | solution.py:355
  70.3 3.0 %collective-permute-start.21 = (f32[8,128,128]{2,1,0:T(8,128)S(1)}, f32[8,128,128]{2,1,0:T(8,128)S(1)}, u32[]{:S(2)}, u32[]{:S(2)}) collective-permute-start(f32[8,128,128]{2,1,0:T(8,128)S(1)} %collective-permute-done.19.refs_2_), channel_id=1, source_target_pairs={{0,8},{8,0},{16,24},{24,16},{1,9},{9,1},{17,25},{25,17},{2,10},{10... | collective-permute-start | bytes 1572872 | tf_op jit(solution)/shard_map/ppermute | solution.py:355
  71.3 36.1 %collective-permute-start.14 = (f32[3,768,128]{2,1,0:T(8,128)S(1)}, f32[3,768,128]{2,1,0:T(8,128)S(1)}, u32[]{:S(2)}, u32[]{:S(2)}) collective-permute-start(f32[3,768,128]{2,1,0:T(8,128)S(1)} %pad_maximum_fusion), channel_id=1, source_target_pairs={{0,1},{1,0},{2,3},{3,2},{4,5},{5,4},{6,7},{7,6},{8,9},{9,8},{10,11... | collective-permute-start | bytes 3538952 | tf_op jit(solution)/shard_map/ppermute | solution.py:355
  72.8 34.6 %collective-permute-start.7 = (f32[768,128]{1,0:T(8,128)S(1)}, f32[768,128]{1,0:T(8,128)S(1)}, u32[]{:S(2)}, u32[]{:S(2)}) collective-permute-start(f32[768,128]{1,0:T(8,128)S(1)} %bitcast.40), channel_id=1, source_target_pairs={{0,1},{1,0},{2,3},{3,2},{4,5},{5,4},{6,7},{7,6},{8,9},{9,8},{10,11... | collective-permute-start | bytes 1179656 | tf_op jit(solution)/shard_map/ppermute | solution.py:355
  (16 other events, 71.9 us)

commit v4 on v3

--- a/solution.py
+++ b/solution.py
@@ -8,7 +8,8 @@
 from jax.sharding import PartitionSpec as P
 
 STEPS = 8
-PANEL = 16
+PANEL = 32
+SUB = 8
 F32 = jnp.float32
 BF16 = jnp.bfloat16
 
@@ -43,35 +44,58 @@
 
 
 def factor_tile(tile, nb, filler):
-    for turn, first in enumerate(range(0, nb, PANEL)):
-        rows = [tile[pl.ds(first + i, 8, stride=0), :] for i in range(PANEL)]
-        left = [r[:, :nb] for r in rows]
-        right = [r[:, nb:] for r in rows]
-        entry = {}
-        for i in range(PANEL):
-            for s in range(i + 1):
-                lane = first + i
-                entry[i, s] = jnp.broadcast_to(left[s][:, lane : lane + 1], (8, nb))
-        for s in range(PANEL):
-            scale = lax.rsqrt(entry[s, s])
-            left[s] = left[s] * scale
-            right[s] = right[s] * scale
-            for i in range(s + 1, PANEL):
-                entry[i, s] = entry[i, s] * scale
-            for i in range(s + 1, PANEL):
-                for t in range(s + 1, i + 1):
-                    entry[i, t] = entry[i, t] - entry[i, s] * entry[t, s]
-            for i in range(s + 1, PANEL):
-                left[i] = left[i] - entry[i, s] * left[s]
-                right[i] = right[i] - entry[i, s] * right[s]
-        for s in range(PANEL):
-            tile[first + s : first + s + 1, :nb] = left[s][:1]
-            tile[first + s : first + s + 1, nb:] = right[s][:1]
-        filler(turn)
+    lane = lax.broadcasted_iota(jnp.int32, (SUB, nb), 1)
+    sub = lax.broadcasted_iota(jnp.int32, (SUB, nb), 0)
+    count = PANEL // SUB
+    for first in range(0, nb, PANEL):
         after = first + PANEL
+        parts = [tile[first + SUB * v : first + SUB * v + SUB, :] for v in range(count)]
+        for b in range(count):
+            at = first + SUB * b
+            inside = (lane >= at) & (lane < at + SUB)
+            row = [jnp.broadcast_to(parts[b][i : i + 1, :], (SUB, nb)) for i in range(SUB)]
+            entry = {}
+            for i in range(SUB):
+                for s in range(i + 1):
+                    entry[i, s] = jnp.broadcast_to(row[s][:, at + i : at + i + 1], (SUB, nb))
+            below = [
+                [jnp.broadcast_to(parts[v][:, at + t : at + t + 1], (SUB, nb)) for t in range(SUB)]
+                for v in range(b + 1, count)
+            ]
+            row = [
+                jnp.where(inside, jnp.where(lane == at + i, 1.0, 0.0), row[i]) for i in range(SUB)
+            ]
+            for s in range(SUB):
+                scale = lax.rsqrt(entry[s, s])
+                row[s] = row[s] * scale
+                for column in below:
+                    column[s] = column[s] * scale
+                for i in range(s + 1, SUB):
+                    entry[i, s] = entry[i, s] * scale
+                for i in range(s + 1, SUB):
+                    for t in range(s + 1, i + 1):
+                        entry[i, t] = entry[i, t] - entry[i, s] * entry[t, s]
+                for i in range(s + 1, SUB):
+                    row[i] = row[i] - entry[i, s] * row[s]
+                for column in below:
+                    for t in range(s + 1, SUB):
+                        column[t] = column[t] - column[s] * entry[t, s]
+            made = row[0]
+            for s in range(1, SUB):
+                made = jnp.where(sub == s, row[s], made)
+            for v, column in zip(range(b + 1, count), below):
+                terms = [column[s] * row[s] for s in range(SUB)]
+                while len(terms) > 1:
+                    terms = [terms[n] + terms[n + 1] for n in range(0, len(terms), 2)]
+                parts[v] = jnp.where(inside, 0.0, parts[v]) - terms[0]
+            parts[b] = jnp.where((lane >= at + SUB) & (lane < after), 0.0, made)
+            filler((first + SUB * b) // SUB)
+        done = jnp.concatenate(parts, 0)
+        tile[first:after, :] = done
         if after < nb:
-            done = tile[first:after, :]
-            tile[after:, :] = tile[after:, :] - gram(done[:, :nb], done)[after:, :]
+            kept = lax.broadcasted_iota(jnp.int32, (nb - after, nb), 1)
+            kept = (kept < first) | (kept >= after)
+            tile[after:, :] = jnp.where(kept, tile[after:, :], 0.0) - gram(done, done)[after:, :]
 
 
 def col_of(my_col, back_h, back_l, cols_dev, n_low):
@@ -101,7 +125,7 @@
     else:
         passed, col_ref, top = refs[:3]
         refs = refs[3:]
-    grid_ref, tile, held, lcol, rrow, upper, sems, out_sems = refs
+    grid_ref, tile, held, origin, lcol, rrow, upper, sems, out_sems = refs
     my_row, my_col = place[0], place[1]
     lead = STEPS * nb
     c0 = phase * rows_dev * nb
@@ -109,7 +133,6 @@
     n_side = sides[0].shape[1]
     ii = lax.broadcasted_iota(jnp.int32, (nb, nb), 0)
     jj = lax.broadcasted_iota(jnp.int32, (nb, nb), 1)
-    eye = jnp.where(ii == jj, 1.0, 0.0).astype(F32)
     MM = ((1,), (0,))
 
     lead_copies = []
@@ -182,9 +205,9 @@
 
     def step(k, here, filler):
         base = k * nb
-        tile[:, nb:] = eye
+        origin[...] = tile[...]
         factor_tile(tile, nb, filler)
-        held[...] = tile[:, nb:]
+        held[...] = jnp.where(ii >= jj, tile[...], 0.0)
 
         @pl.when(k == my_col)
         def _():
@@ -195,7 +218,8 @@
 
                 @pl.when(row == k)
                 def _():
-                    top[a] = jnp.where(ii >= jj, tile[:, :nb].T, 0.0)
+                    own = three(split2(origin[...]), gs, ((1,), (1,)))
+                    top[a] = jnp.where(ii >= jj, own, 0.0)
 
                 @pl.when(row > k)
                 def _():
@@ -211,15 +235,15 @@
     if phase:
         for wanted, copy in side_copies:
             copy.wait()
-        tile[:, :nb] = grid_ref[here, here] - three(
+        tile[...] = grid_ref[here, here] - three(
             split2(grid_ref[here, :c0]), split2(grid_ref[:c0, here]), MM
         )
         step(phase * rows_dev, here, schur)
     else:
-        tile[:, :nb] = grid_ref[here, here]
+        tile[...] = grid_ref[here, here]
 
         def arrive(turn):
-            if turn == nb // PANEL - 1:
+            if turn == nb // SUB - 1:
                 for wanted, copy in side_copies:
                     copy.wait()
 
@@ -230,12 +254,12 @@
         before = pl.ds(pl.multiple_of(k * nb - nb, nb), nb)
         here = pl.ds(pl.multiple_of(k * nb, nb), nb)
         cross = three(split2(held[...]), split2(grid_ref[before, here]), MM)
-        tile[:, :nb] = grid_ref[here, here] - three(split2(cross), split2(cross), ((0,), (0,)))
+        tile[...] = grid_ref[here, here] - three(split2(cross), split2(cross), ((0,), (0,)))
 
         def late(turn):
             if turn == 0:
                 settle(k - 1, before)
-            turns = nb // PANEL - 1
+            turns = nb // SUB - 1
             for i in range(rows // nb):
                 if i % turns == turn - 1:
                     pending(i, c0)
@@ -421,7 +445,8 @@
             )
             + [
                 pltpu.VMEM((rows, width), F32),
-                pltpu.VMEM((nb, 2 * nb), F32),
+                pltpu.VMEM((nb, nb), F32),
+                pltpu.VMEM((nb, nb), F32),
                 pltpu.VMEM((nb, nb), F32),
                 pltpu.VMEM((2, rows, nb), BF16),
                 pltpu.VMEM((2, nb, width - c0), BF16),
@@ -434,7 +459,7 @@
             name="sweep%d" % phase,
         )(place, *pieces, *side, *carried)
         if phase == 0:
-            far = step_to(jnp.stack([tie(x, carried[0]) for x in body[1:]]), "col", cols_dev, n_low, 0, 1)
+            far = step_to(jnp.stack([tie(x, carried[0], body_far) for x in body[1:]]), "col", cols_dev, n_low, 0, 1)
     solved, top = carried
     out = pl.pallas_call(
         functools.partial(close_kernel, nb=nb, na=na, block_rows=block_rows, block_cols=block_cols, cols_dev=cols_dev, n_low=n_low),

time: 117 us -> 108 us (0.923)
  Pallas kernels: 61.2 us -> 56.3 us
  waiting for transfers between devices: 23.7 us -> 19.7 us
  starting transfers between devices: 22.3 us -> 23.5 us
    pallas_call x2, Pallas kernels: 53.6 us -> 48.7 us  [local(): pl.pallas_call(functools.partial(sweep_kernel, phase=phase, last=last, nb...]
    ppermute x22, waiting for transfers between devices: 23.7 us -> 19.7 us  [step_to(): return lax.ppermute(x, axis, pairs)]
    ppermute x22, starting transfers between devices: 22.3 us -> 23.5 us  [step_to(): return lax.ppermute(x, axis, pairs)]
  transfers between devices with their start and end apart: 22 -> 22, of which waited for: 5 -> 5; matrix products, arithmetic and copies ran while one was open for 3% -> 3% of each run, Pallas kernels for 46% -> 45%
where the time goes in v4:
time: 108 us
  Pallas kernels  56.3 us (52%)
  starting transfers between devices  23.5 us (22%)
  waiting for transfers between devices  19.7 us (18%)
  local copies, waits for them, and re-layouts  6.9 us (6%)
    pallas_call x2, Pallas kernels, local(): pl.pallas_call(functools.partial(sweep_kernel, phase=phase, last=last, nb...  48.7 us
    ppermute x22, starting transfers between devices, step_to(): return lax.ppermute(x, axis, pairs)  23.5 us
    ppermute x22, waiting for transfers between devices, step_to(): return lax.ppermute(x, axis, pairs)  19.7 us
    pallas_call x1, Pallas kernels, local(): pl.pallas_call(functools.partial(close_kernel, nb=nb, na=na, block_rows=b...  7.64 us
    unnamed x45, local copies, waits for them, and re-layouts  2.89 us
  transfers between devices with their start and end apart: 22, of which 5 were waited for; matrix products, arithmetic and copies ran while one was open for 3% of the time, Pallas kernels for 45%

profile of v4, /device:TPU:8, one launch (start us, length us, event | category | flops | bytes accessed | tf_op | source)
XLA Modules:
  0.0 107.8 jit_solution(10195420943758164699)
XLA Ops:
  0.0 1.1 %fusion = (f32[1,128,1,128]{3,2,1,0:T(1,128)S(1)}, f32[1,128,1,128]{3,2,1,0:T(1,128)S(1)}) fusion(f32[8,128,4,128]{3,2,1,0:T(4,128)} %param.1), kind=kLoop, calls=%fused_computation.15 | loop fusion | bytes 262144 | tf_op jit(solution)/shard_map/slice | solution.py:392
  1.1 1.6 %collective-permute-start = (f32[128,128]{1,0:T(8,128)S(1)}, f32[128,128]{1,0:T(8,128)S(1)}, u32[]{:S(2)}, u32[]{:S(2)}) collective-permute-start(f32[128,128]{1,0:T(8,128)S(1)} %bitcast.47), channel_id=1, source_target_pairs={{0,2},{1,3},{2,4},{3,5},{4,6},{5,7},{6,0},{7,1},{8,10},{9,11},{10,... | collective-permute-start | bytes 196616 | tf_op jit(solution)/shard_map/ppermute | solution.py:379
  2.8 1.1 %collective-permute-start.1 = (f32[128,128]{1,0:T(8,128)S(1)}, f32[128,128]{1,0:T(8,128)S(1)}, u32[]{:S(2)}, u32[]{:S(2)}) collective-permute-start(f32[128,128]{1,0:T(8,128)S(1)} %bitcast.48), channel_id=1, source_target_pairs={{0,4},{1,5},{2,6},{3,7},{4,0},{5,1},{6,2},{7,3},{8,12},{9,13},{10,... | collective-permute-start | bytes 196616 | tf_op jit(solution)/shard_map/ppermute | solution.py:379
  3.8 1.9 %collective-permute-start.2 = (f32[128,128]{1,0:T(8,128)S(1)}, f32[128,128]{1,0:T(8,128)S(1)}, u32[]{:S(2)}, u32[]{:S(2)}) collective-permute-start(f32[128,128]{1,0:T(8,128)S(1)} %bitcast.49), channel_id=1, source_target_pairs={{0,6},{1,7},{2,0},{3,1},{4,2},{5,3},{6,4},{7,5},{8,14},{9,15},{10,... | collective-permute-start | bytes 196616 | tf_op jit(solution)/shard_map/ppermute | solution.py:379
  5.8 1.2 %slice.14 = f32[2,128,3,128]{3,2,1,0:T(4,128)S(1)} slice(f32[8,128,4,128]{3,2,1,0:T(4,128)} %param.1), slice={[0:2], [0:128], [1:4], [0:128]} | slice | bytes 786432 | tf_op jit(solution)/shard_map/slice | solution.py:394
  7.0 1.6 %collective-permute-start.11 = (f32[2,3,128,128]{3,2,1,0:T(8,128)S(1)}, f32[2,3,128,128]{3,2,1,0:T(8,128)S(1)}, u32[]{:S(2)}, u32[]{:S(2)}) collective-permute-start(f32[2,3,128,128]{3,2,1,0:T(8,128)S(1)} %bitcast.52), channel_id=1, source_target_pairs={{0,16},{8,24},{16,0},{24,8},{1,17},{9,25},{17,1},{25,9},{2,18},{10... | collective-permute-start | bytes 1179656 | tf_op jit(solution)/shard_map/ppermute | solution.py:379
  8.6 1.7 %slice.12 = f32[6,128,1,128]{3,2,1,0:T(1,128)S(1)} slice(f32[8,128,4,128]{3,2,1,0:T(4,128)} %param.1), slice={[2:8], [0:128], [0:1], [0:128]} | slice | bytes 786432 | tf_op jit(solution)/shard_map/slice | solution.py:401
  11.2 3.5 %collective-permute-start.16 = (f32[128,128]{1,0:T(8,128)S(1)}, f32[128,128]{1,0:T(8,128)S(1)}, u32[]{:S(2)}, u32[]{:S(2)}) collective-permute-start(f32[128,128]{1,0:T(8,128)S(1)} %bitcast.43), channel_id=1, source_target_pairs={{0,4},{1,5},{2,6},{3,7},{4,0},{5,1},{6,2},{7,3},{8,12},{9,13},{10,... | collective-permute-start | bytes 196616 | tf_op jit(solution)/shard_map/ppermute | solution.py:379
  14.7 1.5 %collective-permute-start.3 = (f32[4,128,128]{2,1,0:T(8,128)S(1)}, f32[4,128,128]{2,1,0:T(8,128)S(1)}, u32[]{:S(2)}, u32[]{:S(2)}) collective-permute-start(f32[4,128,128]{2,1,0:T(8,128)S(1)} %pad_maximum_fusion.1), channel_id=1, source_target_pairs={{0,1},{1,0},{2,3},{3,2},{4,5},{5,4},{6,7},{7,6},{8,9},{9,8},{10,11... | collective-permute-start | bytes 786440 | tf_op jit(solution)/shard_map/ppermute | solution.py:379
  16.3 4.8 %collective-permute-done.3 = f32[4,128,128]{2,1,0:T(8,128)S(1)} collective-permute-done((f32[4,128,128]{2,1,0:T(8,128)S(1)}, f32[4,128,128]{2,1,0:T(8,128)S(1)}, u32[]{:S(2)}, u32[]{:S(2)}) %collective-permute-start.3) | collective-permute-done | bytes 262176 | tf_op jit(solution)/shard_map/ppermute | solution.py:379
  21.1 1.0 collective-permute-start.8
  22.3 1.6 %collective-permute-start.18 = (f32[4,128,128]{2,1,0:T(8,128)S(1)}, f32[4,128,128]{2,1,0:T(8,128)S(1)}, u32[]{:S(2)}, u32[]{:S(2)}) collective-permute-start(f32[4,128,128]{2,1,0:T(8,128)S(1)} %pad_maximum_fusion.2), channel_id=1, source_target_pairs={{0,1},{1,0},{2,3},{3,2},{4,5},{5,4},{6,7},{7,6},{8,9},{9,8},{10,11... | collective-permute-start | bytes 786440 | tf_op jit(solution)/shard_map/ppermute | solution.py:379
  24.4 7.6 %collective-permute-done.8.refs_2_ = f32[8,128,128]{2,1,0:T(8,128)S(1)} collective-permute-done((f32[8,128,128]{2,1,0:T(8,128)S(1)}, f32[8,128,128]{2,1,0:T(8,128)S(1)}, u32[]{:S(2)}, u32[]{:S(2)}) %collective-permute-start.8) | collective-permute-done | bytes 524320 | tf_op jit(solution)/shard_map/ppermute | solution.py:379
  32.1 1.8 %collective-permute-start.4 = (f32[768,128]{1,0:T(8,128)S(1)}, f32[768,128]{1,0:T(8,128)S(1)}, u32[]{:S(2)}, u32[]{:S(2)}) collective-permute-start(f32[768,128]{1,0:T(8,128)S(1)} %bitcast.37), channel_id=1, source_target_pairs={{0,2},{1,3},{2,4},{3,5},{4,6},{5,7},{6,0},{7,1},{8,10},{9,11},{10,... | collective-permute-start | bytes 1179656 | tf_op jit(solution)/shard_map/ppermute | solution.py:379
  33.9 2.4 %collective-permute-start.5 = (f32[768,128]{1,0:T(8,128)S(1)}, f32[768,128]{1,0:T(8,128)S(1)}, u32[]{:S(2)}, u32[]{:S(2)}) collective-permute-start(f32[768,128]{1,0:T(8,128)S(1)} %bitcast.38), channel_id=1, source_target_pairs={{0,4},{1,5},{2,6},{3,7},{4,0},{5,1},{6,2},{7,3},{8,12},{9,13},{10,... | collective-permute-start | bytes 1179656 | tf_op jit(solution)/shard_map/ppermute | solution.py:379
  36.4 1.6 %collective-permute-start.7 = (f32[768,128]{1,0:T(8,128)S(1)}, f32[768,128]{1,0:T(8,128)S(1)}, u32[]{:S(2)}, u32[]{:S(2)}) collective-permute-start(f32[768,128]{1,0:T(8,128)S(1)} %bitcast.40), channel_id=1, source_target_pairs={{0,1},{1,0},{2,3},{3,2},{4,5},{5,4},{6,7},{7,6},{8,9},{9,8},{10,11... | collective-permute-start | bytes 1179656 | tf_op jit(solution)/shard_map/ppermute | solution.py:379
  38.0 1.3 %collective-permute-start.19 = (f32[8,128,128]{2,1,0:T(8,128)S(1)}, f32[8,128,128]{2,1,0:T(8,128)S(1)}, u32[]{:S(2)}, u32[]{:S(2)}) collective-permute-start(f32[8,128,128]{2,1,0:T(8,128)S(1)} %constant_dynamic-update-slice_fusion.5.refs_1_), channel_id=1, source_target_pairs={{0,16},{8,24},{16,0},{24,8},{1,17},{9,25},{17,1},{25,9},{2,18},{10... | collective-permute-start | bytes 1572872 | tf_op jit(solution)/shard_map/ppermute | solution.py:379
  39.4 24.3 %sweep0.1 = (f32[512,896]{1,0:T(8,128)}, f32[512,128]{1,0:T(8,128)}, f32[2,128,128]{2,1,0:T(8,128)}) custom-call(s32[2]{0:T(128)} %pad_add_fusion.refs_0_.place, f32[8,128,128]{2,1,0:T(8,128)} %copy-done.7, f32[8,128,128]{2,1,0:T(8,128)} %copy-done.9, f32[8,128,128]{2,1,0:T(8,128)} %copy-done.10, f32[8,128,128]{2,1,0:T(8,128)} %copy-done.11, ...), custom_call_target="tpu_custom_call" | custom-call | flops 8000000000 | bytes 10000000 | tf_op jit(solution)/shard_map/sweep0/pallas_call | solution.py:427
  63.9 4.3 %collective-permute-done.5.refs_2_ = f32[768,128]{1,0:T(8,128)S(1)} collective-permute-done((f32[768,128]{1,0:T(8,128)S(1)}, f32[768,128]{1,0:T(8,128)S(1)}, u32[]{:S(2)}, u32[]{:S(2)}) %collective-permute-start.5) | collective-permute-done | bytes 393248 | tf_op jit(solution)/shard_map/ppermute | solution.py:379
  68.2 2.1 %collective-permute-done.6.refs_3_ = f32[768,128]{1,0:T(8,128)S(1)} collective-permute-done((f32[768,128]{1,0:T(8,128)S(1)}, f32[768,128]{1,0:T(8,128)S(1)}, u32[]{:S(2)}, u32[]{:S(2)}) %collective-permute-start.6) | collective-permute-done | bytes 393248 | tf_op jit(solution)/shard_map/ppermute | solution.py:379
  71.2 1.5 %collective-permute-start.14 = (f32[3,768,128]{2,1,0:T(8,128)S(1)}, f32[3,768,128]{2,1,0:T(8,128)S(1)}, u32[]{:S(2)}, u32[]{:S(2)}) collective-permute-start(f32[3,768,128]{2,1,0:T(8,128)S(1)} %pad_maximum_fusion), channel_id=1, source_target_pairs={{0,1},{1,0},{2,3},{3,2},{4,5},{5,4},{6,7},{7,6},{8,9},{9,8},{10,11... | collective-permute-start | bytes 3538952 | tf_op jit(solution)/shard_map/ppermute | solution.py:379
  73.8 24.4 %sweep1.1 = (bf16[2,1024,512]{2,1,0:T(8,128)(2,1)}, f32[2,128,128]{2,1,0:T(8,128)}) custom-call(s32[2]{0:T(128)} %pad_add_fusion.refs_0_.place, f32[8,128,128]{2,1,0:T(8,128)} %copy-done.8, f32[8,128,128]{2,1,0:T(8,128)} %copy-done.12, f32[8,128,128]{2,1,0:T(8,128)} %copy-done.13, f32[8,128,128]{2,1,0:T(8,128)} %copy-done.14, f32[2,3,128,128]{3,2,1,0:T(8,128)} %bitcast.55, ...), custom_call_target="tpu_custom_call" | custom-call | flops 8000000000 | bytes 10000000 | tf_op jit(solution)/shard_map/sweep1/pallas_call | solution.py:427
  98.9 1.0 copy-done.4
  100.0 7.6 %close.1 = f32[4096,128]{1,0:T(8,128)} custom-call(s32[2]{0:T(128)} %pad_add_fusion.refs_0_.place, f32[768,128]{1,0:T(8,128)} %bitcast.41, f32[768,128]{1,0:T(8,128)} %copy-done, f32[768,128]{1,0:T(8,128)} %copy-done.1, f32[768,128]{1,0:T(8,128)} %copy-done.2, f32[768,128]{1,0:T(8,128)} %copy-done.5, f32[3,768,128]{2,1,0:T(8,128)} %copy-done.4, ...), custom_call_target="tpu_custom_call" | custom-call | tf_op jit(solution)/shard_map/close/pallas_call | solution.py:464
  (77 shorter events, 4.5 us)
Async XLA Ops:
  1.1 9.8 %collective-permute-start = (f32[128,128]{1,0:T(8,128)S(1)}, f32[128,128]{1,0:T(8,128)S(1)}, u32[]{:S(2)}, u32[]{:S(2)}) collective-permute-start(f32[128,128]{1,0:T(8,128)S(1)} %bitcast.47), channel_id=1, source_target_pairs={{0,2},{1,3},{2,4},{3,5},{4,6},{5,7},{6,0},{7,1},{8,10},{9,11},{10,... | collective-permute-start | bytes 196616 | tf_op jit(solution)/shard_map/ppermute | solution.py:379
  2.8 8.2 %collective-permute-start.1 = (f32[128,128]{1,0:T(8,128)S(1)}, f32[128,128]{1,0:T(8,128)S(1)}, u32[]{:S(2)}, u32[]{:S(2)}) collective-permute-start(f32[128,128]{1,0:T(8,128)S(1)} %bitcast.48), channel_id=1, source_target_pairs={{0,4},{1,5},{2,6},{3,7},{4,0},{5,1},{6,2},{7,3},{8,12},{9,13},{10,... | collective-permute-start | bytes 196616 | tf_op jit(solution)/shard_map/ppermute | solution.py:379
  3.8 7.1 %collective-permute-start.2 = (f32[128,128]{1,0:T(8,128)S(1)}, f32[128,128]{1,0:T(8,128)S(1)}, u32[]{:S(2)}, u32[]{:S(2)}) collective-permute-start(f32[128,128]{1,0:T(8,128)S(1)} %bitcast.49), channel_id=1, source_target_pairs={{0,6},{1,7},{2,0},{3,1},{4,2},{5,3},{6,4},{7,5},{8,14},{9,15},{10,... | collective-permute-start | bytes 196616 | tf_op jit(solution)/shard_map/ppermute | solution.py:379
  7.0 17.1 %collective-permute-start.11 = (f32[2,3,128,128]{3,2,1,0:T(8,128)S(1)}, f32[2,3,128,128]{3,2,1,0:T(8,128)S(1)}, u32[]{:S(2)}, u32[]{:S(2)}) collective-permute-start(f32[2,3,128,128]{3,2,1,0:T(8,128)S(1)} %bitcast.52), channel_id=1, source_target_pairs={{0,16},{8,24},{16,0},{24,8},{1,17},{9,25},{17,1},{25,9},{2,18},{10... | collective-permute-start | bytes 1179656 | tf_op jit(solution)/shard_map/ppermute | solution.py:379
  10.3 26.1 %copy-start.3 = (f32[6,128,1,128]{3,2,1,0:T(1,128)}, f32[6,128,1,128]{3,2,1,0:T(1,128)S(1)}, u32[]{:S(2)}) copy-start(f32[6,128,1,128]{3,2,1,0:T(1,128)S(1)} %slice.12) | copy-start | bytes 1179652
  11.0 11.2 %collective-permute-start.15 = (f32[128,128]{1,0:T(8,128)S(1)}, f32[128,128]{1,0:T(8,128)S(1)}, u32[]{:S(2)}, u32[]{:S(2)}) collective-permute-start(f32[128,128]{1,0:T(8,128)S(1)} %bitcast.42), channel_id=1, source_target_pairs={{0,2},{1,3},{2,4},{3,5},{4,6},{5,7},{6,0},{7,1},{8,10},{9,11},{10,... | collective-permute-start | bytes 196616 | tf_op jit(solution)/shard_map/ppermute | solution.py:379
  11.2 11.0 %collective-permute-start.16 = (f32[128,128]{1,0:T(8,128)S(1)}, f32[128,128]{1,0:T(8,128)S(1)}, u32[]{:S(2)}, u32[]{:S(2)}) collective-permute-start(f32[128,128]{1,0:T(8,128)S(1)} %bitcast.43), channel_id=1, source_target_pairs={{0,4},{1,5},{2,6},{3,7},{4,0},{5,1},{6,2},{7,3},{8,12},{9,13},{10,... | collective-permute-start | bytes 196616 | tf_op jit(solution)/shard_map/ppermute | solution.py:379
  14.7 7.5 %collective-permute-start.17 = (f32[128,128]{1,0:T(8,128)S(1)}, f32[128,128]{1,0:T(8,128)S(1)}, u32[]{:S(2)}, u32[]{:S(2)}) collective-permute-start(f32[128,128]{1,0:T(8,128)S(1)} %bitcast.44), channel_id=1, source_target_pairs={{0,6},{1,7},{2,0},{3,1},{4,2},{5,3},{6,4},{7,5},{8,14},{9,15},{10,... | collective-permute-start | bytes 196616 | tf_op jit(solution)/shard_map/ppermute | solution.py:379
  14.7 6.4 %collective-permute-start.3 = (f32[4,128,128]{2,1,0:T(8,128)S(1)}, f32[4,128,128]{2,1,0:T(8,128)S(1)}, u32[]{:S(2)}, u32[]{:S(2)}) collective-permute-start(f32[4,128,128]{2,1,0:T(8,128)S(1)} %pad_maximum_fusion.1), channel_id=1, source_target_pairs={{0,1},{1,0},{2,3},{3,2},{4,5},{5,4},{6,7},{7,6},{8,9},{9,8},{10,11... | collective-permute-start | bytes 786440 | tf_op jit(solution)/shard_map/ppermute | solution.py:379
  21.1 10.9 %collective-permute-start.8 = (f32[8,128,128]{2,1,0:T(8,128)S(1)}, f32[8,128,128]{2,1,0:T(8,128)S(1)}, u32[]{:S(2)}, u32[]{:S(2)}) collective-permute-start(f32[8,128,128]{2,1,0:T(8,128)S(1)} %constant_dynamic-update-slice_fusion.refs_1_), channel_id=1, source_target_pairs={{0,16},{8,24},{16,0},{24,8},{1,17},{9,25},{17,1},{25,9},{2,18},{10... | collective-permute-start | bytes 1572872 | tf_op jit(solution)/shard_map/ppermute | solution.py:379
  22.2 11.7 %collective-permute-start.12 = (f32[2,3,128,128]{3,2,1,0:T(8,128)S(1)}, f32[2,3,128,128]{3,2,1,0:T(8,128)S(1)}, u32[]{:S(2)}, u32[]{:S(2)}) collective-permute-start(f32[2,3,128,128]{3,2,1,0:T(8,128)S(1)} %bitcast.53), channel_id=1, source_target_pairs={{0,8},{8,0},{16,24},{24,16},{1,9},{9,1},{17,25},{25,17},{2,10},{10... | collective-permute-start | bytes 1179656 | tf_op jit(solution)/shard_map/ppermute | solution.py:379
  22.3 9.8 %collective-permute-start.18 = (f32[4,128,128]{2,1,0:T(8,128)S(1)}, f32[4,128,128]{2,1,0:T(8,128)S(1)}, u32[]{:S(2)}, u32[]{:S(2)}) collective-permute-start(f32[4,128,128]{2,1,0:T(8,128)S(1)} %pad_maximum_fusion.2), channel_id=1, source_target_pairs={{0,1},{1,0},{2,3},{3,2},{4,5},{5,4},{6,7},{7,6},{8,9},{9,8},{10,11... | collective-permute-start | bytes 786440 | tf_op jit(solution)/shard_map/ppermute | solution.py:379
  23.9 12.5 %collective-permute-start.9 = (f32[8,128,128]{2,1,0:T(8,128)S(1)}, f32[8,128,128]{2,1,0:T(8,128)S(1)}, u32[]{:S(2)}, u32[]{:S(2)}) collective-permute-start(f32[8,128,128]{2,1,0:T(8,128)S(1)} %constant_dynamic-update-slice_fusion.refs_1_), channel_id=1, source_target_pairs={{0,8},{8,0},{16,24},{24,16},{1,9},{9,1},{17,25},{25,17},{2,10},{10... | collective-permute-start | bytes 1572872 | tf_op jit(solution)/shard_map/ppermute | solution.py:379
  24.1 12.3 %collective-permute-start.13 = (f32[2,3,128,128]{3,2,1,0:T(8,128)S(1)}, f32[2,3,128,128]{3,2,1,0:T(8,128)S(1)}, u32[]{:S(2)}, u32[]{:S(2)}) collective-permute-start(f32[2,3,128,128]{3,2,1,0:T(8,128)S(1)} %collective-permute-done.11.refs_6_), channel_id=1, source_target_pairs={{0,8},{8,0},{16,24},{24,16},{1,9},{9,1},{17,25},{25,17},{2,10},{10... | collective-permute-start | bytes 1179656 | tf_op jit(solution)/shard_map/ppermute | solution.py:379
  32.0 6.0 %collective-permute-start.10 = (f32[8,128,128]{2,1,0:T(8,128)S(1)}, f32[8,128,128]{2,1,0:T(8,128)S(1)}, u32[]{:S(2)}, u32[]{:S(2)}) collective-permute-start(f32[8,128,128]{2,1,0:T(8,128)S(1)} %collective-permute-done.8.refs_2_), channel_id=1, source_target_pairs={{0,8},{8,0},{16,24},{24,16},{1,9},{9,1},{17,25},{25,17},{2,10},{10... | collective-permute-start | bytes 1572872 | tf_op jit(solution)/shard_map/ppermute | solution.py:379
  32.1 31.8 %collective-permute-start.4 = (f32[768,128]{1,0:T(8,128)S(1)}, f32[768,128]{1,0:T(8,128)S(1)}, u32[]{:S(2)}, u32[]{:S(2)}) collective-permute-start(f32[768,128]{1,0:T(8,128)S(1)} %bitcast.37), channel_id=1, source_target_pairs={{0,2},{1,3},{2,4},{3,5},{4,6},{5,7},{6,0},{7,1},{8,10},{9,11},{10,... | collective-permute-start | bytes 1179656 | tf_op jit(solution)/shard_map/ppermute | solution.py:379
  33.9 29.9 %copy-start.8 = (f32[8,128,128]{2,1,0:T(8,128)}, f32[8,128,128]{2,1,0:T(8,128)S(1)}, u32[]{:S(2)}) copy-start(f32[8,128,128]{2,1,0:T(8,128)S(1)} %constant_dynamic-update-slice_fusion.5.refs_1_) | copy-start | bytes 1572868
  33.9 34.3 %collective-permute-start.5 = (f32[768,128]{1,0:T(8,128)S(1)}, f32[768,128]{1,0:T(8,128)S(1)}, u32[]{:S(2)}, u32[]{:S(2)}) collective-permute-start(f32[768,128]{1,0:T(8,128)S(1)} %bitcast.38), channel_id=1, source_target_pairs={{0,4},{1,5},{2,6},{3,7},{4,0},{5,1},{6,2},{7,3},{8,12},{9,13},{10,... | collective-permute-start | bytes 1179656 | tf_op jit(solution)/shard_map/ppermute | solution.py:379
  36.4 33.9 %collective-permute-start.6 = (f32[768,128]{1,0:T(8,128)S(1)}, f32[768,128]{1,0:T(8,128)S(1)}, u32[]{:S(2)}, u32[]{:S(2)}) collective-permute-start(f32[768,128]{1,0:T(8,128)S(1)} %bitcast.39), channel_id=1, source_target_pairs={{0,6},{1,7},{2,0},{3,1},{4,2},{5,3},{6,4},{7,5},{8,14},{9,15},{10,... | collective-permute-start | bytes 1179656 | tf_op jit(solution)/shard_map/ppermute | solution.py:379
  36.4 27.3 %collective-permute-start.7 = (f32[768,128]{1,0:T(8,128)S(1)}, f32[768,128]{1,0:T(8,128)S(1)}, u32[]{:S(2)}, u32[]{:S(2)}) collective-permute-start(f32[768,128]{1,0:T(8,128)S(1)} %bitcast.40), channel_id=1, source_target_pairs={{0,1},{1,0},{2,3},{3,2},{4,5},{5,4},{6,7},{7,6},{8,9},{9,8},{10,11... | collective-permute-start | bytes 1179656 | tf_op jit(solution)/shard_map/ppermute | solution.py:379
  38.0 32.3 %collective-permute-start.19 = (f32[8,128,128]{2,1,0:T(8,128)S(1)}, f32[8,128,128]{2,1,0:T(8,128)S(1)}, u32[]{:S(2)}, u32[]{:S(2)}) collective-permute-start(f32[8,128,128]{2,1,0:T(8,128)S(1)} %constant_dynamic-update-slice_fusion.5.refs_1_), channel_id=1, source_target_pairs={{0,16},{8,24},{16,0},{24,8},{1,17},{9,25},{17,1},{25,9},{2,18},{10... | collective-permute-start | bytes 1572872 | tf_op jit(solution)/shard_map/ppermute | solution.py:379
  63.8 9.0 %collective-permute-start.20 = (f32[8,128,128]{2,1,0:T(8,128)S(1)}, f32[8,128,128]{2,1,0:T(8,128)S(1)}, u32[]{:S(2)}, u32[]{:S(2)}) collective-permute-start(f32[8,128,128]{2,1,0:T(8,128)S(1)} %constant_dynamic-update-slice_fusion.5.refs_1_), channel_id=1, source_target_pairs={{0,8},{8,0},{16,24},{24,16},{1,9},{9,1},{17,25},{25,17},{2,10},{10... | collective-permute-start | bytes 1572872 | tf_op jit(solution)/shard_map/ppermute | solution.py:379
  70.3 2.5 %collective-permute-start.21 = (f32[8,128,128]{2,1,0:T(8,128)S(1)}, f32[8,128,128]{2,1,0:T(8,128)S(1)}, u32[]{:S(2)}, u32[]{:S(2)}) collective-permute-start(f32[8,128,128]{2,1,0:T(8,128)S(1)} %collective-permute-done.19.refs_2_), channel_id=1, source_target_pairs={{0,8},{8,0},{16,24},{24,16},{1,9},{9,1},{17,25},{25,17},{2,10},{10... | collective-permute-start | bytes 1572872 | tf_op jit(solution)/shard_map/ppermute | solution.py:379
  71.2 27.7 %collective-permute-start.14 = (f32[3,768,128]{2,1,0:T(8,128)S(1)}, f32[3,768,128]{2,1,0:T(8,128)S(1)}, u32[]{:S(2)}, u32[]{:S(2)}) collective-permute-start(f32[3,768,128]{2,1,0:T(8,128)S(1)} %pad_maximum_fusion), channel_id=1, source_target_pairs={{0,1},{1,0},{2,3},{3,2},{4,5},{5,4},{6,7},{7,6},{8,9},{9,8},{10,11... | collective-permute-start | bytes 3538952 | tf_op jit(solution)/shard_map/ppermute | solution.py:379
  (16 other events, 88.9 us)

commit v5 on v4

--- a/solution.py
+++ b/solution.py
@@ -395,7 +395,7 @@
     strips = []
     for a in range(na):
         if a:
-            lines.append(line_of(blocks[a], line))
+            lines.append(line_of(blocks[a], side[1]))
         line = jnp.stack(lines[a])
         strips.append(jnp.concatenate([line, step_to(line, "col", cols_dev, n_low, 0, 1)]))
     body = line_of(matrix[na:, :, 0, :].reshape(-1, nb), strips[0])
@@ -409,7 +409,7 @@
     vmem = pl.BlockSpec(memory_space=pltpu.VMEM)
     smem = pl.BlockSpec(memory_space=pltpu.SMEM)
     hbm = pl.BlockSpec(memory_space=pl.ANY)
-    params = pltpu.CompilerParams(vmem_limit_bytes=56 << 20)
+    params = pltpu.CompilerParams(vmem_limit_bytes=20 << 20)
     carried = []
     for phase, pieces in enumerate(phases):
         last = phase == na - 1
@@ -455,7 +455,7 @@
                 pltpu.SemaphoreType.DMA((rows // nb,)),
             ],
             compiler_params=params,
-            cost_estimate=pl.CostEstimate(flops=8 * 10**9, bytes_accessed=10**7, transcendentals=0),
+            cost_estimate=pl.CostEstimate(flops=3 * 10**9, bytes_accessed=10**7, transcendentals=0),
             name="sweep%d" % phase,
         )(place, *pieces, *side, *carried)
         if phase == 0:

time: 108 us -> 106 us (0.981)
  waiting for transfers between devices: 19.7 us -> 26.8 us
  Pallas kernels: 56.3 us -> 52 us
  starting transfers between devices: 23.5 us -> 20.2 us
  local copies, waits for them, and re-layouts: 6.9 us -> 5.35 us
    ppermute x22, waiting for transfers between devices: 19.7 us -> 26.8 us  [step_to(): return lax.ppermute(x, axis, pairs)]
    pallas_call x2, Pallas kernels: 48.7 us -> 45.1 us  [local(): pl.pallas_call(functools.partial(sweep_kernel, phase=phase, last=last, nb...]
    ppermute x22, starting transfers between devices: 23.5 us -> 20.2 us  [step_to(): return lax.ppermute(x, axis, pairs)]
    slice x1, local copies, waits for them, and re-layouts: 1.68 us -> 0.27 us  [local(): body = line_of(matrix[na:, :, 0, :].reshape(-1, nb), strips[0])]
    unnamed x45 -> x11, local copies, waits for them, and re-layouts: 2.89 us -> 2.59 us
  transfers between devices with their start and end apart: 22 -> 22, of which waited for: 5 -> 12; matrix products, arithmetic and copies ran while one was open for 3% -> 5% of each run, Pallas kernels for 45% -> 43%
where the time goes in v5:
time: 106 us
  Pallas kernels  52 us (49%)
  waiting for transfers between devices  26.8 us (25%)
  starting transfers between devices  20.2 us (19%)
  local copies, waits for them, and re-layouts  5.35 us (5%)
  other arithmetic  1.1 us (1%)
    pallas_call x2, Pallas kernels, local(): pl.pallas_call(functools.partial(sweep_kernel, phase=phase, last=last, nb...  45.1 us
    ppermute x22, waiting for transfers between devices, step_to(): return lax.ppermute(x, axis, pairs)  26.8 us
    ppermute x22, starting transfers between devices, step_to(): return lax.ppermute(x, axis, pairs)  20.2 us
    pallas_call x1, Pallas kernels, local(): pl.pallas_call(functools.partial(close_kernel, nb=nb, na=na, block_rows=b...  6.87 us
    unnamed x11, local copies, waits for them, and re-layouts  2.59 us
  transfers between devices with their start and end apart: 22, of which 12 were waited for; matrix products, arithmetic and copies ran while one was open for 5% of the time, Pallas kernels for 43%

profile of v5, /device:TPU:8, one launch (start us, length us, event | category | flops | bytes accessed | tf_op | source)
XLA Modules:
  0.0 105.8 jit_solution(5513167323761166838)
XLA Ops:
  0.0 1.3 %fusion = (f32[1,128,1,128]{3,2,1,0:T(1,128)S(1)}, f32[1,128,1,128]{3,2,1,0:T(1,128)S(1)}) fusion(f32[8,128,4,128]{3,2,1,0:T(4,128)} %param.1), kind=kLoop, calls=%fused_computation.15 | loop fusion | bytes 262144 | tf_op jit(solution)/shard_map/slice | solution.py:392
  1.3 1.6 %collective-permute-start = (f32[128,128]{1,0:T(8,128)S(1)}, f32[128,128]{1,0:T(8,128)}, u32[]{:S(2)}, u32[]{:S(2)}) collective-permute-start(f32[128,128]{1,0:T(8,128)S(1)} %bitcast.51), channel_id=1, source_target_pairs={{0,2},{1,3},{2,4},{3,5},{4,6},{5,7},{6,0},{7,1},{8,10},{9,11},{10,... | collective-permute-start | bytes 196616 | tf_op jit(solution)/shard_map/ppermute | solution.py:379
  4.0 1.9 %collective-permute-start.2 = (f32[128,128]{1,0:T(8,128)S(1)}, f32[128,128]{1,0:T(8,128)}, u32[]{:S(2)}, u32[]{:S(2)}) collective-permute-start(f32[128,128]{1,0:T(8,128)S(1)} %bitcast.53), channel_id=1, source_target_pairs={{0,6},{1,7},{2,0},{3,1},{4,2},{5,3},{6,4},{7,5},{8,14},{9,15},{10,... | collective-permute-start | bytes 196616 | tf_op jit(solution)/shard_map/ppermute | solution.py:379
  5.9 1.2 %slice.14 = f32[2,128,3,128]{3,2,1,0:T(4,128)S(1)} slice(f32[8,128,4,128]{3,2,1,0:T(4,128)} %param.1), slice={[0:2], [0:128], [1:4], [0:128]} | slice | bytes 786432 | tf_op jit(solution)/shard_map/slice | solution.py:394
  7.2 1.6 %collective-permute-start.11 = (f32[2,3,128,128]{3,2,1,0:T(8,128)S(1)}, f32[2,3,128,128]{3,2,1,0:T(8,128)}, u32[]{:S(2)}, u32[]{:S(2)}) collective-permute-start(f32[2,3,128,128]{3,2,1,0:T(8,128)S(1)} %bitcast.42), channel_id=1, source_target_pairs={{0,16},{8,24},{16,0},{24,8},{1,17},{9,25},{17,1},{25,9},{2,18},{10... | collective-permute-start | bytes 1179656 | tf_op jit(solution)/shard_map/ppermute | solution.py:379
  9.1 1.2 %collective-permute-done.2 = f32[128,128]{1,0:T(8,128)} collective-permute-done((f32[128,128]{1,0:T(8,128)S(1)}, f32[128,128]{1,0:T(8,128)}, u32[]{:S(2)}, u32[]{:S(2)}) %collective-permute-start.2) | collective-permute-done | bytes 65568 | tf_op jit(solution)/shard_map/ppermute | solution.py:379
  11.3 1.6 %collective-permute-start.3 = (f32[4,128,128]{2,1,0:T(8,128)S(1)}, f32[4,128,128]{2,1,0:T(8,128)S(1)}, u32[]{:S(2)}, u32[]{:S(2)}) collective-permute-start(f32[4,128,128]{2,1,0:T(8,128)S(1)} %pad_maximum_fusion.1), channel_id=1, source_target_pairs={{0,1},{1,0},{2,3},{3,2},{4,5},{5,4},{6,7},{7,6},{8,9},{9,8},{10,11... | collective-permute-start | bytes 786440 | tf_op jit(solution)/shard_map/ppermute | solution.py:379
  15.4 4.1 %collective-permute-done.3 = f32[4,128,128]{2,1,0:T(8,128)S(1)} collective-permute-done((f32[4,128,128]{2,1,0:T(8,128)S(1)}, f32[4,128,128]{2,1,0:T(8,128)S(1)}, u32[]{:S(2)}, u32[]{:S(2)}) %collective-permute-start.3) | collective-permute-done | bytes 262176 | tf_op jit(solution)/shard_map/ppermute | solution.py:379
  19.5 1.3 %collective-permute-start.8 = (f32[8,128,128]{2,1,0:T(8,128)S(1)}, f32[8,128,128]{2,1,0:T(8,128)S(1)}, u32[]{:S(2)}, u32[]{:S(2)}) collective-permute-start(f32[8,128,128]{2,1,0:T(8,128)S(1)} %constant_dynamic-update-slice_fusion.refs_1_), channel_id=1, source_target_pairs={{0,16},{8,24},{16,0},{24,8},{1,17},{9,25},{17,1},{25,9},{2,18},{10... | collective-permute-start | bytes 1572872 | tf_op jit(solution)/shard_map/ppermute | solution.py:379
  20.8 2.4 %collective-permute-start.16 = (f32[128,128]{1,0:T(8,128)S(1)}, f32[128,128]{1,0:T(8,128)S(1)}, u32[]{:S(2)}, u32[]{:S(2)}) collective-permute-start(f32[128,128]{1,0:T(8,128)S(1)} %bitcast.47), channel_id=1, source_target_pairs={{0,4},{1,5},{2,6},{3,7},{4,0},{5,1},{6,2},{7,3},{8,12},{9,13},{10,... | collective-permute-start | bytes 196616 | tf_op jit(solution)/shard_map/ppermute | solution.py:379
  23.4 2.0 %collective-permute-done.15 = f32[128,128]{1,0:T(8,128)S(1)} collective-permute-done((f32[128,128]{1,0:T(8,128)S(1)}, f32[128,128]{1,0:T(8,128)S(1)}, u32[]{:S(2)}, u32[]{:S(2)}) %collective-permute-start.15) | collective-permute-done | bytes 65568 | tf_op jit(solution)/shard_map/ppermute | solution.py:379
  26.4 1.8 %collective-permute-done.17 = f32[128,128]{1,0:T(8,128)S(1)} collective-permute-done((f32[128,128]{1,0:T(8,128)S(1)}, f32[128,128]{1,0:T(8,128)S(1)}, u32[]{:S(2)}, u32[]{:S(2)}) %collective-permute-start.17) | collective-permute-done | bytes 65568 | tf_op jit(solution)/shard_map/ppermute | solution.py:379
  28.3 1.5 %collective-permute-start.18 = (f32[4,128,128]{2,1,0:T(8,128)S(1)}, f32[4,128,128]{2,1,0:T(8,128)S(1)}, u32[]{:S(2)}, u32[]{:S(2)}) collective-permute-start(f32[4,128,128]{2,1,0:T(8,128)S(1)} %pad_maximum_fusion.2), channel_id=1, source_target_pairs={{0,1},{1,0},{2,3},{3,2},{4,5},{5,4},{6,7},{7,6},{8,9},{9,8},{10,11... | collective-permute-start | bytes 786440 | tf_op jit(solution)/shard_map/ppermute | solution.py:379
  29.8 2.7 %collective-permute-done.8.refs_2_ = f32[8,128,128]{2,1,0:T(8,128)S(1)} collective-permute-done((f32[8,128,128]{2,1,0:T(8,128)S(1)}, f32[8,128,128]{2,1,0:T(8,128)S(1)}, u32[]{:S(2)}, u32[]{:S(2)}) %collective-permute-start.8) | collective-permute-done | bytes 524320 | tf_op jit(solution)/shard_map/ppermute | solution.py:379
  32.6 3.0 %collective-permute-done.18 = f32[4,128,128]{2,1,0:T(8,128)S(1)} collective-permute-done((f32[4,128,128]{2,1,0:T(8,128)S(1)}, f32[4,128,128]{2,1,0:T(8,128)S(1)}, u32[]{:S(2)}, u32[]{:S(2)}) %collective-permute-start.18) | collective-permute-done | bytes 262176 | tf_op jit(solution)/shard_map/ppermute | solution.py:379
  35.6 2.4 %collective-permute-start.5 = (f32[768,128]{1,0:T(8,128)S(1)}, f32[768,128]{1,0:T(8,128)S(1)}, u32[]{:S(2)}, u32[]{:S(2)}) collective-permute-start(f32[768,128]{1,0:T(8,128)S(1)} %bitcast.38), channel_id=1, source_target_pairs={{0,4},{1,5},{2,6},{3,7},{4,0},{5,1},{6,2},{7,3},{8,12},{9,13},{10,... | collective-permute-start | bytes 1179656 | tf_op jit(solution)/shard_map/ppermute | solution.py:379
  38.0 1.6 %collective-permute-start.7 = (f32[768,128]{1,0:T(8,128)S(1)}, f32[768,128]{1,0:T(8,128)S(1)}, u32[]{:S(2)}, u32[]{:S(2)}) collective-permute-start(f32[768,128]{1,0:T(8,128)S(1)} %bitcast.40), channel_id=1, source_target_pairs={{0,1},{1,0},{2,3},{3,2},{4,5},{5,4},{6,7},{7,6},{8,9},{9,8},{10,11... | collective-permute-start | bytes 1179656 | tf_op jit(solution)/shard_map/ppermute | solution.py:379
  40.6 22.2 %sweep0.1 = (f32[512,896]{1,0:T(8,128)S(1)}, f32[512,128]{1,0:T(8,128)S(1)}, f32[2,128,128]{2,1,0:T(8,128)S(1)}) custom-call(s32[2]{0:T(128)S(1)} %pad_add_fusion.refs_0_.place, f32[8,128,128]{2,1,0:T(8,128)S(1)} %constant_dynamic-update-slice_fusion.refs_1_, f32[8,128,128]{2,1,0:T(8,128)S(1)} %collective-permute-done.8.refs_2_, ...), custom_call_target="tpu_custom_call" | custom-call | flops 3000000000 | bytes 10000000 | tf_op jit(solution)/shard_map/sweep0/pallas_call | solution.py:427
  62.8 4.4 %collective-permute-done.5.refs_2_ = f32[768,128]{1,0:T(8,128)S(1)} collective-permute-done((f32[768,128]{1,0:T(8,128)S(1)}, f32[768,128]{1,0:T(8,128)S(1)}, u32[]{:S(2)}, u32[]{:S(2)}) %collective-permute-start.5) | collective-permute-done | bytes 393248 | tf_op jit(solution)/shard_map/ppermute | solution.py:379
  67.2 3.5 %collective-permute-done.6.refs_3_ = f32[768,128]{1,0:T(8,128)S(1)} collective-permute-done((f32[768,128]{1,0:T(8,128)S(1)}, f32[768,128]{1,0:T(8,128)S(1)}, u32[]{:S(2)}, u32[]{:S(2)}) %collective-permute-start.6) | collective-permute-done | bytes 393248 | tf_op jit(solution)/shard_map/ppermute | solution.py:379
  70.8 1.5 %collective-permute-start.14 = (f32[3,768,128]{2,1,0:T(8,128)S(1)}, f32[3,768,128]{2,1,0:T(8,128)S(1)}, u32[]{:S(2)}, u32[]{:S(2)}) collective-permute-start(f32[3,768,128]{2,1,0:T(8,128)S(1)} %pad_maximum_fusion), channel_id=1, source_target_pairs={{0,1},{1,0},{2,3},{3,2},{4,5},{5,4},{6,7},{7,6},{8,9},{9,8},{10,11... | collective-permute-start | bytes 3538952 | tf_op jit(solution)/shard_map/ppermute | solution.py:379
  72.8 1.4 %collective-permute-done.20.refs_3_ = f32[8,128,128]{2,1,0:T(8,128)S(1)} collective-permute-done((f32[8,128,128]{2,1,0:T(8,128)S(1)}, f32[8,128,128]{2,1,0:T(8,128)S(1)}, u32[]{:S(2)}, u32[]{:S(2)}) %collective-permute-start.20) | collective-permute-done | bytes 524320 | tf_op jit(solution)/shard_map/ppermute | solution.py:379
  75.0 22.9 %sweep1.1 = (bf16[2,1024,512]{2,1,0:T(8,128)(2,1)S(1)}, f32[2,128,128]{2,1,0:T(8,128)S(1)}) custom-call(s32[2]{0:T(128)S(1)} %pad_add_fusion.refs_0_.place, f32[8,128,128]{2,1,0:T(8,128)S(1)} %constant_dynamic-update-slice_fusion.5.refs_1_, f32[8,128,128]{2,1,0:T(8,128)S(1)} %collective-permute-done.19.refs_2_, ...), custom_call_target="tpu_custom_call" | custom-call | flops 3000000000 | bytes 10000000 | tf_op jit(solution)/shard_map/sweep1/pallas_call | solution.py:427
  98.8 6.9 %close.1 = f32[4096,128]{1,0:T(8,128)} custom-call(s32[2]{0:T(128)S(1)} %pad_add_fusion.refs_0_.place, f32[768,128]{1,0:T(8,128)S(1)} %bitcast.41, f32[768,128]{1,0:T(8,128)S(1)} %collective-permute-done.4.refs_1_, f32[768,128]{1,0:T(8,128)S(1)} %collective-permute-done.5.refs_2_, f32[768,128]{1,0:T(8,128)S(1)} %collective-permute-done.6.refs_3_, ...), custom_call_target="tpu_custom_call" | custom-call | tf_op jit(solution)/shard_map/close/pallas_call | solution.py:464
  (43 shorter events, 9.5 us)
Async XLA Ops:
  0.0 8.7 %copy-start = (f32[8,128,4,128]{3,2,1,0:T(4,128)S(1)}, f32[8,128,4,128]{3,2,1,0:T(4,128)}, u32[]{:S(2)}) copy-start(f32[8,128,4,128]{3,2,1,0:T(4,128)} %param.1) | copy-start | bytes 6291460
  1.3 7.8 %collective-permute-start = (f32[128,128]{1,0:T(8,128)S(1)}, f32[128,128]{1,0:T(8,128)}, u32[]{:S(2)}, u32[]{:S(2)}) collective-permute-start(f32[128,128]{1,0:T(8,128)S(1)} %bitcast.51), channel_id=1, source_target_pairs={{0,2},{1,3},{2,4},{3,5},{4,6},{5,7},{6,0},{7,1},{8,10},{9,11},{10,... | collective-permute-start | bytes 196616 | tf_op jit(solution)/shard_map/ppermute | solution.py:379
  2.9 6.2 %collective-permute-start.1 = (f32[128,128]{1,0:T(8,128)S(1)}, f32[128,128]{1,0:T(8,128)}, u32[]{:S(2)}, u32[]{:S(2)}) collective-permute-start(f32[128,128]{1,0:T(8,128)S(1)} %bitcast.52), channel_id=1, source_target_pairs={{0,4},{1,5},{2,6},{3,7},{4,0},{5,1},{6,2},{7,3},{8,12},{9,13},{10,... | collective-permute-start | bytes 196616 | tf_op jit(solution)/shard_map/ppermute | solution.py:379
  4.0 6.3 %collective-permute-start.2 = (f32[128,128]{1,0:T(8,128)S(1)}, f32[128,128]{1,0:T(8,128)}, u32[]{:S(2)}, u32[]{:S(2)}) collective-permute-start(f32[128,128]{1,0:T(8,128)S(1)} %bitcast.53), channel_id=1, source_target_pairs={{0,6},{1,7},{2,0},{3,1},{4,2},{5,3},{6,4},{7,5},{8,14},{9,15},{10,... | collective-permute-start | bytes 196616 | tf_op jit(solution)/shard_map/ppermute | solution.py:379
  7.2 13.6 %collective-permute-start.11 = (f32[2,3,128,128]{3,2,1,0:T(8,128)S(1)}, f32[2,3,128,128]{3,2,1,0:T(8,128)}, u32[]{:S(2)}, u32[]{:S(2)}) collective-permute-start(f32[2,3,128,128]{3,2,1,0:T(8,128)S(1)} %bitcast.42), channel_id=1, source_target_pairs={{0,16},{8,24},{16,0},{24,8},{1,17},{9,25},{17,1},{25,9},{2,18},{10... | collective-permute-start | bytes 1179656 | tf_op jit(solution)/shard_map/ppermute | solution.py:379
  8.7 23.8 %collective-permute-start.12 = (f32[2,3,128,128]{3,2,1,0:T(8,128)S(1)}, f32[2,3,128,128]{3,2,1,0:T(8,128)}, u32[]{:S(2)}, u32[]{:S(2)}) collective-permute-start(f32[2,3,128,128]{3,2,1,0:T(8,128)S(1)} %bitcast.43), channel_id=1, source_target_pairs={{0,8},{8,0},{16,24},{24,16},{1,9},{9,1},{17,25},{25,17},{2,10},{10... | collective-permute-start | bytes 1179656 | tf_op jit(solution)/shard_map/ppermute | solution.py:379
  11.3 8.2 %collective-permute-start.3 = (f32[4,128,128]{2,1,0:T(8,128)S(1)}, f32[4,128,128]{2,1,0:T(8,128)S(1)}, u32[]{:S(2)}, u32[]{:S(2)}) collective-permute-start(f32[4,128,128]{2,1,0:T(8,128)S(1)} %pad_maximum_fusion.1), channel_id=1, source_target_pairs={{0,1},{1,0},{2,3},{3,2},{4,5},{5,4},{6,7},{7,6},{8,9},{9,8},{10,11... | collective-permute-start | bytes 786440 | tf_op jit(solution)/shard_map/ppermute | solution.py:379
  19.5 13.0 %collective-permute-start.8 = (f32[8,128,128]{2,1,0:T(8,128)S(1)}, f32[8,128,128]{2,1,0:T(8,128)S(1)}, u32[]{:S(2)}, u32[]{:S(2)}) collective-permute-start(f32[8,128,128]{2,1,0:T(8,128)S(1)} %constant_dynamic-update-slice_fusion.refs_1_), channel_id=1, source_target_pairs={{0,16},{8,24},{16,0},{24,8},{1,17},{9,25},{17,1},{25,9},{2,18},{10... | collective-permute-start | bytes 1572872 | tf_op jit(solution)/shard_map/ppermute | solution.py:379
  20.8 4.6 %collective-permute-start.15 = (f32[128,128]{1,0:T(8,128)S(1)}, f32[128,128]{1,0:T(8,128)S(1)}, u32[]{:S(2)}, u32[]{:S(2)}) collective-permute-start(f32[128,128]{1,0:T(8,128)S(1)} %bitcast.46), channel_id=1, source_target_pairs={{0,2},{1,3},{2,4},{3,5},{4,6},{5,7},{6,0},{7,1},{8,10},{9,11},{10,... | collective-permute-start | bytes 196616 | tf_op jit(solution)/shard_map/ppermute | solution.py:379
  20.8 5.6 %collective-permute-start.16 = (f32[128,128]{1,0:T(8,128)S(1)}, f32[128,128]{1,0:T(8,128)S(1)}, u32[]{:S(2)}, u32[]{:S(2)}) collective-permute-start(f32[128,128]{1,0:T(8,128)S(1)} %bitcast.47), channel_id=1, source_target_pairs={{0,4},{1,5},{2,6},{3,7},{4,0},{5,1},{6,2},{7,3},{8,12},{9,13},{10,... | collective-permute-start | bytes 196616 | tf_op jit(solution)/shard_map/ppermute | solution.py:379
  23.2 5.1 %collective-permute-start.17 = (f32[128,128]{1,0:T(8,128)S(1)}, f32[128,128]{1,0:T(8,128)S(1)}, u32[]{:S(2)}, u32[]{:S(2)}) collective-permute-start(f32[128,128]{1,0:T(8,128)S(1)} %bitcast.48), channel_id=1, source_target_pairs={{0,6},{1,7},{2,0},{3,1},{4,2},{5,3},{6,4},{7,5},{8,14},{9,15},{10,... | collective-permute-start | bytes 196616 | tf_op jit(solution)/shard_map/ppermute | solution.py:379
  25.4 12.6 %collective-permute-start.9 = (f32[8,128,128]{2,1,0:T(8,128)S(1)}, f32[8,128,128]{2,1,0:T(8,128)S(1)}, u32[]{:S(2)}, u32[]{:S(2)}) collective-permute-start(f32[8,128,128]{2,1,0:T(8,128)S(1)} %constant_dynamic-update-slice_fusion.refs_1_), channel_id=1, source_target_pairs={{0,8},{8,0},{16,24},{24,16},{1,9},{9,1},{17,25},{25,17},{2,10},{10... | collective-permute-start | bytes 1572872 | tf_op jit(solution)/shard_map/ppermute | solution.py:379
  26.4 11.6 %collective-permute-start.13 = (f32[2,3,128,128]{3,2,1,0:T(8,128)}, f32[2,3,128,128]{3,2,1,0:T(8,128)S(1)}, u32[]{:S(2)}, u32[]{:S(2)}) collective-permute-start(f32[2,3,128,128]{3,2,1,0:T(8,128)} %collective-permute-done.11.refs_6_), channel_id=1, source_target_pairs={{0,8},{8,0},{16,24},{24,16},{1,9},{9,1},{17,25},{25,17},{2,10},{10... | collective-permute-start | bytes 1179656 | tf_op jit(solution)/shard_map/ppermute | solution.py:379
  28.3 7.3 %collective-permute-start.18 = (f32[4,128,128]{2,1,0:T(8,128)S(1)}, f32[4,128,128]{2,1,0:T(8,128)S(1)}, u32[]{:S(2)}, u32[]{:S(2)}) collective-permute-start(f32[4,128,128]{2,1,0:T(8,128)S(1)} %pad_maximum_fusion.2), channel_id=1, source_target_pairs={{0,1},{1,0},{2,3},{3,2},{4,5},{5,4},{6,7},{7,6},{8,9},{9,8},{10,11... | collective-permute-start | bytes 786440 | tf_op jit(solution)/shard_map/ppermute | solution.py:379
  32.5 7.1 %collective-permute-start.10 = (f32[8,128,128]{2,1,0:T(8,128)S(1)}, f32[8,128,128]{2,1,0:T(8,128)S(1)}, u32[]{:S(2)}, u32[]{:S(2)}) collective-permute-start(f32[8,128,128]{2,1,0:T(8,128)S(1)} %collective-permute-done.8.refs_2_), channel_id=1, source_target_pairs={{0,8},{8,0},{16,24},{24,16},{1,9},{9,1},{17,25},{25,17},{2,10},{10... | collective-permute-start | bytes 1572872 | tf_op jit(solution)/shard_map/ppermute | solution.py:379
  32.6 30.2 %collective-permute-start.4 = (f32[768,128]{1,0:T(8,128)S(1)}, f32[768,128]{1,0:T(8,128)S(1)}, u32[]{:S(2)}, u32[]{:S(2)}) collective-permute-start(f32[768,128]{1,0:T(8,128)S(1)} %bitcast.37), channel_id=1, source_target_pairs={{0,2},{1,3},{2,4},{3,5},{4,6},{5,7},{6,0},{7,1},{8,10},{9,11},{10,... | collective-permute-start | bytes 1179656 | tf_op jit(solution)/shard_map/ppermute | solution.py:379
  35.6 31.6 %collective-permute-start.5 = (f32[768,128]{1,0:T(8,128)S(1)}, f32[768,128]{1,0:T(8,128)S(1)}, u32[]{:S(2)}, u32[]{:S(2)}) collective-permute-start(f32[768,128]{1,0:T(8,128)S(1)} %bitcast.38), channel_id=1, source_target_pairs={{0,4},{1,5},{2,6},{3,7},{4,0},{5,1},{6,2},{7,3},{8,12},{9,13},{10,... | collective-permute-start | bytes 1179656 | tf_op jit(solution)/shard_map/ppermute | solution.py:379
  38.0 32.7 %collective-permute-start.6 = (f32[768,128]{1,0:T(8,128)S(1)}, f32[768,128]{1,0:T(8,128)S(1)}, u32[]{:S(2)}, u32[]{:S(2)}) collective-permute-start(f32[768,128]{1,0:T(8,128)S(1)} %bitcast.39), channel_id=1, source_target_pairs={{0,6},{1,7},{2,0},{3,1},{4,2},{5,3},{6,4},{7,5},{8,14},{9,15},{10,... | collective-permute-start | bytes 1179656 | tf_op jit(solution)/shard_map/ppermute | solution.py:379
  38.0 24.8 %collective-permute-start.7 = (f32[768,128]{1,0:T(8,128)S(1)}, f32[768,128]{1,0:T(8,128)S(1)}, u32[]{:S(2)}, u32[]{:S(2)}) collective-permute-start(f32[768,128]{1,0:T(8,128)S(1)} %bitcast.40), channel_id=1, source_target_pairs={{0,1},{1,0},{2,3},{3,2},{4,5},{5,4},{6,7},{7,6},{8,9},{9,8},{10,11... | collective-permute-start | bytes 1179656 | tf_op jit(solution)/shard_map/ppermute | solution.py:379
  39.6 32.7 %collective-permute-start.19 = (f32[8,128,128]{2,1,0:T(8,128)S(1)}, f32[8,128,128]{2,1,0:T(8,128)S(1)}, u32[]{:S(2)}, u32[]{:S(2)}) collective-permute-start(f32[8,128,128]{2,1,0:T(8,128)S(1)} %constant_dynamic-update-slice_fusion.5.refs_1_), channel_id=1, source_target_pairs={{0,16},{8,24},{16,0},{24,8},{1,17},{9,25},{17,1},{25,9},{2,18},{10... | collective-permute-start | bytes 1572872 | tf_op jit(solution)/shard_map/ppermute | solution.py:379
  70.8 28.0 %collective-permute-start.14 = (f32[3,768,128]{2,1,0:T(8,128)S(1)}, f32[3,768,128]{2,1,0:T(8,128)S(1)}, u32[]{:S(2)}, u32[]{:S(2)}) collective-permute-start(f32[3,768,128]{2,1,0:T(8,128)S(1)} %pad_maximum_fusion), channel_id=1, source_target_pairs={{0,1},{1,0},{2,3},{3,2},{4,5},{5,4},{6,7},{7,6},{8,9},{9,8},{10,11... | collective-permute-start | bytes 3538952 | tf_op jit(solution)/shard_map/ppermute | solution.py:379
  72.3 1.9 %collective-permute-start.20 = (f32[8,128,128]{2,1,0:T(8,128)S(1)}, f32[8,128,128]{2,1,0:T(8,128)S(1)}, u32[]{:S(2)}, u32[]{:S(2)}) collective-permute-start(f32[8,128,128]{2,1,0:T(8,128)S(1)} %constant_dynamic-update-slice_fusion.5.refs_1_), channel_id=1, source_target_pairs={{0,8},{8,0},{16,24},{24,16},{1,9},{9,1},{17,25},{25,17},{2,10},{10... | collective-permute-start | bytes 1572872 | tf_op jit(solution)/shard_map/ppermute | solution.py:379
  72.3 2.7 %collective-permute-start.21 = (f32[8,128,128]{2,1,0:T(8,128)S(1)}, f32[8,128,128]{2,1,0:T(8,128)S(1)}, u32[]{:S(2)}, u32[]{:S(2)}) collective-permute-start(f32[8,128,128]{2,1,0:T(8,128)S(1)} %collective-permute-done.19.refs_2_), channel_id=1, source_target_pairs={{0,8},{8,0},{16,24},{24,16},{1,9},{9,1},{17,25},{25,17},{2,10},{10... | collective-permute-start | bytes 1572872 | tf_op jit(solution)/shard_map/ppermute | solution.py:379

commit v6 on v5

--- a/solution.py
+++ b/solution.py
@@ -8,7 +8,7 @@
 from jax.sharding import PartitionSpec as P
 
 STEPS = 8
-PANEL = 32
+PANEL = 64
 SUB = 8
 F32 = jnp.float32
 BF16 = jnp.bfloat16
@@ -193,15 +193,17 @@
                 split2(grid_ref[at, :c0]), (upper[0], upper[1]), MM
             )
 
-    def settle(k, here):
+    def settle(k, here, first_col):
         base = k * nb
+        off = first_col - c0
         g = held[...]
-        r = three(split2(gram(g, g)), split2(grid_ref[here, c0:]), MM)
+        gs = split2(g)
+        r = three(split2(three(gs, gs, ((0,), (0,)))), split2(grid_ref[here, first_col:]), MM)
         at = lax.broadcasted_iota(jnp.int32, (rows, nb), 0)
         column = jnp.where((at >= base) & (at < base + nb), 0.0, grid_ref[:rows, here])
         lcol[0], lcol[1] = split2(column)
-        rrow[0], rrow[1] = split2(r)
-        grid_ref[here, c0:] = r
+        rrow[0, :, off:], rrow[1, :, off:] = split2(r)
+        grid_ref[here, first_col:] = r
 
     def step(k, here, filler):
         base = k * nb
@@ -258,7 +260,7 @@
 
         def late(turn):
             if turn == 0:
-                settle(k - 1, before)
+                settle(k - 1, before, c0)
             turns = nb // SUB - 1
             for i in range(rows // nb):
                 if i % turns == turn - 1:
@@ -266,7 +268,7 @@
 
         step(k, here, late)
 
-    settle((phase + 1) * rows_dev - 1, slice(rows - nb, rows))
+    settle((phase + 1) * rows_dev - 1, slice(rows - nb, rows), lead if last else rows)
     sent = []
     for i in range(rows // nb):
         at = slice(i * nb, i * nb + nb)
@@ -392,14 +394,14 @@
     blocks = [matrix[a, :, 0, :] for a in range(na)]
     lines = [line_of(blocks[0])]
     side = across_rows(matrix[:na, :, fwd:, :].transpose(0, 2, 1, 3))
+    side = side + [swap_core(x) for x in side]
     strips = []
     for a in range(na):
         if a:
-            lines.append(line_of(blocks[a], side[1]))
+            lines.append(line_of(blocks[a], side[rows_dev // 2]))
         line = jnp.stack(lines[a])
         strips.append(jnp.concatenate([line, step_to(line, "col", cols_dev, n_low, 0, 1)]))
     body = line_of(matrix[na:, :, 0, :].reshape(-1, nb), strips[0])
-    side = side + [swap_core(x) for x in side]
     body_far = step_to(tie(body[0], strips[0]), "col", cols_dev, n_low, 0, 1)
     phases = []
     for a in range(na):

time: 106 us -> 99.9 us (0.942); the launches traced: 106 us -> 98.4 us
  waiting for transfers between devices: 26.8 us -> 17.3 us
  starting transfers between devices: 20.2 us -> 22.3 us
    ppermute x22, waiting for transfers between devices: 26.8 us -> 17.3 us  [step_to(): return lax.ppermute(x, axis, pairs)]
    ppermute x22, starting transfers between devices: 20.2 us -> 22.3 us  [step_to(): return lax.ppermute(x, axis, pairs)]
  transfers between devices with their start and end apart: 22 -> 22, of which waited for: 12 -> 10; matrix products, arithmetic and copies ran while one was open for 5% -> 5% of each run, Pallas kernels for 43% -> 46%
where the time goes in v6:
time: 99.9 us; the launch traced here: 98.4 us
  Pallas kernels  52.1 us (52%)
  starting transfers between devices  22.3 us (22%)
  waiting for transfers between devices  17.3 us (17%)
  local copies, waits for them, and re-layouts  5.35 us (5%)
  other arithmetic  1.09 us (1%)
    pallas_call x2, Pallas kernels, local(): pl.pallas_call(functools.partial(sweep_kernel, phase=phase, last=last, nb...  45.2 us
    ppermute x22, starting transfers between devices, step_to(): return lax.ppermute(x, axis, pairs)  22.3 us
    ppermute x22, waiting for transfers between devices, step_to(): return lax.ppermute(x, axis, pairs)  17.3 us
    pallas_call x1, Pallas kernels, local(): pl.pallas_call(functools.partial(close_kernel, nb=nb, na=na, block_rows=b...  6.87 us
    unnamed x11, local copies, waits for them, and re-layouts  2.59 us
  transfers between devices with their start and end apart: 22, of which 10 were waited for; matrix products, arithmetic and copies ran while one was open for 5% of the time, Pallas kernels for 46%

profile of v6, /device:TPU:8, one launch (start us, length us, event | category | flops | bytes accessed | tf_op | source)
XLA Modules:
  0.0 98.4 jit_solution(9767243242514162616)
XLA Ops:
  0.0 1.3 %fusion = (f32[1,128,1,128]{3,2,1,0:T(1,128)S(1)}, f32[1,128,1,128]{3,2,1,0:T(1,128)S(1)}) fusion(f32[8,128,4,128]{3,2,1,0:T(4,128)} %param.1), kind=kLoop, calls=%fused_computation.15 | loop fusion | bytes 262144 | tf_op jit(solution)/shard_map/slice | solution.py:394
  1.3 1.6 %collective-permute-start = (f32[128,128]{1,0:T(8,128)S(1)}, f32[128,128]{1,0:T(8,128)}, u32[]{:S(2)}, u32[]{:S(2)}) collective-permute-start(f32[128,128]{1,0:T(8,128)S(1)} %bitcast.51), channel_id=1, source_target_pairs={{0,2},{1,3},{2,4},{3,5},{4,6},{5,7},{6,0},{7,1},{8,10},{9,11},{10,... | collective-permute-start | bytes 196616 | tf_op jit(solution)/shard_map/ppermute | solution.py:381
  4.0 1.9 %collective-permute-start.2 = (f32[128,128]{1,0:T(8,128)S(1)}, f32[128,128]{1,0:T(8,128)}, u32[]{:S(2)}, u32[]{:S(2)}) collective-permute-start(f32[128,128]{1,0:T(8,128)S(1)} %bitcast.53), channel_id=1, source_target_pairs={{0,6},{1,7},{2,0},{3,1},{4,2},{5,3},{6,4},{7,5},{8,14},{9,15},{10,... | collective-permute-start | bytes 196616 | tf_op jit(solution)/shard_map/ppermute | solution.py:381
  5.9 1.2 %slice.14 = f32[2,128,3,128]{3,2,1,0:T(4,128)S(1)} slice(f32[8,128,4,128]{3,2,1,0:T(4,128)} %param.1), slice={[0:2], [0:128], [1:4], [0:128]} | slice | bytes 786432 | tf_op jit(solution)/shard_map/slice | solution.py:396
  7.2 1.6 %collective-permute-start.11 = (f32[2,3,128,128]{3,2,1,0:T(8,128)S(1)}, f32[2,3,128,128]{3,2,1,0:T(8,128)}, u32[]{:S(2)}, u32[]{:S(2)}) collective-permute-start(f32[2,3,128,128]{3,2,1,0:T(8,128)S(1)} %bitcast.43), channel_id=1, source_target_pairs={{0,16},{8,24},{16,0},{24,8},{1,17},{9,25},{17,1},{25,9},{2,18},{10... | collective-permute-start | bytes 1179656 | tf_op jit(solution)/shard_map/ppermute | solution.py:381
  9.2 1.2 %collective-permute-done.2 = f32[128,128]{1,0:T(8,128)} collective-permute-done((f32[128,128]{1,0:T(8,128)S(1)}, f32[128,128]{1,0:T(8,128)}, u32[]{:S(2)}, u32[]{:S(2)}) %collective-permute-start.2) | collective-permute-done | bytes 65568 | tf_op jit(solution)/shard_map/ppermute | solution.py:381
  11.3 1.6 %collective-permute-start.3 = (f32[4,128,128]{2,1,0:T(8,128)S(1)}, f32[4,128,128]{2,1,0:T(8,128)S(1)}, u32[]{:S(2)}, u32[]{:S(2)}) collective-permute-start(f32[4,128,128]{2,1,0:T(8,128)S(1)} %pad_maximum_fusion.1), channel_id=1, source_target_pairs={{0,1},{1,0},{2,3},{3,2},{4,5},{5,4},{6,7},{7,6},{8,9},{9,8},{10,11... | collective-permute-start | bytes 786440 | tf_op jit(solution)/shard_map/ppermute | solution.py:381
  15.4 4.1 %collective-permute-done.3 = f32[4,128,128]{2,1,0:T(8,128)S(1)} collective-permute-done((f32[4,128,128]{2,1,0:T(8,128)S(1)}, f32[4,128,128]{2,1,0:T(8,128)S(1)}, u32[]{:S(2)}, u32[]{:S(2)}) %collective-permute-start.3) | collective-permute-done | bytes 262176 | tf_op jit(solution)/shard_map/ppermute | solution.py:381
  19.5 1.3 %collective-permute-start.8 = (f32[8,128,128]{2,1,0:T(8,128)S(1)}, f32[8,128,128]{2,1,0:T(8,128)S(1)}, u32[]{:S(2)}, u32[]{:S(2)}) collective-permute-start(f32[8,128,128]{2,1,0:T(8,128)S(1)} %constant_dynamic-update-slice_fusion.refs_1_), channel_id=1, source_target_pairs={{0,16},{8,24},{16,0},{24,8},{1,17},{9,25},{17,1},{25,9},{2,18},{10... | collective-permute-start | bytes 1572872 | tf_op jit(solution)/shard_map/ppermute | solution.py:381
  20.8 2.1 %collective-permute-start.16 = (f32[128,128]{1,0:T(8,128)S(1)}, f32[128,128]{1,0:T(8,128)S(1)}, u32[]{:S(2)}, u32[]{:S(2)}) collective-permute-start(f32[128,128]{1,0:T(8,128)S(1)} %bitcast.47), channel_id=1, source_target_pairs={{0,4},{1,5},{2,6},{3,7},{4,0},{5,1},{6,2},{7,3},{8,12},{9,13},{10,... | collective-permute-start | bytes 196616 | tf_op jit(solution)/shard_map/ppermute | solution.py:381
  23.5 2.0 %collective-permute-done.15 = f32[128,128]{1,0:T(8,128)S(1)} collective-permute-done((f32[128,128]{1,0:T(8,128)S(1)}, f32[128,128]{1,0:T(8,128)S(1)}, u32[]{:S(2)}, u32[]{:S(2)}) %collective-permute-start.15) | collective-permute-done | bytes 65568 | tf_op jit(solution)/shard_map/ppermute | solution.py:381
  25.5 1.2 %collective-permute-start.4 = (f32[768,128]{1,0:T(8,128)S(1)}, f32[768,128]{1,0:T(8,128)S(1)}, u32[]{:S(2)}, u32[]{:S(2)}) collective-permute-start(f32[768,128]{1,0:T(8,128)S(1)} %bitcast.37), channel_id=1, source_target_pairs={{0,2},{1,3},{2,4},{3,5},{4,6},{5,7},{6,0},{7,1},{8,10},{9,11},{10,... | collective-permute-start | bytes 1179656 | tf_op jit(solution)/shard_map/ppermute | solution.py:381
  26.7 1.2 %collective-permute-done.17 = f32[128,128]{1,0:T(8,128)S(1)} collective-permute-done((f32[128,128]{1,0:T(8,128)S(1)}, f32[128,128]{1,0:T(8,128)S(1)}, u32[]{:S(2)}, u32[]{:S(2)}) %collective-permute-start.17) | collective-permute-done | bytes 65568 | tf_op jit(solution)/shard_map/ppermute | solution.py:381
  27.9 1.6 %collective-permute-start.18 = (f32[4,128,128]{2,1,0:T(8,128)S(1)}, f32[4,128,128]{2,1,0:T(8,128)S(1)}, u32[]{:S(2)}, u32[]{:S(2)}) collective-permute-start(f32[4,128,128]{2,1,0:T(8,128)S(1)} %pad_maximum_fusion.2), channel_id=1, source_target_pairs={{0,1},{1,0},{2,3},{3,2},{4,5},{5,4},{6,7},{7,6},{8,9},{9,8},{10,11... | collective-permute-start | bytes 786440 | tf_op jit(solution)/shard_map/ppermute | solution.py:381
  29.5 3.1 %collective-permute-done.8.refs_2_ = f32[8,128,128]{2,1,0:T(8,128)S(1)} collective-permute-done((f32[8,128,128]{2,1,0:T(8,128)S(1)}, f32[8,128,128]{2,1,0:T(8,128)S(1)}, u32[]{:S(2)}, u32[]{:S(2)}) %collective-permute-start.8) | collective-permute-done | bytes 524320 | tf_op jit(solution)/shard_map/ppermute | solution.py:381
  32.6 2.9 %collective-permute-done.18 = f32[4,128,128]{2,1,0:T(8,128)S(1)} collective-permute-done((f32[4,128,128]{2,1,0:T(8,128)S(1)}, f32[4,128,128]{2,1,0:T(8,128)S(1)}, u32[]{:S(2)}, u32[]{:S(2)}) %collective-permute-start.18) | collective-permute-done | bytes 262176 | tf_op jit(solution)/shard_map/ppermute | solution.py:381
  35.5 2.9 %collective-permute-start.5 = (f32[768,128]{1,0:T(8,128)S(1)}, f32[768,128]{1,0:T(8,128)S(1)}, u32[]{:S(2)}, u32[]{:S(2)}) collective-permute-start(f32[768,128]{1,0:T(8,128)S(1)} %bitcast.38), channel_id=1, source_target_pairs={{0,4},{1,5},{2,6},{3,7},{4,0},{5,1},{6,2},{7,3},{8,12},{9,13},{10,... | collective-permute-start | bytes 1179656 | tf_op jit(solution)/shard_map/ppermute | solution.py:381
  38.4 1.6 %collective-permute-start.7 = (f32[768,128]{1,0:T(8,128)S(1)}, f32[768,128]{1,0:T(8,128)S(1)}, u32[]{:S(2)}, u32[]{:S(2)}) collective-permute-start(f32[768,128]{1,0:T(8,128)S(1)} %bitcast.40), channel_id=1, source_target_pairs={{0,1},{1,0},{2,3},{3,2},{4,5},{5,4},{6,7},{7,6},{8,9},{9,8},{10,11... | collective-permute-start | bytes 1179656 | tf_op jit(solution)/shard_map/ppermute | solution.py:381
  40.1 1.1 %collective-permute-start.19 = (f32[8,128,128]{2,1,0:T(8,128)S(1)}, f32[8,128,128]{2,1,0:T(8,128)S(1)}, u32[]{:S(2)}, u32[]{:S(2)}) collective-permute-start(f32[8,128,128]{2,1,0:T(8,128)S(1)} %constant_dynamic-update-slice_fusion.5.refs_1_), channel_id=1, source_target_pairs={{0,16},{8,24},{16,0},{24,8},{1,17},{9,25},{17,1},{25,9},{2,18},{10... | collective-permute-start | bytes 1572872 | tf_op jit(solution)/shard_map/ppermute | solution.py:381
  41.2 21.8 %sweep0.1 = (f32[512,896]{1,0:T(8,128)S(1)}, f32[512,128]{1,0:T(8,128)S(1)}, f32[2,128,128]{2,1,0:T(8,128)S(1)}) custom-call(s32[2]{0:T(128)S(1)} %pad_add_fusion.refs_0_.place, f32[8,128,128]{2,1,0:T(8,128)S(1)} %constant_dynamic-update-slice_fusion.refs_1_, f32[8,128,128]{2,1,0:T(8,128)S(1)} %collective-permute-done.8.refs_2_, ...), custom_call_target="tpu_custom_call" | custom-call | flops 3000000000 | bytes 10000000 | tf_op jit(solution)/shard_map/sweep0/pallas_call | solution.py:429
  63.4 1.6 %collective-permute-start.14 = (f32[3,768,128]{2,1,0:T(8,128)S(1)}, f32[3,768,128]{2,1,0:T(8,128)S(1)}, u32[]{:S(2)}, u32[]{:S(2)}) collective-permute-start(f32[3,768,128]{2,1,0:T(8,128)S(1)} %pad_maximum_fusion), channel_id=1, source_target_pairs={{0,1},{1,0},{2,3},{3,2},{4,5},{5,4},{6,7},{7,6},{8,9},{9,8},{10,11... | collective-permute-start | bytes 3538952 | tf_op jit(solution)/shard_map/ppermute | solution.py:381
  65.5 1.4 %collective-permute-done.20.refs_3_ = f32[8,128,128]{2,1,0:T(8,128)S(1)} collective-permute-done((f32[8,128,128]{2,1,0:T(8,128)S(1)}, f32[8,128,128]{2,1,0:T(8,128)S(1)}, u32[]{:S(2)}, u32[]{:S(2)}) %collective-permute-start.20) | collective-permute-done | bytes 524320 | tf_op jit(solution)/shard_map/ppermute | solution.py:381
  67.6 23.3 %sweep1.1 = (bf16[2,1024,512]{2,1,0:T(8,128)(2,1)S(1)}, f32[2,128,128]{2,1,0:T(8,128)S(1)}) custom-call(s32[2]{0:T(128)S(1)} %pad_add_fusion.refs_0_.place, f32[8,128,128]{2,1,0:T(8,128)S(1)} %constant_dynamic-update-slice_fusion.5.refs_1_, f32[8,128,128]{2,1,0:T(8,128)S(1)} %collective-permute-done.19.refs_2_, ...), custom_call_target="tpu_custom_call" | custom-call | flops 3000000000 | bytes 10000000 | tf_op jit(solution)/shard_map/sweep1/pallas_call | solution.py:429
  91.4 6.9 %close.1 = f32[4096,128]{1,0:T(8,128)} custom-call(s32[2]{0:T(128)S(1)} %pad_add_fusion.refs_0_.place, f32[768,128]{1,0:T(8,128)S(1)} %bitcast.41, f32[768,128]{1,0:T(8,128)S(1)} %collective-permute-done.4.refs_1_, f32[768,128]{1,0:T(8,128)S(1)} %collective-permute-done.5.refs_2_, f32[768,128]{1,0:T(8,128)S(1)} %collective-permute-done.6.refs_3_, ...), custom_call_target="tpu_custom_call" | custom-call | tf_op jit(solution)/shard_map/close/pallas_call | solution.py:466
  (43 shorter events, 7.6 us)
Async XLA Ops:
  0.0 8.8 %copy-start = (f32[8,128,4,128]{3,2,1,0:T(4,128)S(1)}, f32[8,128,4,128]{3,2,1,0:T(4,128)}, u32[]{:S(2)}) copy-start(f32[8,128,4,128]{3,2,1,0:T(4,128)} %param.1) | copy-start | bytes 6291460
  1.3 7.9 %collective-permute-start = (f32[128,128]{1,0:T(8,128)S(1)}, f32[128,128]{1,0:T(8,128)}, u32[]{:S(2)}, u32[]{:S(2)}) collective-permute-start(f32[128,128]{1,0:T(8,128)S(1)} %bitcast.51), channel_id=1, source_target_pairs={{0,2},{1,3},{2,4},{3,5},{4,6},{5,7},{6,0},{7,1},{8,10},{9,11},{10,... | collective-permute-start | bytes 196616 | tf_op jit(solution)/shard_map/ppermute | solution.py:381
  2.9 6.3 %collective-permute-start.1 = (f32[128,128]{1,0:T(8,128)S(1)}, f32[128,128]{1,0:T(8,128)}, u32[]{:S(2)}, u32[]{:S(2)}) collective-permute-start(f32[128,128]{1,0:T(8,128)S(1)} %bitcast.52), channel_id=1, source_target_pairs={{0,4},{1,5},{2,6},{3,7},{4,0},{5,1},{6,2},{7,3},{8,12},{9,13},{10,... | collective-permute-start | bytes 196616 | tf_op jit(solution)/shard_map/ppermute | solution.py:381
  4.0 6.3 %collective-permute-start.2 = (f32[128,128]{1,0:T(8,128)S(1)}, f32[128,128]{1,0:T(8,128)}, u32[]{:S(2)}, u32[]{:S(2)}) collective-permute-start(f32[128,128]{1,0:T(8,128)S(1)} %bitcast.53), channel_id=1, source_target_pairs={{0,6},{1,7},{2,0},{3,1},{4,2},{5,3},{6,4},{7,5},{8,14},{9,15},{10,... | collective-permute-start | bytes 196616 | tf_op jit(solution)/shard_map/ppermute | solution.py:381
  7.2 13.6 %collective-permute-start.12 = (f32[2,3,128,128]{3,2,1,0:T(8,128)S(1)}, f32[2,3,128,128]{3,2,1,0:T(8,128)}, u32[]{:S(2)}, u32[]{:S(2)}) collective-permute-start(f32[2,3,128,128]{3,2,1,0:T(8,128)S(1)} %bitcast.42), channel_id=1, source_target_pairs={{0,8},{8,0},{16,24},{24,16},{1,9},{9,1},{17,25},{25,17},{2,10},{10... | collective-permute-start | bytes 1179656 | tf_op jit(solution)/shard_map/ppermute | solution.py:381
  7.2 16.1 %collective-permute-start.11 = (f32[2,3,128,128]{3,2,1,0:T(8,128)S(1)}, f32[2,3,128,128]{3,2,1,0:T(8,128)}, u32[]{:S(2)}, u32[]{:S(2)}) collective-permute-start(f32[2,3,128,128]{3,2,1,0:T(8,128)S(1)} %bitcast.43), channel_id=1, source_target_pairs={{0,16},{8,24},{16,0},{24,8},{1,17},{9,25},{17,1},{25,9},{2,18},{10... | collective-permute-start | bytes 1179656 | tf_op jit(solution)/shard_map/ppermute | solution.py:381
  11.3 8.2 %collective-permute-start.3 = (f32[4,128,128]{2,1,0:T(8,128)S(1)}, f32[4,128,128]{2,1,0:T(8,128)S(1)}, u32[]{:S(2)}, u32[]{:S(2)}) collective-permute-start(f32[4,128,128]{2,1,0:T(8,128)S(1)} %pad_maximum_fusion.1), channel_id=1, source_target_pairs={{0,1},{1,0},{2,3},{3,2},{4,5},{5,4},{6,7},{7,6},{8,9},{9,8},{10,11... | collective-permute-start | bytes 786440 | tf_op jit(solution)/shard_map/ppermute | solution.py:381
  19.5 13.1 %collective-permute-start.8 = (f32[8,128,128]{2,1,0:T(8,128)S(1)}, f32[8,128,128]{2,1,0:T(8,128)S(1)}, u32[]{:S(2)}, u32[]{:S(2)}) collective-permute-start(f32[8,128,128]{2,1,0:T(8,128)S(1)} %constant_dynamic-update-slice_fusion.refs_1_), channel_id=1, source_target_pairs={{0,16},{8,24},{16,0},{24,8},{1,17},{9,25},{17,1},{25,9},{2,18},{10... | collective-permute-start | bytes 1572872 | tf_op jit(solution)/shard_map/ppermute | solution.py:381
  20.8 4.7 %collective-permute-start.15 = (f32[128,128]{1,0:T(8,128)S(1)}, f32[128,128]{1,0:T(8,128)S(1)}, u32[]{:S(2)}, u32[]{:S(2)}) collective-permute-start(f32[128,128]{1,0:T(8,128)S(1)} %bitcast.46), channel_id=1, source_target_pairs={{0,2},{1,3},{2,4},{3,5},{4,6},{5,7},{6,0},{7,1},{8,10},{9,11},{10,... | collective-permute-start | bytes 196616 | tf_op jit(solution)/shard_map/ppermute | solution.py:381
  20.8 5.9 %collective-permute-start.16 = (f32[128,128]{1,0:T(8,128)S(1)}, f32[128,128]{1,0:T(8,128)S(1)}, u32[]{:S(2)}, u32[]{:S(2)}) collective-permute-start(f32[128,128]{1,0:T(8,128)S(1)} %bitcast.47), channel_id=1, source_target_pairs={{0,4},{1,5},{2,6},{3,7},{4,0},{5,1},{6,2},{7,3},{8,12},{9,13},{10,... | collective-permute-start | bytes 196616 | tf_op jit(solution)/shard_map/ppermute | solution.py:381
  22.9 5.0 %collective-permute-start.17 = (f32[128,128]{1,0:T(8,128)S(1)}, f32[128,128]{1,0:T(8,128)S(1)}, u32[]{:S(2)}, u32[]{:S(2)}) collective-permute-start(f32[128,128]{1,0:T(8,128)S(1)} %bitcast.48), channel_id=1, source_target_pairs={{0,6},{1,7},{2,0},{3,1},{4,2},{5,3},{6,4},{7,5},{8,14},{9,15},{10,... | collective-permute-start | bytes 196616 | tf_op jit(solution)/shard_map/ppermute | solution.py:381
  23.4 15.0 %collective-permute-start.9 = (f32[8,128,128]{2,1,0:T(8,128)S(1)}, f32[8,128,128]{2,1,0:T(8,128)S(1)}, u32[]{:S(2)}, u32[]{:S(2)}) collective-permute-start(f32[8,128,128]{2,1,0:T(8,128)S(1)} %constant_dynamic-update-slice_fusion.refs_1_), channel_id=1, source_target_pairs={{0,8},{8,0},{16,24},{24,16},{1,9},{9,1},{17,25},{25,17},{2,10},{10... | collective-permute-start | bytes 1572872 | tf_op jit(solution)/shard_map/ppermute | solution.py:381
  25.5 37.6 %collective-permute-start.4 = (f32[768,128]{1,0:T(8,128)S(1)}, f32[768,128]{1,0:T(8,128)S(1)}, u32[]{:S(2)}, u32[]{:S(2)}) collective-permute-start(f32[768,128]{1,0:T(8,128)S(1)} %bitcast.37), channel_id=1, source_target_pairs={{0,2},{1,3},{2,4},{3,5},{4,6},{5,7},{6,0},{7,1},{8,10},{9,11},{10,... | collective-permute-start | bytes 1179656 | tf_op jit(solution)/shard_map/ppermute | solution.py:381
  26.7 11.7 %collective-permute-start.13 = (f32[2,3,128,128]{3,2,1,0:T(8,128)}, f32[2,3,128,128]{3,2,1,0:T(8,128)S(1)}, u32[]{:S(2)}, u32[]{:S(2)}) collective-permute-start(f32[2,3,128,128]{3,2,1,0:T(8,128)} %collective-permute-done.11.refs_6_), channel_id=1, source_target_pairs={{0,8},{8,0},{16,24},{24,16},{1,9},{9,1},{17,25},{25,17},{2,10},{10... | collective-permute-start | bytes 1179656 | tf_op jit(solution)/shard_map/ppermute | solution.py:381
  27.9 7.6 %collective-permute-start.18 = (f32[4,128,128]{2,1,0:T(8,128)S(1)}, f32[4,128,128]{2,1,0:T(8,128)S(1)}, u32[]{:S(2)}, u32[]{:S(2)}) collective-permute-start(f32[4,128,128]{2,1,0:T(8,128)S(1)} %pad_maximum_fusion.2), channel_id=1, source_target_pairs={{0,1},{1,0},{2,3},{3,2},{4,5},{5,4},{6,7},{7,6},{8,9},{9,8},{10,11... | collective-permute-start | bytes 786440 | tf_op jit(solution)/shard_map/ppermute | solution.py:381
  32.6 7.4 %collective-permute-start.10 = (f32[8,128,128]{2,1,0:T(8,128)S(1)}, f32[8,128,128]{2,1,0:T(8,128)S(1)}, u32[]{:S(2)}, u32[]{:S(2)}) collective-permute-start(f32[8,128,128]{2,1,0:T(8,128)S(1)} %collective-permute-done.8.refs_2_), channel_id=1, source_target_pairs={{0,8},{8,0},{16,24},{24,16},{1,9},{9,1},{17,25},{25,17},{2,10},{10... | collective-permute-start | bytes 1572872 | tf_op jit(solution)/shard_map/ppermute | solution.py:381
  35.5 27.5 %collective-permute-start.5 = (f32[768,128]{1,0:T(8,128)S(1)}, f32[768,128]{1,0:T(8,128)S(1)}, u32[]{:S(2)}, u32[]{:S(2)}) collective-permute-start(f32[768,128]{1,0:T(8,128)S(1)} %bitcast.38), channel_id=1, source_target_pairs={{0,4},{1,5},{2,6},{3,7},{4,0},{5,1},{6,2},{7,3},{8,12},{9,13},{10,... | collective-permute-start | bytes 1179656 | tf_op jit(solution)/shard_map/ppermute | solution.py:381
  38.4 24.9 %collective-permute-start.6 = (f32[768,128]{1,0:T(8,128)S(1)}, f32[768,128]{1,0:T(8,128)S(1)}, u32[]{:S(2)}, u32[]{:S(2)}) collective-permute-start(f32[768,128]{1,0:T(8,128)S(1)} %bitcast.39), channel_id=1, source_target_pairs={{0,6},{1,7},{2,0},{3,1},{4,2},{5,3},{6,4},{7,5},{8,14},{9,15},{10,... | collective-permute-start | bytes 1179656 | tf_op jit(solution)/shard_map/ppermute | solution.py:381
  38.4 24.6 %collective-permute-start.7 = (f32[768,128]{1,0:T(8,128)S(1)}, f32[768,128]{1,0:T(8,128)S(1)}, u32[]{:S(2)}, u32[]{:S(2)}) collective-permute-start(f32[768,128]{1,0:T(8,128)S(1)} %bitcast.40), channel_id=1, source_target_pairs={{0,1},{1,0},{2,3},{3,2},{4,5},{5,4},{6,7},{7,6},{8,9},{9,8},{10,11... | collective-permute-start | bytes 1179656 | tf_op jit(solution)/shard_map/ppermute | solution.py:381
  40.1 24.9 %collective-permute-start.19 = (f32[8,128,128]{2,1,0:T(8,128)S(1)}, f32[8,128,128]{2,1,0:T(8,128)S(1)}, u32[]{:S(2)}, u32[]{:S(2)}) collective-permute-start(f32[8,128,128]{2,1,0:T(8,128)S(1)} %constant_dynamic-update-slice_fusion.5.refs_1_), channel_id=1, source_target_pairs={{0,16},{8,24},{16,0},{24,8},{1,17},{9,25},{17,1},{25,9},{2,18},{10... | collective-permute-start | bytes 1572872 | tf_op jit(solution)/shard_map/ppermute | solution.py:381
  63.4 28.0 %collective-permute-start.14 = (f32[3,768,128]{2,1,0:T(8,128)S(1)}, f32[3,768,128]{2,1,0:T(8,128)S(1)}, u32[]{:S(2)}, u32[]{:S(2)}) collective-permute-start(f32[3,768,128]{2,1,0:T(8,128)S(1)} %pad_maximum_fusion), channel_id=1, source_target_pairs={{0,1},{1,0},{2,3},{3,2},{4,5},{5,4},{6,7},{7,6},{8,9},{9,8},{10,11... | collective-permute-start | bytes 3538952 | tf_op jit(solution)/shard_map/ppermute | solution.py:381
  65.0 1.9 %collective-permute-start.20 = (f32[8,128,128]{2,1,0:T(8,128)S(1)}, f32[8,128,128]{2,1,0:T(8,128)S(1)}, u32[]{:S(2)}, u32[]{:S(2)}) collective-permute-start(f32[8,128,128]{2,1,0:T(8,128)S(1)} %constant_dynamic-update-slice_fusion.5.refs_1_), channel_id=1, source_target_pairs={{0,8},{8,0},{16,24},{24,16},{1,9},{9,1},{17,25},{25,17},{2,10},{10... | collective-permute-start | bytes 1572872 | tf_op jit(solution)/shard_map/ppermute | solution.py:381
  65.0 2.7 %collective-permute-start.21 = (f32[8,128,128]{2,1,0:T(8,128)S(1)}, f32[8,128,128]{2,1,0:T(8,128)S(1)}, u32[]{:S(2)}, u32[]{:S(2)}) collective-permute-start(f32[8,128,128]{2,1,0:T(8,128)S(1)} %collective-permute-done.19.refs_2_), channel_id=1, source_target_pairs={{0,8},{8,0},{16,24},{24,16},{1,9},{9,1},{17,25},{25,17},{2,10},{10... | collective-permute-start | bytes 1572872 | tf_op jit(solution)/shard_map/ppermute | solution.py:381

commit v7 on v6

--- a/solution.py
+++ b/solution.py
@@ -8,7 +8,7 @@
 from jax.sharding import PartitionSpec as P
 
 STEPS = 8
-PANEL = 64
+PANELS = (64, 32)
 SUB = 8
 F32 = jnp.float32
 BF16 = jnp.bfloat16
@@ -43,12 +43,12 @@
     return contract(lh, rh, dims) + (contract(lh, rm, dims) + contract(lm, rh, dims))
 
 
-def factor_tile(tile, nb, filler):
+def factor_tile(tile, nb, panel, filler):
     lane = lax.broadcasted_iota(jnp.int32, (SUB, nb), 1)
     sub = lax.broadcasted_iota(jnp.int32, (SUB, nb), 0)
-    count = PANEL // SUB
-    for first in range(0, nb, PANEL):
-        after = first + PANEL
+    count = panel // SUB
+    for first in range(0, nb, panel):
+        after = first + panel
         parts = [tile[first + SUB * v : first + SUB * v + SUB, :] for v in range(count)]
         for b in range(count):
             at = first + SUB * b
@@ -208,7 +208,7 @@
     def step(k, here, filler):
         base = k * nb
         origin[...] = tile[...]
-        factor_tile(tile, nb, filler)
+        factor_tile(tile, nb, PANELS[min(phase, 1)], filler)
         held[...] = jnp.where(ii >= jj, tile[...], 0.0)
 
         @pl.when(k == my_col)

time: 99.9 us -> 99.9 us (level)
  no operation moved by 1% of the time
where the time goes in v7:
time: 99.9 us; the launch traced here: 98.4 us
  Pallas kernels  52.1 us (52%)
  starting transfers between devices  22.3 us (22%)
  waiting for transfers between devices  17.2 us (17%)
  local copies, waits for them, and re-layouts  5.35 us (5%)
  other arithmetic  1.09 us (1%)
    pallas_call x2, Pallas kernels, local(): pl.pallas_call(functools.partial(sweep_kernel, phase=phase, last=last, nb...  45.2 us
    ppermute x22, starting transfers between devices, step_to(): return lax.ppermute(x, axis, pairs)  22.3 us
    ppermute x22, waiting for transfers between devices, step_to(): return lax.ppermute(x, axis, pairs)  17.2 us
    pallas_call x1, Pallas kernels, local(): pl.pallas_call(functools.partial(close_kernel, nb=nb, na=na, block_rows=b...  6.87 us
    unnamed x11, local copies, waits for them, and re-layouts  2.59 us
  transfers between devices with their start and end apart: 22, of which 10 were waited for; matrix products, arithmetic and copies ran while one was open for 5% of the time, Pallas kernels for 46%

profile of v7, /device:TPU:8, one launch (start us, length us, event | category | flops | bytes accessed | tf_op | source)
XLA Modules:
  0.0 98.4 jit_solution(13543568977983759644)
XLA Ops:
  0.0 1.3 %fusion = (f32[1,128,1,128]{3,2,1,0:T(1,128)S(1)}, f32[1,128,1,128]{3,2,1,0:T(1,128)S(1)}) fusion(f32[8,128,4,128]{3,2,1,0:T(4,128)} %param.1), kind=kLoop, calls=%fused_computation.15 | loop fusion | bytes 262144 | tf_op jit(solution)/shard_map/slice | solution.py:394
  1.3 1.6 %collective-permute-start = (f32[128,128]{1,0:T(8,128)S(1)}, f32[128,128]{1,0:T(8,128)}, u32[]{:S(2)}, u32[]{:S(2)}) collective-permute-start(f32[128,128]{1,0:T(8,128)S(1)} %bitcast.51), channel_id=1, source_target_pairs={{0,2},{1,3},{2,4},{3,5},{4,6},{5,7},{6,0},{7,1},{8,10},{9,11},{10,... | collective-permute-start | bytes 196616 | tf_op jit(solution)/shard_map/ppermute | solution.py:381
  4.0 1.9 %collective-permute-start.2 = (f32[128,128]{1,0:T(8,128)S(1)}, f32[128,128]{1,0:T(8,128)}, u32[]{:S(2)}, u32[]{:S(2)}) collective-permute-start(f32[128,128]{1,0:T(8,128)S(1)} %bitcast.53), channel_id=1, source_target_pairs={{0,6},{1,7},{2,0},{3,1},{4,2},{5,3},{6,4},{7,5},{8,14},{9,15},{10,... | collective-permute-start | bytes 196616 | tf_op jit(solution)/shard_map/ppermute | solution.py:381
  5.9 1.2 %slice.14 = f32[2,128,3,128]{3,2,1,0:T(4,128)S(1)} slice(f32[8,128,4,128]{3,2,1,0:T(4,128)} %param.1), slice={[0:2], [0:128], [1:4], [0:128]} | slice | bytes 786432 | tf_op jit(solution)/shard_map/slice | solution.py:396
  7.2 1.6 %collective-permute-start.11 = (f32[2,3,128,128]{3,2,1,0:T(8,128)S(1)}, f32[2,3,128,128]{3,2,1,0:T(8,128)}, u32[]{:S(2)}, u32[]{:S(2)}) collective-permute-start(f32[2,3,128,128]{3,2,1,0:T(8,128)S(1)} %bitcast.43), channel_id=1, source_target_pairs={{0,16},{8,24},{16,0},{24,8},{1,17},{9,25},{17,1},{25,9},{2,18},{10... | collective-permute-start | bytes 1179656 | tf_op jit(solution)/shard_map/ppermute | solution.py:381
  9.2 1.2 %collective-permute-done.2 = f32[128,128]{1,0:T(8,128)} collective-permute-done((f32[128,128]{1,0:T(8,128)S(1)}, f32[128,128]{1,0:T(8,128)}, u32[]{:S(2)}, u32[]{:S(2)}) %collective-permute-start.2) | collective-permute-done | bytes 65568 | tf_op jit(solution)/shard_map/ppermute | solution.py:381
  11.3 1.6 %collective-permute-start.3 = (f32[4,128,128]{2,1,0:T(8,128)S(1)}, f32[4,128,128]{2,1,0:T(8,128)S(1)}, u32[]{:S(2)}, u32[]{:S(2)}) collective-permute-start(f32[4,128,128]{2,1,0:T(8,128)S(1)} %pad_maximum_fusion.1), channel_id=1, source_target_pairs={{0,1},{1,0},{2,3},{3,2},{4,5},{5,4},{6,7},{7,6},{8,9},{9,8},{10,11... | collective-permute-start | bytes 786440 | tf_op jit(solution)/shard_map/ppermute | solution.py:381
  15.4 4.1 %collective-permute-done.3 = f32[4,128,128]{2,1,0:T(8,128)S(1)} collective-permute-done((f32[4,128,128]{2,1,0:T(8,128)S(1)}, f32[4,128,128]{2,1,0:T(8,128)S(1)}, u32[]{:S(2)}, u32[]{:S(2)}) %collective-permute-start.3) | collective-permute-done | bytes 262176 | tf_op jit(solution)/shard_map/ppermute | solution.py:381
  19.5 1.3 %collective-permute-start.8 = (f32[8,128,128]{2,1,0:T(8,128)S(1)}, f32[8,128,128]{2,1,0:T(8,128)S(1)}, u32[]{:S(2)}, u32[]{:S(2)}) collective-permute-start(f32[8,128,128]{2,1,0:T(8,128)S(1)} %constant_dynamic-update-slice_fusion.refs_1_), channel_id=1, source_target_pairs={{0,16},{8,24},{16,0},{24,8},{1,17},{9,25},{17,1},{25,9},{2,18},{10... | collective-permute-start | bytes 1572872 | tf_op jit(solution)/shard_map/ppermute | solution.py:381
  20.8 2.1 %collective-permute-start.16 = (f32[128,128]{1,0:T(8,128)S(1)}, f32[128,128]{1,0:T(8,128)S(1)}, u32[]{:S(2)}, u32[]{:S(2)}) collective-permute-start(f32[128,128]{1,0:T(8,128)S(1)} %bitcast.47), channel_id=1, source_target_pairs={{0,4},{1,5},{2,6},{3,7},{4,0},{5,1},{6,2},{7,3},{8,12},{9,13},{10,... | collective-permute-start | bytes 196616 | tf_op jit(solution)/shard_map/ppermute | solution.py:381
  23.5 2.0 %collective-permute-done.15 = f32[128,128]{1,0:T(8,128)S(1)} collective-permute-done((f32[128,128]{1,0:T(8,128)S(1)}, f32[128,128]{1,0:T(8,128)S(1)}, u32[]{:S(2)}, u32[]{:S(2)}) %collective-permute-start.15) | collective-permute-done | bytes 65568 | tf_op jit(solution)/shard_map/ppermute | solution.py:381
  25.5 1.2 %collective-permute-start.4 = (f32[768,128]{1,0:T(8,128)S(1)}, f32[768,128]{1,0:T(8,128)S(1)}, u32[]{:S(2)}, u32[]{:S(2)}) collective-permute-start(f32[768,128]{1,0:T(8,128)S(1)} %bitcast.37), channel_id=1, source_target_pairs={{0,2},{1,3},{2,4},{3,5},{4,6},{5,7},{6,0},{7,1},{8,10},{9,11},{10,... | collective-permute-start | bytes 1179656 | tf_op jit(solution)/shard_map/ppermute | solution.py:381
  26.7 1.2 %collective-permute-done.17 = f32[128,128]{1,0:T(8,128)S(1)} collective-permute-done((f32[128,128]{1,0:T(8,128)S(1)}, f32[128,128]{1,0:T(8,128)S(1)}, u32[]{:S(2)}, u32[]{:S(2)}) %collective-permute-start.17) | collective-permute-done | bytes 65568 | tf_op jit(solution)/shard_map/ppermute | solution.py:381
  27.9 1.6 %collective-permute-start.18 = (f32[4,128,128]{2,1,0:T(8,128)S(1)}, f32[4,128,128]{2,1,0:T(8,128)S(1)}, u32[]{:S(2)}, u32[]{:S(2)}) collective-permute-start(f32[4,128,128]{2,1,0:T(8,128)S(1)} %pad_maximum_fusion.2), channel_id=1, source_target_pairs={{0,1},{1,0},{2,3},{3,2},{4,5},{5,4},{6,7},{7,6},{8,9},{9,8},{10,11... | collective-permute-start | bytes 786440 | tf_op jit(solution)/shard_map/ppermute | solution.py:381
  29.5 3.1 %collective-permute-done.8.refs_2_ = f32[8,128,128]{2,1,0:T(8,128)S(1)} collective-permute-done((f32[8,128,128]{2,1,0:T(8,128)S(1)}, f32[8,128,128]{2,1,0:T(8,128)S(1)}, u32[]{:S(2)}, u32[]{:S(2)}) %collective-permute-start.8) | collective-permute-done | bytes 524320 | tf_op jit(solution)/shard_map/ppermute | solution.py:381
  32.6 2.9 %collective-permute-done.18 = f32[4,128,128]{2,1,0:T(8,128)S(1)} collective-permute-done((f32[4,128,128]{2,1,0:T(8,128)S(1)}, f32[4,128,128]{2,1,0:T(8,128)S(1)}, u32[]{:S(2)}, u32[]{:S(2)}) %collective-permute-start.18) | collective-permute-done | bytes 262176 | tf_op jit(solution)/shard_map/ppermute | solution.py:381
  35.5 2.9 %collective-permute-start.5 = (f32[768,128]{1,0:T(8,128)S(1)}, f32[768,128]{1,0:T(8,128)S(1)}, u32[]{:S(2)}, u32[]{:S(2)}) collective-permute-start(f32[768,128]{1,0:T(8,128)S(1)} %bitcast.38), channel_id=1, source_target_pairs={{0,4},{1,5},{2,6},{3,7},{4,0},{5,1},{6,2},{7,3},{8,12},{9,13},{10,... | collective-permute-start | bytes 1179656 | tf_op jit(solution)/shard_map/ppermute | solution.py:381
  38.4 1.6 %collective-permute-start.7 = (f32[768,128]{1,0:T(8,128)S(1)}, f32[768,128]{1,0:T(8,128)S(1)}, u32[]{:S(2)}, u32[]{:S(2)}) collective-permute-start(f32[768,128]{1,0:T(8,128)S(1)} %bitcast.40), channel_id=1, source_target_pairs={{0,1},{1,0},{2,3},{3,2},{4,5},{5,4},{6,7},{7,6},{8,9},{9,8},{10,11... | collective-permute-start | bytes 1179656 | tf_op jit(solution)/shard_map/ppermute | solution.py:381
  40.1 1.1 %collective-permute-start.19 = (f32[8,128,128]{2,1,0:T(8,128)S(1)}, f32[8,128,128]{2,1,0:T(8,128)S(1)}, u32[]{:S(2)}, u32[]{:S(2)}) collective-permute-start(f32[8,128,128]{2,1,0:T(8,128)S(1)} %constant_dynamic-update-slice_fusion.5.refs_1_), channel_id=1, source_target_pairs={{0,16},{8,24},{16,0},{24,8},{1,17},{9,25},{17,1},{25,9},{2,18},{10... | collective-permute-start | bytes 1572872 | tf_op jit(solution)/shard_map/ppermute | solution.py:381
  41.2 21.8 %sweep0.1 = (f32[512,896]{1,0:T(8,128)S(1)}, f32[512,128]{1,0:T(8,128)S(1)}, f32[2,128,128]{2,1,0:T(8,128)S(1)}) custom-call(s32[2]{0:T(128)S(1)} %pad_add_fusion.refs_0_.place, f32[8,128,128]{2,1,0:T(8,128)S(1)} %constant_dynamic-update-slice_fusion.refs_1_, f32[8,128,128]{2,1,0:T(8,128)S(1)} %collective-permute-done.8.refs_2_, ...), custom_call_target="tpu_custom_call" | custom-call | flops 3000000000 | bytes 10000000 | tf_op jit(solution)/shard_map/sweep0/pallas_call | solution.py:429
  63.4 1.6 %collective-permute-start.14 = (f32[3,768,128]{2,1,0:T(8,128)S(1)}, f32[3,768,128]{2,1,0:T(8,128)S(1)}, u32[]{:S(2)}, u32[]{:S(2)}) collective-permute-start(f32[3,768,128]{2,1,0:T(8,128)S(1)} %pad_maximum_fusion), channel_id=1, source_target_pairs={{0,1},{1,0},{2,3},{3,2},{4,5},{5,4},{6,7},{7,6},{8,9},{9,8},{10,11... | collective-permute-start | bytes 3538952 | tf_op jit(solution)/shard_map/ppermute | solution.py:381
  65.5 1.4 %collective-permute-done.20.refs_3_ = f32[8,128,128]{2,1,0:T(8,128)S(1)} collective-permute-done((f32[8,128,128]{2,1,0:T(8,128)S(1)}, f32[8,128,128]{2,1,0:T(8,128)S(1)}, u32[]{:S(2)}, u32[]{:S(2)}) %collective-permute-start.20) | collective-permute-done | bytes 524320 | tf_op jit(solution)/shard_map/ppermute | solution.py:381
  67.6 23.4 %sweep1.1 = (bf16[2,1024,512]{2,1,0:T(8,128)(2,1)S(1)}, f32[2,128,128]{2,1,0:T(8,128)S(1)}) custom-call(s32[2]{0:T(128)S(1)} %pad_add_fusion.refs_0_.place, f32[8,128,128]{2,1,0:T(8,128)S(1)} %constant_dynamic-update-slice_fusion.5.refs_1_, f32[8,128,128]{2,1,0:T(8,128)S(1)} %collective-permute-done.19.refs_2_, ...), custom_call_target="tpu_custom_call" | custom-call | flops 3000000000 | bytes 10000000 | tf_op jit(solution)/shard_map/sweep1/pallas_call | solution.py:429
  91.4 6.9 %close.1 = f32[4096,128]{1,0:T(8,128)} custom-call(s32[2]{0:T(128)S(1)} %pad_add_fusion.refs_0_.place, f32[768,128]{1,0:T(8,128)S(1)} %bitcast.41, f32[768,128]{1,0:T(8,128)S(1)} %collective-permute-done.4.refs_1_, f32[768,128]{1,0:T(8,128)S(1)} %collective-permute-done.5.refs_2_, f32[768,128]{1,0:T(8,128)S(1)} %collective-permute-done.6.refs_3_, ...), custom_call_target="tpu_custom_call" | custom-call | tf_op jit(solution)/shard_map/close/pallas_call | solution.py:466
  (43 shorter events, 7.6 us)
Async XLA Ops:
  0.0 8.8 %copy-start = (f32[8,128,4,128]{3,2,1,0:T(4,128)S(1)}, f32[8,128,4,128]{3,2,1,0:T(4,128)}, u32[]{:S(2)}) copy-start(f32[8,128,4,128]{3,2,1,0:T(4,128)} %param.1) | copy-start | bytes 6291460
  1.3 7.9 %collective-permute-start = (f32[128,128]{1,0:T(8,128)S(1)}, f32[128,128]{1,0:T(8,128)}, u32[]{:S(2)}, u32[]{:S(2)}) collective-permute-start(f32[128,128]{1,0:T(8,128)S(1)} %bitcast.51), channel_id=1, source_target_pairs={{0,2},{1,3},{2,4},{3,5},{4,6},{5,7},{6,0},{7,1},{8,10},{9,11},{10,... | collective-permute-start | bytes 196616 | tf_op jit(solution)/shard_map/ppermute | solution.py:381
  2.9 6.3 %collective-permute-start.1 = (f32[128,128]{1,0:T(8,128)S(1)}, f32[128,128]{1,0:T(8,128)}, u32[]{:S(2)}, u32[]{:S(2)}) collective-permute-start(f32[128,128]{1,0:T(8,128)S(1)} %bitcast.52), channel_id=1, source_target_pairs={{0,4},{1,5},{2,6},{3,7},{4,0},{5,1},{6,2},{7,3},{8,12},{9,13},{10,... | collective-permute-start | bytes 196616 | tf_op jit(solution)/shard_map/ppermute | solution.py:381
  4.0 6.3 %collective-permute-start.2 = (f32[128,128]{1,0:T(8,128)S(1)}, f32[128,128]{1,0:T(8,128)}, u32[]{:S(2)}, u32[]{:S(2)}) collective-permute-start(f32[128,128]{1,0:T(8,128)S(1)} %bitcast.53), channel_id=1, source_target_pairs={{0,6},{1,7},{2,0},{3,1},{4,2},{5,3},{6,4},{7,5},{8,14},{9,15},{10,... | collective-permute-start | bytes 196616 | tf_op jit(solution)/shard_map/ppermute | solution.py:381
  7.2 13.6 %collective-permute-start.12 = (f32[2,3,128,128]{3,2,1,0:T(8,128)S(1)}, f32[2,3,128,128]{3,2,1,0:T(8,128)}, u32[]{:S(2)}, u32[]{:S(2)}) collective-permute-start(f32[2,3,128,128]{3,2,1,0:T(8,128)S(1)} %bitcast.42), channel_id=1, source_target_pairs={{0,8},{8,0},{16,24},{24,16},{1,9},{9,1},{17,25},{25,17},{2,10},{10... | collective-permute-start | bytes 1179656 | tf_op jit(solution)/shard_map/ppermute | solution.py:381
  7.2 16.1 %collective-permute-start.11 = (f32[2,3,128,128]{3,2,1,0:T(8,128)S(1)}, f32[2,3,128,128]{3,2,1,0:T(8,128)}, u32[]{:S(2)}, u32[]{:S(2)}) collective-permute-start(f32[2,3,128,128]{3,2,1,0:T(8,128)S(1)} %bitcast.43), channel_id=1, source_target_pairs={{0,16},{8,24},{16,0},{24,8},{1,17},{9,25},{17,1},{25,9},{2,18},{10... | collective-permute-start | bytes 1179656 | tf_op jit(solution)/shard_map/ppermute | solution.py:381
  11.3 8.2 %collective-permute-start.3 = (f32[4,128,128]{2,1,0:T(8,128)S(1)}, f32[4,128,128]{2,1,0:T(8,128)S(1)}, u32[]{:S(2)}, u32[]{:S(2)}) collective-permute-start(f32[4,128,128]{2,1,0:T(8,128)S(1)} %pad_maximum_fusion.1), channel_id=1, source_target_pairs={{0,1},{1,0},{2,3},{3,2},{4,5},{5,4},{6,7},{7,6},{8,9},{9,8},{10,11... | collective-permute-start | bytes 786440 | tf_op jit(solution)/shard_map/ppermute | solution.py:381
  19.5 13.1 %collective-permute-start.8 = (f32[8,128,128]{2,1,0:T(8,128)S(1)}, f32[8,128,128]{2,1,0:T(8,128)S(1)}, u32[]{:S(2)}, u32[]{:S(2)}) collective-permute-start(f32[8,128,128]{2,1,0:T(8,128)S(1)} %constant_dynamic-update-slice_fusion.refs_1_), channel_id=1, source_target_pairs={{0,16},{8,24},{16,0},{24,8},{1,17},{9,25},{17,1},{25,9},{2,18},{10... | collective-permute-start | bytes 1572872 | tf_op jit(solution)/shard_map/ppermute | solution.py:381
  20.8 4.7 %collective-permute-start.15 = (f32[128,128]{1,0:T(8,128)S(1)}, f32[128,128]{1,0:T(8,128)S(1)}, u32[]{:S(2)}, u32[]{:S(2)}) collective-permute-start(f32[128,128]{1,0:T(8,128)S(1)} %bitcast.46), channel_id=1, source_target_pairs={{0,2},{1,3},{2,4},{3,5},{4,6},{5,7},{6,0},{7,1},{8,10},{9,11},{10,... | collective-permute-start | bytes 196616 | tf_op jit(solution)/shard_map/ppermute | solution.py:381
  20.8 5.9 %collective-permute-start.16 = (f32[128,128]{1,0:T(8,128)S(1)}, f32[128,128]{1,0:T(8,128)S(1)}, u32[]{:S(2)}, u32[]{:S(2)}) collective-permute-start(f32[128,128]{1,0:T(8,128)S(1)} %bitcast.47), channel_id=1, source_target_pairs={{0,4},{1,5},{2,6},{3,7},{4,0},{5,1},{6,2},{7,3},{8,12},{9,13},{10,... | collective-permute-start | bytes 196616 | tf_op jit(solution)/shard_map/ppermute | solution.py:381
  22.9 5.0 %collective-permute-start.17 = (f32[128,128]{1,0:T(8,128)S(1)}, f32[128,128]{1,0:T(8,128)S(1)}, u32[]{:S(2)}, u32[]{:S(2)}) collective-permute-start(f32[128,128]{1,0:T(8,128)S(1)} %bitcast.48), channel_id=1, source_target_pairs={{0,6},{1,7},{2,0},{3,1},{4,2},{5,3},{6,4},{7,5},{8,14},{9,15},{10,... | collective-permute-start | bytes 196616 | tf_op jit(solution)/shard_map/ppermute | solution.py:381
  23.4 15.0 %collective-permute-start.9 = (f32[8,128,128]{2,1,0:T(8,128)S(1)}, f32[8,128,128]{2,1,0:T(8,128)S(1)}, u32[]{:S(2)}, u32[]{:S(2)}) collective-permute-start(f32[8,128,128]{2,1,0:T(8,128)S(1)} %constant_dynamic-update-slice_fusion.refs_1_), channel_id=1, source_target_pairs={{0,8},{8,0},{16,24},{24,16},{1,9},{9,1},{17,25},{25,17},{2,10},{10... | collective-permute-start | bytes 1572872 | tf_op jit(solution)/shard_map/ppermute | solution.py:381
  25.5 37.6 %collective-permute-start.4 = (f32[768,128]{1,0:T(8,128)S(1)}, f32[768,128]{1,0:T(8,128)S(1)}, u32[]{:S(2)}, u32[]{:S(2)}) collective-permute-start(f32[768,128]{1,0:T(8,128)S(1)} %bitcast.37), channel_id=1, source_target_pairs={{0,2},{1,3},{2,4},{3,5},{4,6},{5,7},{6,0},{7,1},{8,10},{9,11},{10,... | collective-permute-start | bytes 1179656 | tf_op jit(solution)/shard_map/ppermute | solution.py:381
  26.7 11.7 %collective-permute-start.13 = (f32[2,3,128,128]{3,2,1,0:T(8,128)}, f32[2,3,128,128]{3,2,1,0:T(8,128)S(1)}, u32[]{:S(2)}, u32[]{:S(2)}) collective-permute-start(f32[2,3,128,128]{3,2,1,0:T(8,128)} %collective-permute-done.11.refs_6_), channel_id=1, source_target_pairs={{0,8},{8,0},{16,24},{24,16},{1,9},{9,1},{17,25},{25,17},{2,10},{10... | collective-permute-start | bytes 1179656 | tf_op jit(solution)/shard_map/ppermute | solution.py:381
  27.9 7.6 %collective-permute-start.18 = (f32[4,128,128]{2,1,0:T(8,128)S(1)}, f32[4,128,128]{2,1,0:T(8,128)S(1)}, u32[]{:S(2)}, u32[]{:S(2)}) collective-permute-start(f32[4,128,128]{2,1,0:T(8,128)S(1)} %pad_maximum_fusion.2), channel_id=1, source_target_pairs={{0,1},{1,0},{2,3},{3,2},{4,5},{5,4},{6,7},{7,6},{8,9},{9,8},{10,11... | collective-permute-start | bytes 786440 | tf_op jit(solution)/shard_map/ppermute | solution.py:381
  32.6 7.4 %collective-permute-start.10 = (f32[8,128,128]{2,1,0:T(8,128)S(1)}, f32[8,128,128]{2,1,0:T(8,128)S(1)}, u32[]{:S(2)}, u32[]{:S(2)}) collective-permute-start(f32[8,128,128]{2,1,0:T(8,128)S(1)} %collective-permute-done.8.refs_2_), channel_id=1, source_target_pairs={{0,8},{8,0},{16,24},{24,16},{1,9},{9,1},{17,25},{25,17},{2,10},{10... | collective-permute-start | bytes 1572872 | tf_op jit(solution)/shard_map/ppermute | solution.py:381
  35.5 27.5 %collective-permute-start.5 = (f32[768,128]{1,0:T(8,128)S(1)}, f32[768,128]{1,0:T(8,128)S(1)}, u32[]{:S(2)}, u32[]{:S(2)}) collective-permute-start(f32[768,128]{1,0:T(8,128)S(1)} %bitcast.38), channel_id=1, source_target_pairs={{0,4},{1,5},{2,6},{3,7},{4,0},{5,1},{6,2},{7,3},{8,12},{9,13},{10,... | collective-permute-start | bytes 1179656 | tf_op jit(solution)/shard_map/ppermute | solution.py:381
  38.4 24.9 %collective-permute-start.6 = (f32[768,128]{1,0:T(8,128)S(1)}, f32[768,128]{1,0:T(8,128)S(1)}, u32[]{:S(2)}, u32[]{:S(2)}) collective-permute-start(f32[768,128]{1,0:T(8,128)S(1)} %bitcast.39), channel_id=1, source_target_pairs={{0,6},{1,7},{2,0},{3,1},{4,2},{5,3},{6,4},{7,5},{8,14},{9,15},{10,... | collective-permute-start | bytes 1179656 | tf_op jit(solution)/shard_map/ppermute | solution.py:381
  38.4 24.6 %collective-permute-start.7 = (f32[768,128]{1,0:T(8,128)S(1)}, f32[768,128]{1,0:T(8,128)S(1)}, u32[]{:S(2)}, u32[]{:S(2)}) collective-permute-start(f32[768,128]{1,0:T(8,128)S(1)} %bitcast.40), channel_id=1, source_target_pairs={{0,1},{1,0},{2,3},{3,2},{4,5},{5,4},{6,7},{7,6},{8,9},{9,8},{10,11... | collective-permute-start | bytes 1179656 | tf_op jit(solution)/shard_map/ppermute | solution.py:381
  40.1 24.9 %collective-permute-start.19 = (f32[8,128,128]{2,1,0:T(8,128)S(1)}, f32[8,128,128]{2,1,0:T(8,128)S(1)}, u32[]{:S(2)}, u32[]{:S(2)}) collective-permute-start(f32[8,128,128]{2,1,0:T(8,128)S(1)} %constant_dynamic-update-slice_fusion.5.refs_1_), channel_id=1, source_target_pairs={{0,16},{8,24},{16,0},{24,8},{1,17},{9,25},{17,1},{25,9},{2,18},{10... | collective-permute-start | bytes 1572872 | tf_op jit(solution)/shard_map/ppermute | solution.py:381
  63.4 28.0 %collective-permute-start.14 = (f32[3,768,128]{2,1,0:T(8,128)S(1)}, f32[3,768,128]{2,1,0:T(8,128)S(1)}, u32[]{:S(2)}, u32[]{:S(2)}) collective-permute-start(f32[3,768,128]{2,1,0:T(8,128)S(1)} %pad_maximum_fusion), channel_id=1, source_target_pairs={{0,1},{1,0},{2,3},{3,2},{4,5},{5,4},{6,7},{7,6},{8,9},{9,8},{10,11... | collective-permute-start | bytes 3538952 | tf_op jit(solution)/shard_map/ppermute | solution.py:381
  65.0 1.9 %collective-permute-start.20 = (f32[8,128,128]{2,1,0:T(8,128)S(1)}, f32[8,128,128]{2,1,0:T(8,128)S(1)}, u32[]{:S(2)}, u32[]{:S(2)}) collective-permute-start(f32[8,128,128]{2,1,0:T(8,128)S(1)} %constant_dynamic-update-slice_fusion.5.refs_1_), channel_id=1, source_target_pairs={{0,8},{8,0},{16,24},{24,16},{1,9},{9,1},{17,25},{25,17},{2,10},{10... | collective-permute-start | bytes 1572872 | tf_op jit(solution)/shard_map/ppermute | solution.py:381
  65.0 2.7 %collective-permute-start.21 = (f32[8,128,128]{2,1,0:T(8,128)S(1)}, f32[8,128,128]{2,1,0:T(8,128)S(1)}, u32[]{:S(2)}, u32[]{:S(2)}) collective-permute-start(f32[8,128,128]{2,1,0:T(8,128)S(1)} %collective-permute-done.19.refs_2_), channel_id=1, source_target_pairs={{0,8},{8,0},{16,24},{24,16},{1,9},{9,1},{17,25},{25,17},{2,10},{10... | collective-permute-start | bytes 1572872 | tf_op jit(solution)/shard_map/ppermute | solution.py:381
